TPU v7x, 32 devices: a whole 2x2x4 slice. The times are simulated.
32 devices in a mesh: row: 8 (over y, x, core), col: 4 (over z).
Axes of the slice: x: 2, y: 2, z: 4, core: 2. Of those that a mesh axis runs over, the one named last changes fastest.
Arguments:
- layer_input: bfloat16 [8192, 1536], P('row', 'col'), may hold values from -6 to 6
- cotangent: bfloat16 [8192, 1536], P('row', 'col'), may hold values from -8 to 8
- gain_attention: float32 [1536], P('col'), may hold values from 0.5 to 1.5
- gain_mixture: float32 [1536], P('col'), may hold values from 0.5 to 1.5
- w_query: bfloat16 [1536, 1536], P('row', 'col'), may hold values from -0.625 to 0.625
- w_key: bfloat16 [1536, 512], P('row', 'col'), may hold values from -0.625 to 0.625
- w_value: bfloat16 [1536, 512], P('row', 'col'), may hold values from -0.15625 to 0.15625
- w_out: bfloat16 [1536, 1536], P('row', 'col'), may hold values from -1.5 to 1.5
- w_router: bfloat16 [1536, 40], P('row'), may hold values from -0.078125 to 0.078125
- w_gate: bfloat16 [1536, 40, 512], P('row', 'col'), may hold values from -0.15625 to 0.15625
- w_up: bfloat16 [1536, 40, 512], P('row', 'col'), may hold values from -0.15625 to 0.15625
- w_down: bfloat16 [1536, 40, 512], P('row', 'col'), may hold values from -6 to 6
- routes: int32 [8192, 8], P('row'), may hold values from 0 to 39, all different within a row
- priority: int32 [8192, 8], P('row'), may hold values from 0 to 8191, as said below
- ancestry: int32 [8192, 3], P('row'), may hold values from 0 to 12, as said below
Outputs:
- layer_output: bfloat16 [8192, 1536], P('row', 'col')
- input_grad: float32 [8192, 1536], P('row', 'col')
- gain_attention_grad: float32 [1536], P('col')
- gain_mixture_grad: float32 [1536], P('col')
- w_query_grad: float32 [1536, 1536], P('row', 'col')
- w_key_grad: float32 [1536, 512], P('row', 'col')
- w_value_grad: float32 [1536, 512], P('row', 'col')
- w_out_grad: float32 [1536, 1536], P('row', 'col')
- w_router_grad: float32 [1536, 40], P('row')
- w_gate_grad: float32 [1536, 40, 512], P('row', 'col')
- w_up_grad: float32 [1536, 40, 512], P('row', 'col')
- w_down_grad: float32 [1536, 40, 512], P('row', 'col')
Inputs may be any that keep to these rules, and one draw needn't show every extreme that they name: `routes`: each token names 8 different experts. `priority`: within each aligned block of 1024 tokens the 8192 entries hold each of 0 to 8191 once. `ancestry`: the 13 segments are contiguous runs of tokens in depth-first order: the trunk (segment 0, its own parent), 4 branches, and 2 leaves under each branch; the trunk holds 3276 tokens. Columns 1 and 2 give the parent's and grandparent's segment.
All inputs are finite; a program needn't handle non-finite values.
Results may differ from a plain program's by a relative error of at most 0.02.
Values may be sent and summed in bfloat16 or wider, within the bound.
No kernel may reach another device: no remote copies, remote signals or barrier semaphores. Data moves between devices by JAX's collectives and lax.ppermute only.
A program may use at most 256 MiB of HBM per device.

v0:
```python
import math

import jax
import jax.numpy as jnp
from jax import lax
from jax.sharding import PartitionSpec as P

D = 1536
HD = 64
H = 512
EXPERTS = 40
TOPK = 8
SEGS = 13
CAP = 230


epsilon = 1e-06
branch_scale = 0.22
score_scale = 0.015625
rope_base = 10000.0
masked_score = -1e30


def contract_rows(left, right):
    return lax.dot_general(
        left, right, (((0,), (0,)), ((), ())), preferred_element_type=jnp.float32
    )


def contract_last(left, right):
    return lax.dot_general(
        left, right, (((1,), (1,)), ((), ())), preferred_element_type=jnp.float32
    )


def features_gather(values):
    return lax.all_gather(values, "col", axis=1, tiled=True)


def features_reduce(values):
    return lax.psum_scatter(values, "col", scatter_dimension=1, tiled=True)


def token_total(values):
    return lax.psum(values, "col")


def expert_matrices(w_gate, w_up, w_down, expert):
    return (
        lax.all_gather(w_gate[:, expert], "row", axis=0, tiled=True),
        lax.all_gather(w_up[:, expert], "row", axis=0, tiled=True),
        lax.all_gather(w_down[:, expert], "row", axis=0, tiled=True),
    )


def rope_tables(position):
    half = HD // 2
    freq = rope_base ** (-(jnp.arange(half, dtype=jnp.float32) * 2.0) / HD)
    angle = position.astype(jnp.float32)[:, None] * freq[None, :]
    return (jnp.cos(angle), jnp.sin(angle))


def rotate(values, cosine, sine):
    half = HD // 2
    first_half = values[..., :half]
    second_half = values[..., half:]
    cos_b = cosine[:, None, :]
    sin_b = sine[:, None, :]
    return jnp.concatenate(
        [first_half * cos_b - second_half * sin_b, second_half * cos_b + first_half * sin_b],
        axis=-1,
    )


def slot_tables(group_routes, group_priority, first_expert, expert_count):
    pairs = group_routes.shape[0] * TOPK
    flat_routes = group_routes.reshape(pairs)
    flat_priority = group_priority.reshape(pairs)
    numbers = jnp.arange(pairs, dtype=jnp.int32)
    order = jnp.zeros((pairs,), jnp.int32).at[flat_priority].set(numbers)
    ordered = flat_routes[order]
    member = (ordered[:, None] == jnp.arange(EXPERTS, dtype=jnp.int32)[None, :]).astype(jnp.int32)
    running = jnp.cumsum(member, axis=0, dtype=jnp.int32)
    rank_ordered = jnp.sum(running * member, axis=1, dtype=jnp.int32) - 1
    rank = rank_ordered[flat_priority]
    local = flat_routes - first_expert
    inside = (local >= 0) & (local < expert_count) & (rank < CAP)
    target = jnp.where(inside, local * CAP + rank, expert_count * CAP)
    slot_pair = (
        jnp.zeros((expert_count * CAP + 1,), jnp.int32)
        .at[target]
        .set(numbers)[: expert_count * CAP]
    )
    slot_live = (
        jnp.zeros((expert_count * CAP + 1,), jnp.float32).at[target].set(1.0)[: expert_count * CAP]
    )
    return (slot_pair, slot_live)


def block_view(queries, path, query_index, own_all, key_rows, start, block, key_heads):
    keys_block = lax.dynamic_slice_in_dim(key_rows, start, block, 0)
    key_part = keys_block[:, : key_heads * HD].reshape(block, key_heads, HD)
    value_part = keys_block[:, key_heads * HD :].reshape(block, key_heads, HD)
    key_segment = lax.dynamic_slice_in_dim(own_all, start, block, 0)
    key_index = start + jnp.arange(block, dtype=jnp.int32)
    on_path = (
        (path[:, 0:1] == key_segment[None, :])
        | (path[:, 1:2] == key_segment[None, :])
        | (path[:, 2:3] == key_segment[None, :])
    )
    allowed = on_path & (query_index[:, None] >= key_index[None, :])
    scores = score_scale * jnp.einsum(
        "qhgd,khd->hgqk", queries, key_part, preferred_element_type=jnp.float32
    )
    return (scores, key_part, value_part, allowed[None, None])


def attend_forward(queries, path, query_index, own_all, key_rows, block, key_heads):
    count = queries.shape[0]
    group = queries.shape[2]
    key_blocks = key_rows.shape[0] // block

    def advance(carry, block_number):
        peak, total, weighted = carry
        scores, key_part, value_part, allowed = block_view(
            queries, path, query_index, own_all, key_rows, block_number * block, block, key_heads
        )
        new_peak = jnp.maximum(peak, jnp.max(jnp.where(allowed, scores, masked_score), axis=-1))
        weights = jnp.where(allowed, jnp.exp(scores - new_peak[..., None]), 0.0)
        factor = jnp.exp(peak - new_peak)
        total = total * factor + jnp.sum(weights, axis=-1)
        weighted = weighted * factor[..., None] + jnp.einsum(
            "hgqk,khd->hgqd", weights, value_part, preferred_element_type=jnp.float32
        )
        return ((new_peak, total, weighted), None)

    start_state = (
        jnp.full((key_heads, group, count), masked_score, jnp.float32),
        jnp.zeros((key_heads, group, count), jnp.float32),
        jnp.zeros((key_heads, group, count, HD), jnp.float32),
    )
    (peak, total, weighted), unused = lax.scan(
        advance, start_state, jnp.arange(key_blocks, dtype=jnp.int32)
    )
    return (weighted / total[..., None], peak + jnp.log(total))


def attend_backward(
    queries,
    path,
    query_index,
    own_all,
    key_rows,
    block,
    key_heads,
    log_total,
    mixed_grad,
    delta,
    key_grads,
):
    key_blocks = key_rows.shape[0] // block

    def advance(carry, block_number):
        query_grad, key_grads = carry
        start = block_number * block
        scores, key_part, value_part, allowed = block_view(
            queries, path, query_index, own_all, key_rows, start, block, key_heads
        )
        weights = jnp.where(allowed, jnp.exp(scores - log_total[..., None]), 0.0)
        weight_grad = jnp.einsum(
            "qhgd,khd->hgqk", mixed_grad, value_part, preferred_element_type=jnp.float32
        )
        score_grad = (weights * (weight_grad - delta[..., None])).astype(jnp.bfloat16)
        query_grad = query_grad + score_scale * jnp.einsum(
            "hgqk,khd->qhgd", score_grad, key_part, preferred_element_type=jnp.float32
        )
        key_grad = score_scale * jnp.einsum(
            "hgqk,qhgd->khd", score_grad, queries, preferred_element_type=jnp.float32
        )
        value_grad = jnp.einsum(
            "hgqk,qhgd->khd", weights, mixed_grad, preferred_element_type=jnp.float32
        )
        update = jnp.concatenate(
            [key_grad.reshape(block, key_heads * HD), value_grad.reshape(block, key_heads * HD)],
            axis=1,
        )
        current = lax.dynamic_slice_in_dim(key_grads, start, block, 0)
        key_grads = lax.dynamic_update_slice_in_dim(key_grads, current + update, start, 0)
        return ((query_grad, key_grads), None)

    start_state = (jnp.zeros(queries.shape, jnp.float32), key_grads)
    (query_grad, key_grads), unused = lax.scan(
        advance, start_state, jnp.arange(key_blocks, dtype=jnp.int32)
    )
    return (query_grad, key_grads)


def expert_term_fn(inputs_e, slot_grad, activity):
    return jnp.concatenate(
        [
            contract_rows(inputs_e, activity[:, : 2 * H]),
            contract_rows(slot_grad, activity[:, 2 * H :]),
        ],
        axis=1,
    )


def body(
    layer_input,
    cotangent,
    gain_attention,
    gain_mixture,
    w_query,
    w_key,
    w_value,
    w_out,
    w_router,
    w_gate,
    w_up,
    w_down,
    routes,
    priority,
    ancestry,
):
    local_rows = layer_input.shape[0]
    width_local = layer_input.shape[1]
    query_heads = w_query.shape[1] // HD
    key_heads = w_key.shape[1] // HD
    group = query_heads // key_heads
    local_experts = w_gate.shape[1]
    tokens_all = local_rows * lax.axis_size("row")
    token_start = lax.axis_index("row") * local_rows
    feature_start = lax.axis_index("col") * width_local
    query_block = math.gcd(local_rows, 512)
    key_block = math.gcd(tokens_all, 1024)
    segment_ids = jnp.arange(SEGS, dtype=jnp.int32)
    x_wide = layer_input.astype(jnp.float32)
    squares_one = token_total(jnp.sum(x_wide * x_wide, axis=1))
    inverse_one = lax.rsqrt(squares_one / D + epsilon)[:, None]
    h_one = features_gather((x_wide * inverse_one * gain_attention[None, :]).astype(jnp.bfloat16))
    full_query, full_key, full_value, full_out, full_router = (
        lax.all_gather(w_query, "row", axis=0, tiled=True),
        lax.all_gather(w_key, "row", axis=0, tiled=True),
        lax.all_gather(w_value, "row", axis=0, tiled=True),
        lax.all_gather(w_out, "row", axis=0, tiled=True),
        lax.all_gather(w_router, "row", axis=0, tiled=True),
    )
    query_pre = jnp.dot(h_one, full_query, preferred_element_type=jnp.float32)
    key_pre = jnp.dot(h_one, full_key, preferred_element_type=jnp.float32)
    value = jnp.dot(h_one, full_value, preferred_element_type=jnp.float32).astype(jnp.bfloat16)
    own_all = lax.all_gather(ancestry[:, 0], "row", axis=0, tiled=True)
    member_all = (own_all[:, None] == segment_ids[None, :]).astype(jnp.int32)
    before_all = jnp.cumsum(member_all, axis=0, dtype=jnp.int32) - member_all
    before = lax.dynamic_slice_in_dim(before_all, token_start, local_rows, 0)
    on_path = (
        (ancestry[:, 0:1] == segment_ids[None, :])
        | (ancestry[:, 1:2] == segment_ids[None, :])
        | (ancestry[:, 2:3] == segment_ids[None, :])
    ).astype(jnp.int32)
    position = jnp.sum(on_path * before, axis=1, dtype=jnp.int32)
    cosine, sine = rope_tables(position)
    query = (
        rotate(query_pre.reshape(local_rows, query_heads, HD), cosine, sine)
        .astype(jnp.bfloat16)
        .reshape(local_rows, key_heads, group, HD)
    )
    keys = rotate(key_pre.reshape(local_rows, key_heads, HD), cosine, sine).astype(jnp.bfloat16)
    key_rows = lax.all_gather(
        jnp.concatenate([keys.reshape(local_rows, key_heads * HD), value], axis=1),
        "row",
        axis=0,
        tiled=True,
    )
    query_index = token_start + jnp.arange(local_rows, dtype=jnp.int32)
    mixed_parts = []
    total_parts = []
    for begin in range(0, local_rows, query_block):
        stop = begin + query_block
        part_mixed, part_total = attend_forward(
            query[begin:stop],
            ancestry[begin:stop],
            query_index[begin:stop],
            own_all,
            key_rows,
            key_block,
            key_heads,
        )
        mixed_parts.append(part_mixed)
        total_parts.append(part_total)
    mixed_f = jnp.concatenate(mixed_parts, axis=2)
    log_total = jnp.concatenate(total_parts, axis=2)
    mixed = mixed_f.transpose(2, 0, 1, 3).reshape(local_rows, query_heads * HD).astype(jnp.bfloat16)
    attention_slice = features_reduce(contract_last(mixed, full_out))
    x_middle = x_wide + branch_scale * attention_slice
    squares_two = token_total(jnp.sum(x_middle * x_middle, axis=1))
    inverse_two = lax.rsqrt(squares_two / D + epsilon)[:, None]
    h_two = features_gather((x_middle * inverse_two * gain_mixture[None, :]).astype(jnp.bfloat16))
    logits = jnp.dot(h_two, full_router, preferred_element_type=jnp.float32)
    chosen = (routes[:, :, None] == jnp.arange(EXPERTS, dtype=jnp.int32)[None, None, :]).astype(
        jnp.float32
    )
    gates = jax.nn.softmax(jnp.sum(chosen * logits[:, None, :], axis=2), axis=1)
    slot_pair, slot_live = slot_tables(
        routes, priority, lax.axis_index("col") * local_experts, local_experts
    )
    slot_token = slot_pair // TOPK
    slot_weight = gates.reshape(-1)[slot_pair] * slot_live
    mix_part = jnp.zeros((local_rows, D), jnp.float32)
    kept = []
    for expert in range(local_experts):
        matrices = expert_matrices(w_gate, w_up, w_down, expert)
        gate_matrix, up_matrix, down_matrix = matrices
        tokens_e = slot_token[expert * CAP : (expert + 1) * CAP]
        inputs_e = h_two[tokens_e]
        gate_pre = jnp.dot(inputs_e, gate_matrix, preferred_element_type=jnp.float32)
        up_pre = jnp.dot(inputs_e, up_matrix, preferred_element_type=jnp.float32)
        active = (jax.nn.silu(gate_pre) * up_pre).astype(jnp.bfloat16)
        expert_out = contract_last(active, down_matrix)
        mix_part = mix_part.at[tokens_e].add(
            expert_out * slot_weight[expert * CAP : (expert + 1) * CAP][:, None]
        )
        kept.append((matrices, inputs_e, gate_pre, up_pre, active, expert_out))
    mix_slice = features_reduce(mix_part)
    result = (x_middle + branch_scale * mix_slice).astype(jnp.bfloat16)
    grad_out = cotangent.astype(jnp.float32)
    mix_grad = features_gather((branch_scale * grad_out).astype(jnp.bfloat16))
    pair_grad = jnp.zeros((local_rows * TOPK,), jnp.float32)
    token_grads = jnp.zeros((local_rows, D), jnp.float32)
    gate_sums = []
    up_sums = []
    down_sums = []
    for expert in range(local_experts):
        matrices, inputs_e, gate_pre, up_pre, active, expert_out = kept[expert]
        matrices = expert_matrices(w_gate, w_up, w_down, expert)
        gate_matrix, up_matrix, down_matrix = matrices
        tokens_e = slot_token[expert * CAP : (expert + 1) * CAP]
        pairs_e = slot_pair[expert * CAP : (expert + 1) * CAP]
        live_e = slot_live[expert * CAP : (expert + 1) * CAP]
        weight_e = slot_weight[expert * CAP : (expert + 1) * CAP]
        upstream = mix_grad[tokens_e].astype(jnp.float32)
        pair_grad = pair_grad.at[pairs_e].add(jnp.sum(upstream * expert_out, axis=1) * live_e)
        slot_grad = (weight_e[:, None] * upstream).astype(jnp.bfloat16)
        act_grad = jnp.dot(slot_grad, down_matrix, preferred_element_type=jnp.float32)
        sigma = jax.nn.sigmoid(gate_pre)
        gate_grad = (act_grad * up_pre * sigma * (1.0 + gate_pre * (1.0 - sigma))).astype(
            jnp.bfloat16
        )
        up_grad = (act_grad * jax.nn.silu(gate_pre)).astype(jnp.bfloat16)
        token_grads = token_grads.at[tokens_e].add(
            contract_last(gate_grad, gate_matrix) + contract_last(up_grad, up_matrix)
        )
        activity = jnp.concatenate([gate_grad, up_grad, active], axis=1)
        summed = lax.psum_scatter(
            expert_term_fn(inputs_e, slot_grad, activity).astype(jnp.bfloat16),
            "row",
            scatter_dimension=0,
            tiled=True,
        ).astype(jnp.float32)
        gate_sums.append(summed[:, :H])
        up_sums.append(summed[:, H : 2 * H])
        down_sums.append(summed[:, 2 * H :])
    pair_grad = lax.psum(pair_grad.reshape(local_rows, TOPK), "col")
    picked_grad = gates * (pair_grad - jnp.sum(gates * pair_grad, axis=1, keepdims=True))
    logit_grad = jnp.sum(chosen * picked_grad[:, :, None], axis=1).astype(jnp.bfloat16)
    router_rows = lax.dynamic_slice_in_dim(full_router, feature_start, width_local, 0)
    h_two_grad = features_reduce(token_grads) + contract_last(logit_grad, router_rows)
    scaled_two = h_two_grad * gain_mixture[None, :]
    inner_two = token_total(jnp.sum(scaled_two * x_middle, axis=1))[:, None]
    x_middle_grad = grad_out + inverse_two * scaled_two - x_middle * inverse_two**3 * inner_two / D
    gain_mixture_grad = jnp.sum(h_two_grad * x_middle * inverse_two, axis=0)
    branch_grad = features_gather((branch_scale * x_middle_grad).astype(jnp.bfloat16))
    mixed_grad = jnp.dot(branch_grad, full_out, preferred_element_type=jnp.float32).astype(
        jnp.bfloat16
    )
    mixed_grad_heads = mixed_grad.reshape(local_rows, key_heads, group, HD)
    delta = jnp.einsum("qhgd,hgqd->hgq", mixed_grad_heads.astype(jnp.float32), mixed_f)
    key_grads = jnp.zeros((tokens_all, 2 * key_heads * HD), jnp.float32)
    query_parts = []
    for begin in range(0, local_rows, query_block):
        stop = begin + query_block
        part_grad, key_grads = attend_backward(
            query[begin:stop],
            ancestry[begin:stop],
            query_index[begin:stop],
            own_all,
            key_rows,
            key_block,
            key_heads,
            log_total[:, :, begin:stop],
            mixed_grad_heads[begin:stop],
            delta[:, :, begin:stop],
            key_grads,
        )
        query_parts.append(part_grad)
    query_grad = jnp.concatenate(query_parts, axis=0)
    key_local = lax.psum_scatter(key_grads, "row", scatter_dimension=0, tiled=True)
    query_pre_grad = (
        rotate(query_grad.reshape(local_rows, query_heads, HD), cosine, -sine)
        .astype(jnp.bfloat16)
        .reshape(local_rows, query_heads * HD)
    )
    key_pre_grad = (
        rotate(key_local[:, : key_heads * HD].reshape(local_rows, key_heads, HD), cosine, -sine)
        .astype(jnp.bfloat16)
        .reshape(local_rows, key_heads * HD)
    )
    value_pre_grad = key_local[:, key_heads * HD :].astype(jnp.bfloat16)
    h_one_grad = features_reduce(
        contract_last(query_pre_grad, full_query)
        + contract_last(key_pre_grad, full_key)
        + contract_last(value_pre_grad, full_value)
    )
    scaled_one = h_one_grad * gain_attention[None, :]
    inner_one = token_total(jnp.sum(scaled_one * x_wide, axis=1))[:, None]
    input_grad = x_middle_grad + inverse_one * scaled_one - x_wide * inverse_one**3 * inner_one / D
    gain_attention_grad = jnp.sum(h_one_grad * x_wide * inverse_one, axis=0)
    project_grad = jnp.concatenate([query_pre_grad, key_pre_grad, value_pre_grad], axis=1)
    attention_sums = lax.psum_scatter(
        jnp.concatenate(
            [
                contract_rows(h_one, project_grad),
                contract_rows(branch_grad, mixed),
                contract_rows(h_two, logit_grad),
            ],
            axis=1,
        ).astype(jnp.bfloat16),
        "row",
        scatter_dimension=0,
        tiled=True,
    ).astype(jnp.float32)
    gain_attention_grad, gain_mixture_grad = lax.psum(
        (gain_attention_grad, gain_mixture_grad), "row"
    )
    query_width = query_heads * HD
    key_width = key_heads * HD
    w_query_grad = attention_sums[:, :query_width]
    w_key_grad = attention_sums[:, query_width : query_width + key_width]
    w_value_grad = attention_sums[:, query_width + key_width : query_width + 2 * key_width]
    w_out_grad = attention_sums[:, query_width + 2 * key_width : 2 * query_width + 2 * key_width]
    w_router_grad = attention_sums[:, 2 * query_width + 2 * key_width :]
    w_gate_grad = jnp.stack(gate_sums, axis=1)
    w_up_grad = jnp.stack(up_sums, axis=1)
    w_down_grad = jnp.stack(down_sums, axis=1)
    return (
        result,
        input_grad,
        gain_attention_grad,
        gain_mixture_grad,
        w_query_grad,
        w_key_grad,
        w_value_grad,
        w_out_grad,
        w_router_grad,
        w_gate_grad,
        w_up_grad,
        w_down_grad,
    )


def solution(mesh):
    return jax.shard_map(
        body,
        mesh=mesh,
        in_specs=(
            P("row", "col"),
            P("row", "col"),
            P("col"),
            P("col"),
            P("row", "col"),
            P("row", "col"),
            P("row", "col"),
            P("row", "col"),
            P("row", None),
            P("row", "col", None),
            P("row", "col", None),
            P("row", "col", None),
            P("row", None),
            P("row", None),
            P("row", None),
        ),
        out_specs=(
            P("row", "col"),
            P("row", "col"),
            P("col"),
            P("col"),
            P("row", "col"),
            P("row", "col"),
            P("row", "col"),
            P("row", "col"),
            P("row", None),
            P("row", "col", None),
            P("row", "col", None),
            P("row", "col", None),
        ),
        check_vma=False,
    )
```

profile of v0, /device:TPU:0, one launch (start us, length us, event | category | flops | bytes accessed | tf_op | source)
XLA Modules:
  0.0 3190.1 jit_solution(8726157120714174645)
XLA Ops:
  115.6 35.4 %all-gather.72.cloned.1.call-done = bf16[8192,256]{0,1:T(8,128)(2,1)} async-done(((bf16[1024,256]{0,1:T(8,128)(2,1)}), bf16[8192,256]{0,1:T(8,128)(2,1)}) %all-gather.72.cloned.1.call-update) | async-done | bytes 4194320 | tf_op jit(solution)/shard_map/all_gather | solution.py:268
  151.6 127.4 %while.57 = (s32[]{:T(128)}, f32[2,3,512]{2,1,0:T(4,128)S(1)}, f32[2,3,512]{2,1,0:T(4,128)S(1)}, f32[2,3,512,64]{2,3,1,0:T(8,128)}, s32[512,3]{0,1:T(4,128)S(1)}...) while((s32[]{:T(128)}, f32[2,3,512]{2,1,0:T(4,128)S(1)}, ...), condition=%wide.region_12.13_spmd.clone, body=%wide.region_9.12_spmd.clone.sunk | while | flops 841039872 | bytes 45719824 | solution.py:142
  279.7 118.1 %while.56 = (s32[]{:T(128)}, f32[2,3,512]{2,1,0:T(4,128)S(1)}, f32[2,3,512]{2,1,0:T(4,128)S(1)}, f32[2,3,512,64]{2,3,1,0:T(8,128)}, s32[512,3]{0,1:T(4,128)S(1)}...) while((s32[]{:T(128)}, f32[2,3,512]{2,1,0:T(4,128)S(1)}, ...), condition=%wide.region_8.9_spmd.clone, body=%wide.region_5.8_spmd.clone.sunk | while | flops 841039872 | bytes 48341632 | solution.py:142
  409.1 108.7 %reduce-scatter.39.cloned.1.call-done = f32[1024,384]{1,0:T(8,128)} async-done(((f32[1024,1536]{1,0:T(8,128)}), f32[1024,384]{1,0:T(8,128)}) %reduce-scatter.39.cloned.1.call-update) | async-done | bytes 1572880 | tf_op jit(solution)/shard_map/reduce_scatter | solution.py:41
  559.4 30.5 scatter_custom_fusion
  590.2 45.5 %gather_fusion = s32[8192]{0:T(1024)S(1)} fusion(s32[8192]{0:T(1024)S(1)} %reshape.817, s32[8192]{0:T(1024)S(1)} %get-tuple-element.773), kind=kCustom, calls=%fused_computation | custom fusion | bytes 98304 | tf_op jit(solution)/shard_map/gather | solution.py:81
  650.7 45.5 %gather_fusion.1 = s32[8192]{0:T(1024)S(1)} fusion(s32[8192]{0:T(1024)S(1)} %broadcast_add_fusion.2, s32[8192]{0:T(1024)S(1)} %get-tuple-element.774), kind=kCustom, calls=%fused_computation.1 | custom fusion | bytes 98304 | tf_op jit(solution)/shard_map/gather | solution.py:85
  696.4 30.5 scatter_custom_fusion.1
  738.6 30.6 scatter_custom_fusion.2
  843.7 25.3 all-gather.114.cloned.1.call-done
  1793.1 99.6 %reduce-scatter.41.cloned.1.call-done = f32[1024,384]{1,0:T(8,128)} async-done(((f32[1024,1536]{1,0:T(8,128)}), f32[1024,384]{1,0:T(8,128)}) %reduce-scatter.41.cloned.1.call-update) | async-done | bytes 1572880 | tf_op jit(solution)/shard_map/reduce_scatter | solution.py:41
  1896.3 63.8 %all-gather.82.cloned.1.call-done = bf16[1024,1536]{1,0:T(8,128)(2,1)} async-done(((bf16[1024,384]{1,0:T(8,128)(2,1)}), bf16[1024,1536]{1,0:T(8,128)(2,1)}) %all-gather.82.cloned.1.call-update) | async-done | bytes 3145744 | tf_op jit(solution)/shard_map/all_gather | solution.py:37
  1970.0 194.6 %while.58 = (s32[]{:T(128)}, f32[512,2,3,64]{0,3,2,1:T(8,128)}, f32[8192,256]{0,1:T(8,128)}, s32[8]{0:T(128)S(1)}, bf16[8192,256]{0,1:T(8,128)(2,1)}, /*index=5*...) while((s32[]{:T(128)}, f32[512,2,3,64]{0,3,2,1:T(8,128)}, ...), condition=%wide.region_73.74_spmd.clone, body=%wide.region_72.73_spmd.clone.sunk | while | flops 2046493696 | bytes 69546272 | solution.py:192
  2164.7 180.2 %while.59 = (s32[]{:T(128)}, f32[512,2,3,64]{0,3,2,1:T(8,128)S(1)}, f32[8192,256]{0,1:T(8,128)}, s32[8]{0:T(128)S(1)}, bf16[8192,256]{0,1:T(8,128)(2,1)}, /*inde...) while((s32[]{:T(128)}, f32[512,2,3,64]{0,3,2,1:T(8,128)S(1)}, ...), condition=%wide.region_75.76_spmd.clone, body=%wide.region_74.75_spmd.clone.sunk | while | flops 2046493696 | bytes 69546272 | solution.py:192
  2498.0 31.9 reduce-scatter.53.cloned.1.call-done
  2532.4 55.2 %reduce-scatter.55.cloned.1.call-done = bf16[192,1536]{1,0:T(8,128)(2,1)} async-done(((bf16[1536,1536]{1,0:T(8,128)(2,1)}), bf16[192,1536]{1,0:T(8,128)(2,1)}) %reduce-scatter.55.cloned.1.call-update) | async-done | bytes 589840
  2590.2 54.6 %reduce-scatter.57.cloned.1.call-done = bf16[192,1536]{1,0:T(8,128)(2,1)} async-done(((bf16[1536,1536]{1,0:T(8,128)(2,1)}), bf16[192,1536]{1,0:T(8,128)(2,1)}) %reduce-scatter.57.cloned.1.call-update) | async-done | bytes 589840
  2647.4 55.0 %reduce-scatter.59.cloned.1.call-done = bf16[192,1536]{1,0:T(8,128)(2,1)} async-done(((bf16[1536,1536]{1,0:T(8,128)(2,1)}), bf16[192,1536]{1,0:T(8,128)(2,1)}) %reduce-scatter.59.cloned.1.call-update) | async-done | bytes 589840
  2705.1 54.6 %reduce-scatter.61.cloned.1.call-done = bf16[192,1536]{1,0:T(8,128)(2,1)} async-done(((bf16[1536,1536]{1,0:T(8,128)(2,1)}), bf16[192,1536]{1,0:T(8,128)(2,1)}) %reduce-scatter.61.cloned.1.call-update) | async-done | bytes 589840
  2762.2 55.0 %reduce-scatter.63.cloned.1.call-done = bf16[192,1536]{1,0:T(8,128)(2,1)} async-done(((bf16[1536,1536]{1,0:T(8,128)(2,1)}), bf16[192,1536]{1,0:T(8,128)(2,1)}) %reduce-scatter.63.cloned.1.call-update) | async-done | bytes 589840
  2819.9 54.6 %reduce-scatter.65.cloned.1.call-done = bf16[192,1536]{1,0:T(8,128)(2,1)} async-done(((bf16[1536,1536]{1,0:T(8,128)(2,1)}), bf16[192,1536]{1,0:T(8,128)(2,1)}) %reduce-scatter.65.cloned.1.call-update) | async-done | bytes 589840
  2875.9 56.3 %reduce-scatter.67.cloned.1.call-done = bf16[192,1536]{1,0:T(8,128)(2,1)} async-done(((bf16[1536,1536]{1,0:T(8,128)(2,1)}), bf16[192,1536]{1,0:T(8,128)(2,1)}) %reduce-scatter.67.cloned.1.call-update) | async-done | bytes 589840
  2935.7 53.8 %reduce-scatter.69.cloned.1.call-done = bf16[192,1536]{1,0:T(8,128)(2,1)} async-done(((bf16[1536,1536]{1,0:T(8,128)(2,1)}), bf16[192,1536]{1,0:T(8,128)(2,1)}) %reduce-scatter.69.cloned.1.call-update) | async-done | bytes 589840
  3046.6 107.9 %reduce-scatter.47.cloned.1.call-done = f32[1024,384]{1,0:T(8,128)} async-done(((f32[1024,1536]{1,0:T(8,128)}), f32[1024,384]{1,0:T(8,128)}) %reduce-scatter.47.cloned.1.call-update) | async-done | bytes 1572880 | tf_op jit(solution)/shard_map/reduce_scatter | solution.py:41
  (1517 shorter events, 2054.2 us)
Async XLA Ops:
  545.0 461.4 %all-gather.92.cloned.1.call-start = ((), (), s32[]{:S(2)}) async-start(), calls=%async_computation.32 | async-start | bytes 1769472 | tf_op jit(solution)/shard_map/all_gather | solution.py:51
  545.6 488.5 %all-gather.98.cloned.1.call-start = ((), (), s32[]{:S(2)}) async-start(), calls=%async_computation.35 | async-start | bytes 1769472 | tf_op jit(solution)/shard_map/all_gather | solution.py:51
  546.3 515.3 %all-gather.104.cloned.1.call-start = ((), (), s32[]{:S(2)}) async-start(), calls=%async_computation.38 | async-start | bytes 1769472 | tf_op jit(solution)/shard_map/all_gather | solution.py:51
  547.1 542.2 %all-gather.110.cloned.1.call-start = ((), (), s32[]{:S(2)}) async-start(), calls=%async_computation.41 | async-start | bytes 1769472 | tf_op jit(solution)/shard_map/all_gather | solution.py:51
  547.8 568.9 %all-gather.116.cloned.1.call-start = ((), (), s32[]{:S(2)}) async-start(), calls=%async_computation.44 | async-start | bytes 1769472 | tf_op jit(solution)/shard_map/all_gather | solution.py:51
  548.4 596.0 %all-gather.122.cloned.1.call-start = ((), (), s32[]{:S(2)}) async-start(), calls=%async_computation.47 | async-start | bytes 1769472 | tf_op jit(solution)/shard_map/all_gather | solution.py:51
  549.1 622.7 %all-gather.128.cloned.1.call-start = ((), (), s32[]{:S(2)}) async-start(), calls=%async_computation.50 | async-start | bytes 1769472 | tf_op jit(solution)/shard_map/all_gather | solution.py:51
  549.7 649.6 %all-gather.134.cloned.1.call-start = ((), (), s32[]{:S(2)}) async-start(), calls=%async_computation.53 | async-start | bytes 1769472 | tf_op jit(solution)/shard_map/all_gather | solution.py:51
  550.3 676.6 %all-gather.140.cloned.1.call-start = ((), (), s32[]{:S(2)}) async-start(), calls=%async_computation.56 | async-start | bytes 1769472 | tf_op jit(solution)/shard_map/all_gather | solution.py:51
  551.1 703.5 %all-gather.142.cloned.1.call-start = ((), (), s32[]{:S(2)}) async-start(), calls=%async_computation.57 | async-start | bytes 1769472 | tf_op jit(solution)/shard_map/all_gather | solution.py:52
  551.8 730.2 %all-gather.136.cloned.1.call-start = ((), (), s32[]{:S(2)}) async-start(), calls=%async_computation.54 | async-start | bytes 1769472 | tf_op jit(solution)/shard_map/all_gather | solution.py:52
  552.4 757.2 %all-gather.130.cloned.1.call-start = ((), (), s32[]{:S(2)}) async-start(), calls=%async_computation.51 | async-start | bytes 1769472 | tf_op jit(solution)/shard_map/all_gather | solution.py:52
  553.1 784.1 %all-gather.124.cloned.1.call-start = ((), (), s32[]{:S(2)}) async-start(), calls=%async_computation.48 | async-start | bytes 1769472 | tf_op jit(solution)/shard_map/all_gather | solution.py:52
  553.9 810.8 %all-gather.118.cloned.1.call-start = ((), (), s32[]{:S(2)}) async-start(), calls=%async_computation.45 | async-start | bytes 1769472 | tf_op jit(solution)/shard_map/all_gather | solution.py:52
  554.4 837.8 %all-gather.112.cloned.1.call-start = ((), (), s32[]{:S(2)}) async-start(), calls=%async_computation.42 | async-start | bytes 1769472 | tf_op jit(solution)/shard_map/all_gather | solution.py:52
  555.2 864.7 %all-gather.106.cloned.1.call-start = ((), (), s32[]{:S(2)}) async-start(), calls=%async_computation.39 | async-start | bytes 1769472 | tf_op jit(solution)/shard_map/all_gather | solution.py:52
  555.9 891.4 %all-gather.100.cloned.1.call-start = ((), (), s32[]{:S(2)}) async-start(), calls=%async_computation.36 | async-start | bytes 1769472 | tf_op jit(solution)/shard_map/all_gather | solution.py:52
  556.5 918.3 %all-gather.94.cloned.1.call-start = ((), (), s32[]{:S(2)}) async-start(), calls=%async_computation.33 | async-start | bytes 1769472 | tf_op jit(solution)/shard_map/all_gather | solution.py:52
  557.1 1222.1 %reduce-scatter.43.cloned.1.call-start = ((), (), s32[]{:S(2)}) async-start(), calls=%async_computation.24 | async-start | bytes 7864320 | tf_op jit(solution)/shard_map/reduce_scatter | solution.py:41
  1896.2 580.5 %reduce-scatter.45.cloned.1.call-start = ((), (), s32[]{:S(2)}) async-start(), calls=%async_computation.26 | async-start | bytes 9437184 | tf_op jit(solution)/shard_map/reduce_scatter | solution.py:396
  2443.5 488.7 %reduce-scatter.67.cloned.1.call-start = ((), (), s32[]{:S(2)}) async-start(), calls=%async_computation.67 | async-start | bytes 5308416
  2455.5 534.0 %reduce-scatter.69.cloned.1.call-start = ((), (), s32[]{:S(2)}) async-start(), calls=%async_computation.68 | async-start | bytes 5308416
  2467.6 573.9 %reduce-scatter.49.cloned.1.call-start = ((), (), s32[]{:S(2)}) async-start(), calls=%async_computation.58 | async-start | bytes 3981312
  2486.7 667.8 %reduce-scatter.47.cloned.1.call-start = ((), (), s32[]{:S(2)}) async-start(), calls=%async_computation.27 | async-start | bytes 7864320 | tf_op jit(solution)/shard_map/reduce_scatter | solution.py:41
  (358 other events, 14025.1 us)
Sparse Core Ops, SparseCore 0:
  25.7 61.5 all-gather.69
  114.3 36.7 all-gather.71
  407.0 110.7 reduce-scatter.38
  519.8 63.8 all-gather.79
  585.8 61.9 all-gather.77
  675.9 25.6 all-gather.85
  759.0 25.6 all-gather.131
  815.2 25.6 all-gather.119
  1671.2 107.9 reduce-scatter.42
  1781.3 111.3 reduce-scatter.40
  1896.3 63.7 all-gather.81
  2345.0 69.8 reduce-scatter.44
  2418.7 53.8 reduce-scatter.50
  2475.9 53.8 reduce-scatter.52
  2533.7 53.8 reduce-scatter.54
  2590.9 53.8 reduce-scatter.56
  2648.5 53.8 reduce-scatter.58
  2705.7 53.8 reduce-scatter.60
  2763.3 53.8 reduce-scatter.62
  2820.5 53.8 reduce-scatter.64
  2878.3 53.8 reduce-scatter.66
  2935.5 53.8 reduce-scatter.68
  2993.3 48.0 reduce-scatter.48
  3043.7 110.7 reduce-scatter.46
  (29 shorter events, 737.2 us)
where the time goes:
time: 3200 us; the launch traced here: 3190 us
  waiting for transfers between devices  1550 us (48%)
  matrix products  543 us (17%)
  local copies, waits for them, and re-layouts  524 us (16%)
  other arithmetic  411 us (13%)
  blocking collectives  117 us (4%)
    unnamed x64, waiting for transfers between devices  503 us
    reduce_scatter x4, waiting for transfers between devices, features_reduce(): return lax.psum_scatter(values, 'col', scatter_dimension=1, tiled=True)  340 us
    all_gather x10, waiting for transfers between devices, expert_matrices(): lax.all_gather(w_up[:, expert], 'row', axis=0, tiled=True)  221 us
    all_gather x10, waiting for transfers between devices, expert_matrices(): lax.all_gather(w_down[:, expert], 'row', axis=0, tiled=True)  216 us
    unnamed x573, local copies, waits for them, and re-layouts  160 us
    all_gather x10, waiting for transfers between devices, expert_matrices(): lax.all_gather(w_gate[:, expert], 'row', axis=0, tiled=True)  129 us
    all_gather x4, waiting for transfers between devices, features_gather(): return lax.all_gather(values, 'col', axis=1, tiled=True)  87.5 us
    scatter-add x10, other arithmetic, body(): token_grads.at[tokens_e]  87.1 us
  transfers between devices with their start and end apart: 53, of which 42 were waited for; matrix products, arithmetic and copies ran while one was open for 28% of the time, Pallas kernels for 0%

commit v1 on v0

v1 whole, which is shorter than its diff:
```python
import functools

import jax
import jax.numpy as jnp
from jax import lax
from jax.experimental import pallas as pl
from jax.experimental.pallas import tpu as pltpu
from jax.sharding import Mesh
from jax.sharding import PartitionSpec as P

D = 1536
HD = 64
H = 512
KVH = 8
EXPERTS = 40
TOPK = 8
SEGS = 13
CAP = 230
SLOTS = 256

epsilon = 1e-06
branch_scale = 0.22
score_scale = 0.015625
rope_base = 10000.0
masked_score = -1e30

bf16 = jnp.bfloat16
f32 = jnp.float32
i32 = jnp.int32

QUERY_BLOCK = 256
KEY_BLOCK = 512
VMEM_LIMIT = 60 * 1024 * 1024


def dot(left, right):
    return jnp.dot(left, right, preferred_element_type=f32)


def dot_dims(left, right, left_dim, right_dim):
    return lax.dot_general(
        left, right, (((left_dim,), (right_dim,)), ((), ())), preferred_element_type=f32
    )


def swap(values, axis, bit):
    size = lax.axis_size(axis)
    return lax.ppermute(values, axis, [(i, i ^ bit) for i in range(size)])


def swap_core(values):
    return swap(values, "core", 1)


def chip_bits(chips):
    return [1 << b for b in range(chips.bit_length() - 1)]


def chip_gather(values, chips, descending):
    bits = chip_bits(chips)
    blocks = {0: values}
    for bit in reversed(bits) if descending else bits:
        for j in sorted(blocks):
            blocks[j ^ bit] = swap(blocks[j], "chip", bit)
    return [blocks[j] for j in range(chips)]


def chip_reduce(parts, chips, descending):
    blocks = dict(enumerate(parts))
    bits = chip_bits(chips)
    for bit in reversed(bits) if descending else bits:
        for j in sorted(blocks):
            if j & bit:
                continue
            taken = swap(blocks.pop(j ^ bit), "chip", bit)
            blocks[j] = (blocks[j].astype(f32) + taken.astype(f32)).astype(blocks[j].dtype)
    return blocks[0]


def own_and_other(values, core, share):
    if share == 1:
        return values[0], None
    mine = lax.dynamic_index_in_dim(values, core, 0, keepdims=False)
    other = lax.dynamic_index_in_dim(values, 1 - core, 0, keepdims=False)
    return mine, other


def in_core_order(mine, other, core):
    if other is None:
        return mine[None]
    first = core == 0
    return jnp.stack([jnp.where(first, mine, other), jnp.where(first, other, mine)])


def load_keys(offsets, parts, kv_rows, kv_columns):
    for n, part in enumerate(parts):
        count = part.shape[1]
        start = pl.multiple_of(offsets[n], count)
        kv_columns[:, pl.ds(start, count)] = part[...]
        kv_rows[pl.ds(start, count), :] = part[...].astype(f32).T.astype(bf16)


def visible(path_bits, key_bits, query_start, key_start, shape):
    keys = key_start + lax.broadcasted_iota(i32, shape, 0)
    queries = query_start + lax.broadcasted_iota(i32, shape, 1)
    return ((key_bits & path_bits) != 0) & (keys <= queries)


def attend_forward_kernel(
    offsets, starts, codes, query, path, key_bits, *rest, parts, key_blocks, key_block
):
    kv_parts = rest[:parts]
    out, log_total, kv_rows, kv_columns, padded, peak, total, mixed = rest[parts:]
    step = pl.program_id(0)
    heads, width, count = query.shape[1:]

    @pl.when(step == 0)
    def _():
        load_keys(offsets, kv_parts, kv_rows, kv_columns)
        padded[...] = jnp.zeros_like(padded)

    padded[:, :width, :] = query[0]
    peak[...] = jnp.full_like(peak, masked_score)
    total[...] = jnp.zeros_like(total)
    mixed[...] = jnp.zeros_like(mixed)

    def block(number, masked):
        start = pl.multiple_of(number * key_block, key_block)
        keys = kv_rows[pl.ds(start, key_block), :]
        values = kv_columns[width:, pl.ds(start, key_block)]
        if masked:
            allowed = visible(
                path[0], key_bits[pl.ds(start, key_block), :], starts[step], start, (key_block, count)
            )
        for head in range(heads):
            scores = dot(keys, padded[head])
            if masked:
                scores = jnp.where(allowed, scores, masked_score)
            old = peak[head]
            new = jnp.maximum(old, jnp.max(scores, axis=0, keepdims=True))
            weights = jnp.exp(scores - new)
            factor = jnp.exp(old - new)
            peak[head] = new
            total[head] = total[head] * factor + jnp.sum(weights, axis=0, keepdims=True)
            mixed[head] = mixed[head] * factor + dot(values, weights.astype(bf16))

    @pl.loop(0, key_blocks)
    def _(number):
        code = codes[step * key_blocks + number]

        @pl.when(code == 1)
        def _():
            block(number, True)

        @pl.when(code == 2)
        def _():
            block(number, False)

    for head in range(heads):
        out[0, head] = mixed[head] / total[head]
        log_total[0, head] = peak[head] + jnp.log(total[head])


def attend_backward_kernel(
    offsets,
    starts,
    codes,
    query,
    mixed_grad,
    mixed,
    log_total,
    path,
    key_bits,
    *rest,
    parts,
    key_blocks,
    key_block,
):
    kv_parts = rest[:parts]
    query_grad = rest[parts]
    grad_parts = rest[parts + 1 : 2 * parts + 1]
    (kv_rows, kv_columns, padded, padded_grad, query_rows, grad_rows, delta, query_sum, kv_sum) = rest[
        2 * parts + 1 :
    ]
    step = pl.program_id(0)
    heads, width, count = query.shape[1:]

    @pl.when(step == 0)
    def _():
        load_keys(offsets, kv_parts, kv_rows, kv_columns)
        padded[...] = jnp.zeros_like(padded)
        padded_grad[...] = jnp.zeros_like(padded_grad)
        kv_sum[...] = jnp.zeros_like(kv_sum)

    padded[:, :width, :] = query[0]
    padded_grad[:, width:, :] = mixed_grad[0]
    for head in range(heads):
        delta[head] = jnp.sum(mixed_grad[0, head].astype(f32) * mixed[0, head], axis=0, keepdims=True)
        query_rows[head] = padded[head].astype(f32).T.astype(bf16)
        grad_rows[head] = padded_grad[head].astype(f32).T.astype(bf16)
    query_sum[...] = jnp.zeros_like(query_sum)

    def block(number, masked):
        start = pl.multiple_of(number * key_block, key_block)
        keys = kv_rows[pl.ds(start, key_block), :]
        key_columns = kv_columns[:width, pl.ds(start, key_block)]
        if masked:
            allowed = visible(
                path[0], key_bits[pl.ds(start, key_block), :], starts[step], start, (key_block, count)
            )
        update = kv_sum[pl.ds(start, key_block), :]
        for head in range(heads):
            scores = dot(keys, padded[head])
            if masked:
                scores = jnp.where(allowed, scores, masked_score)
            weights = jnp.exp(scores - log_total[0, head])
            weight_grad = dot(keys, padded_grad[head])
            score_grad = (weights * (weight_grad - delta[head])).astype(bf16)
            update += dot(score_grad, query_rows[head]) + dot(weights.astype(bf16), grad_rows[head])
            query_sum[head] += dot(key_columns, score_grad)
        kv_sum[pl.ds(start, key_block), :] = update

    @pl.loop(0, key_blocks)
    def _(number):
        code = codes[step * key_blocks + number]

        @pl.when(code == 1)
        def _():
            block(number, True)

        @pl.when(code == 2)
        def _():
            block(number, False)

    query_grad[0] = score_scale * query_sum[...]

    @pl.when(step == pl.num_programs(0) - 1)
    def _():
        for n, part in enumerate(grad_parts):
            rows = part.shape[0]
            part[...] = kv_sum[pl.ds(pl.multiple_of(offsets[n], rows), rows), :].astype(part.dtype)


def whole(shape):
    return pl.BlockSpec(shape, lambda *_: (0,) * len(shape), pipeline_mode=pl.Buffered(1))


def attention_specs(groups, heads, rows, block):
    per_group = rows // block

    def four(step, *_):
        return (step // per_group, 0, 0, step % per_group)

    def three(step, *_):
        return (step // per_group, 0, step % per_group)

    return (
        pl.BlockSpec((1, heads, HD, block), four),
        pl.BlockSpec((1, heads, 1, block), four),
        pl.BlockSpec((1, 1, block), three),
    )


def attend_forward(offsets, starts, codes, query, path, key_bits, kv_parts):
    groups, heads, _, rows = query.shape
    block = min(QUERY_BLOCK, rows)
    tokens = key_bits.shape[0]
    key_block = min(KEY_BLOCK, tokens)
    wide, row, flat = attention_specs(groups, heads, rows, block)
    kernel = functools.partial(
        attend_forward_kernel,
        parts=len(kv_parts),
        key_blocks=tokens // key_block,
        key_block=key_block,
    )
    pairs = groups * heads * rows * tokens // 2
    return pl.pallas_call(
        kernel,
        name="attend_forward",
        grid_spec=pltpu.PrefetchScalarGridSpec(
            num_scalar_prefetch=3,
            grid=(groups * rows // block,),
            in_specs=[wide, flat, whole(key_bits.shape)] + [whole(p.shape) for p in kv_parts],
            out_specs=[wide, row],
            scratch_shapes=[
                pltpu.VMEM((tokens, 2 * HD), bf16),
                pltpu.VMEM((2 * HD, tokens), bf16),
                pltpu.VMEM((heads, 2 * HD, block), bf16),
                pltpu.VMEM((heads, 1, block), f32),
                pltpu.VMEM((heads, 1, block), f32),
                pltpu.VMEM((heads, HD, block), f32),
            ],
        ),
        out_shape=[
            jax.ShapeDtypeStruct(query.shape, f32),
            jax.ShapeDtypeStruct((groups, heads, 1, rows), f32),
        ],
        compiler_params=pltpu.CompilerParams(
            dimension_semantics=("arbitrary",), vmem_limit_bytes=VMEM_LIMIT
        ),
        cost_estimate=pl.CostEstimate(
            flops=4 * pairs * HD, transcendentals=pairs, bytes_accessed=8 * 1024 * 1024
        ),
    )(offsets, starts, codes, query, path, key_bits, *kv_parts)


def attend_backward(offsets, starts, codes, query, mixed_grad, mixed, log_total, path, key_bits, kv_parts):
    groups, heads, _, rows = query.shape
    block = min(QUERY_BLOCK, rows)
    tokens = key_bits.shape[0]
    key_block = min(KEY_BLOCK, tokens)
    part_rows = kv_parts[0].shape[1]
    wide, row, flat = attention_specs(groups, heads, rows, block)
    kernel = functools.partial(
        attend_backward_kernel,
        parts=len(kv_parts),
        key_blocks=tokens // key_block,
        key_block=key_block,
    )
    pairs = groups * heads * rows * tokens // 2
    grad_shape = (part_rows, 2 * HD)
    outs = pl.pallas_call(
        kernel,
        name="attend_backward",
        grid_spec=pltpu.PrefetchScalarGridSpec(
            num_scalar_prefetch=3,
            grid=(groups * rows // block,),
            in_specs=[wide, wide, wide, row, flat, whole(key_bits.shape)]
            + [whole(p.shape) for p in kv_parts],
            out_specs=[wide] + [whole(grad_shape) for _ in kv_parts],
            scratch_shapes=[
                pltpu.VMEM((tokens, 2 * HD), bf16),
                pltpu.VMEM((2 * HD, tokens), bf16),
                pltpu.VMEM((heads, 2 * HD, block), bf16),
                pltpu.VMEM((heads, 2 * HD, block), bf16),
                pltpu.VMEM((heads, block, 2 * HD), bf16),
                pltpu.VMEM((heads, block, 2 * HD), bf16),
                pltpu.VMEM((heads, 1, block), f32),
                pltpu.VMEM((heads, HD, block), f32),
                pltpu.VMEM((tokens, 2 * HD), f32),
            ],
        ),
        out_shape=[jax.ShapeDtypeStruct(query.shape, f32)]
        + [jax.ShapeDtypeStruct(grad_shape, bf16) for _ in kv_parts],
        compiler_params=pltpu.CompilerParams(
            dimension_semantics=("arbitrary",), vmem_limit_bytes=VMEM_LIMIT
        ),
        cost_estimate=pl.CostEstimate(
            flops=10 * pairs * HD, transcendentals=pairs, bytes_accessed=16 * 1024 * 1024
        ),
    )(offsets, starts, codes, query, mixed_grad, mixed, log_total, path, key_bits, *kv_parts)
    return outs[0], outs[1:]


def rank_kernel(first, route_rows, priority_rows, route_columns, priority_columns, out, *, experts):
    rows = route_rows.shape[2]
    never = rows * TOPK
    for e in range(experts):
        expert = first[0] + e
        along = jnp.min(
            jnp.where(route_rows[0] == expert, priority_rows[0], never), axis=0, keepdims=True
        )
        down = jnp.min(
            jnp.where(route_columns[0] == expert, priority_columns[0], never), axis=1, keepdims=True
        )
        count = jnp.zeros((8, rows), i32)
        for begin in range(0, rows, 8):
            count += (down[begin : begin + 8] < along).astype(i32)
        rank = jnp.sum(count, axis=0, keepdims=True)
        out[0, e : e + 1, :] = jnp.where((along < never) & (rank < CAP), rank, -1)


def slot_ranks(first, routes, priority, experts):
    groups, rows, _ = routes.shape
    tall = pl.BlockSpec((1, rows, TOPK), lambda g, *_: (g, 0, 0))
    flat = pl.BlockSpec((1, TOPK, rows), lambda g, *_: (g, 0, 0))
    padded = -(-experts // 8) * 8
    return pl.pallas_call(
        functools.partial(rank_kernel, experts=experts),
        name="slot_ranks",
        grid_spec=pltpu.PrefetchScalarGridSpec(
            num_scalar_prefetch=1,
            grid=(groups,),
            in_specs=[flat, flat, tall, tall],
            out_specs=pl.BlockSpec((1, padded, rows), lambda g, *_: (g, 0, 0)),
        ),
        out_shape=jax.ShapeDtypeStruct((groups, padded, rows), i32),
        compiler_params=pltpu.CompilerParams(vmem_limit_bytes=VMEM_LIMIT),
    )(
        first.reshape(1),
        routes.transpose(0, 2, 1),
        priority.transpose(0, 2, 1),
        routes,
        priority,
    )[:, :experts]


def expert_kernel(offsets, tokens, grads, ranks, gates, *rest, parts, groups):
    weights = rest[:parts]
    weighted_out, token_grad, inputs, slot_grads, hidden, pair_grads, matrices = rest[parts:]
    rows = tokens.shape[1]
    for n, part in enumerate(weights):
        count = part.shape[2]
        start = pl.multiple_of(offsets[n], count)
        for m in range(3):
            matrices[m, pl.ds(start, count), :] = part[0, m]
    slot = lax.broadcasted_iota(i32, (SLOTS, rows), 0)
    for g in range(groups):
        inside = slot == ranks[0, g]
        pick = inside.astype(bf16)
        weight = jnp.sum(jnp.where(inside, gates[0, g], 0.0), axis=1, keepdims=True)
        picked = dot(pick, tokens[g]).astype(bf16)
        inputs[0, g * SLOTS : (g + 1) * SLOTS, :] = picked
        gate_pre = dot(picked, matrices[0])
        up_pre = dot(picked, matrices[1])
        sigma = jax.nn.sigmoid(gate_pre)
        silu = gate_pre * sigma
        active = (silu * up_pre).astype(bf16)
        out = dot_dims(active, matrices[2], 1, 1)
        weighted_out[g, 0] = (out * weight).astype(bf16)
        upstream = dot(pick, grads[g])
        pair = jnp.sum(upstream * out, axis=1, keepdims=True)
        pair_grads[0, g] = jnp.sum(jnp.where(inside, pair, 0.0), axis=0, keepdims=True)
        slot_grad = (weight * upstream).astype(bf16)
        slot_grads[0, g * SLOTS : (g + 1) * SLOTS, :] = slot_grad
        act_grad = dot(slot_grad, matrices[2])
        gate_grad = (act_grad * up_pre * sigma * (1.0 + gate_pre * (1.0 - sigma))).astype(bf16)
        up_grad = (act_grad * silu).astype(bf16)
        hidden[0, 0, g * SLOTS : (g + 1) * SLOTS, :] = gate_grad
        hidden[0, 1, g * SLOTS : (g + 1) * SLOTS, :] = up_grad
        hidden[0, 2, g * SLOTS : (g + 1) * SLOTS, :] = active
        token_grad[g, 0] = (
            dot_dims(gate_grad, matrices[0], 1, 1) + dot_dims(up_grad, matrices[1], 1, 1)
        ).astype(bf16)


def run_experts(offsets, tokens, grads, ranks, gates, weight_parts):
    groups, rows, _ = tokens.shape
    experts, _, part_rows, _ = weight_parts[0].shape
    slots = groups * SLOTS
    per_expert = pl.BlockSpec((1, groups, 1, rows), lambda e, *_: (e, 0, 0, 0))
    by_group = pl.BlockSpec((groups, 1, SLOTS, D), lambda e, *_: (0, e, 0, 0))
    stash = pl.BlockSpec((1, slots, D), lambda e, *_: (e, 0, 0))
    flops = experts * slots * 2 * D * (2 * rows + 6 * H)
    return pl.pallas_call(
        functools.partial(expert_kernel, parts=len(weight_parts), groups=groups),
        name="experts",
        grid_spec=pltpu.PrefetchScalarGridSpec(
            num_scalar_prefetch=1,
            grid=(experts,),
            in_specs=[whole(tokens.shape), whole(grads.shape), per_expert, per_expert]
            + [pl.BlockSpec((1, 3, part_rows, H), lambda e, *_: (e, 0, 0, 0)) for _ in weight_parts],
            out_specs=[
                by_group,
                by_group,
                stash,
                stash,
                pl.BlockSpec((1, 3, slots, H), lambda e, *_: (e, 0, 0, 0)),
                per_expert,
            ],
            scratch_shapes=[pltpu.VMEM((3, D, H), bf16)],
        ),
        out_shape=[
            jax.ShapeDtypeStruct((groups, experts, SLOTS, D), bf16),
            jax.ShapeDtypeStruct((groups, experts, SLOTS, D), bf16),
            jax.ShapeDtypeStruct((experts, slots, D), bf16),
            jax.ShapeDtypeStruct((experts, slots, D), bf16),
            jax.ShapeDtypeStruct((experts, 3, slots, H), bf16),
            jax.ShapeDtypeStruct((experts, groups, 1, rows), f32),
        ],
        compiler_params=pltpu.CompilerParams(
            dimension_semantics=("arbitrary",), vmem_limit_bytes=VMEM_LIMIT
        ),
        cost_estimate=pl.CostEstimate(
            flops=flops, transcendentals=experts * slots * H, bytes_accessed=64 * 1024 * 1024
        ),
    )(offsets, tokens, grads, ranks, gates, *weight_parts)


def expert_grad_kernel(offsets, inputs, slot_grads, hidden, *rest, parts):
    outs = rest[:parts]
    total = rest[parts]
    for m in range(3):
        left = inputs if m < 2 else slot_grads
        total[...] = dot_dims(left[0], hidden[0, m], 0, 0)
        for n, out in enumerate(outs):
            count = out.shape[2]
            out[0, m] = total[pl.ds(pl.multiple_of(offsets[n], count), count), :].astype(bf16)


def expert_grads(offsets, inputs, slot_grads, hidden, parts, part_rows):
    experts, slots, _ = inputs.shape
    stash = pl.BlockSpec((1, slots, D), lambda e, *_: (e, 0, 0))
    return pl.pallas_call(
        functools.partial(expert_grad_kernel, parts=parts),
        name="expert_grads",
        grid_spec=pltpu.PrefetchScalarGridSpec(
            num_scalar_prefetch=1,
            grid=(experts,),
            in_specs=[stash, stash, pl.BlockSpec((1, 3, slots, H), lambda e, *_: (e, 0, 0, 0))],
            out_specs=[
                pl.BlockSpec((1, 3, part_rows, H), lambda e, *_: (e, 0, 0, 0)) for _ in range(parts)
            ],
            scratch_shapes=[pltpu.VMEM((D, H), f32)],
        ),
        out_shape=[jax.ShapeDtypeStruct((experts, 3, part_rows, H), bf16) for _ in range(parts)],
        compiler_params=pltpu.CompilerParams(
            dimension_semantics=("arbitrary",), vmem_limit_bytes=VMEM_LIMIT
        ),
        cost_estimate=pl.CostEstimate(
            flops=experts * slots * 2 * D * 3 * H, transcendentals=0, bytes_accessed=48 * 1024 * 1024
        ),
    )(offsets, inputs, slot_grads, hidden)


def combine_kernel(ranks, rows_in, out, *, experts):
    count = out.shape[0]
    slot = lax.broadcasted_iota(i32, (count, SLOTS), 1)
    pick = jnp.concatenate(
        [(ranks[:, e : e + 1] == slot).astype(bf16) for e in range(experts)], axis=1
    )
    out[...] = dot(pick, rows_in[...]).astype(bf16)


def combine(ranks, slot_rows):
    rows, experts = ranks.shape
    block = min(256, rows)
    return pl.pallas_call(
        functools.partial(combine_kernel, experts=experts),
        name="combine",
        grid=(rows // block,),
        in_specs=[
            pl.BlockSpec((block, experts), lambda i: (i, 0)),
            whole((experts * SLOTS, D)),
        ],
        out_specs=pl.BlockSpec((block, D), lambda i: (i, 0)),
        out_shape=jax.ShapeDtypeStruct((rows, D), bf16),
        compiler_params=pltpu.CompilerParams(vmem_limit_bytes=VMEM_LIMIT),
        cost_estimate=pl.CostEstimate(
            flops=2 * rows * experts * SLOTS * D, transcendentals=0, bytes_accessed=8 * 1024 * 1024
        ),
    )(ranks, slot_rows.reshape(experts * SLOTS, D))


def rotate(values, cosine, sine):
    first = values[..., : HD // 2, :]
    second = values[..., HD // 2 :, :]
    return jnp.concatenate([first * cosine - second * sine, second * cosine + first * sine], axis=-2)


def tree_tables(ancestry, own_all, token_starts, query_block, key_block):
    groups, rows, _ = ancestry.shape
    tokens = own_all.shape[0]
    segments = jnp.arange(SEGS, dtype=i32)
    index = jnp.arange(tokens, dtype=i32)
    member = own_all[None, :] == segments[:, None]
    begin = jnp.min(jnp.where(member, index[None, :], tokens), axis=1)
    length = jnp.sum(member.astype(i32), axis=1)
    on_path = jnp.any(ancestry[:, :, :, None] == segments, axis=2)
    at = token_starts[:, None] + jnp.arange(rows, dtype=i32)[None, :]
    before = jnp.clip(at[:, :, None] - begin, 0, length)
    position = jnp.sum(jnp.where(on_path, before, 0), axis=2)
    bits = jnp.sum(on_path.astype(i32) << segments, axis=2)
    blocked = on_path.reshape(groups * rows // query_block, query_block, SEGS)
    path_any = jnp.any(blocked, axis=1)
    path_all = jnp.all(blocked, axis=1)
    keys = jnp.any(member.reshape(SEGS, tokens // key_block, key_block), axis=2).T
    some = jnp.any(path_any[:, None, :] & keys[None, :, :], axis=2)
    every = jnp.all(path_all[:, None, :] | ~keys[None, :, :], axis=2)
    query_start = at.reshape(-1, query_block)[:, 0]
    key_start = jnp.arange(tokens // key_block, dtype=i32) * key_block
    some &= key_start[None, :] < query_start[:, None] + query_block
    every &= key_start[None, :] + key_block <= query_start[:, None] + 1
    codes = jnp.where(some, jnp.where(every, 2, 1), 0).astype(i32)
    return position, bits, query_start, codes.reshape(-1)


def body(
    layer_input,
    cotangent,
    gain_attention,
    gain_mixture,
    w_query,
    w_key,
    w_value,
    w_out,
    w_router,
    w_gate,
    w_up,
    w_down,
    routes,
    priority,
    ancestry,
):
    chips, share, columns = lax.axis_size("chip"), lax.axis_size("core"), lax.axis_size("col")
    chip, core, column = lax.axis_index("chip"), lax.axis_index("core"), lax.axis_index("col")
    row_axes = ("chip", "core")
    rows, width = layer_input.shape
    weight_rows = w_query.shape[0]
    query_heads = w_query.shape[1] // HD
    key_heads = w_key.shape[1] // HD
    group = query_heads // key_heads
    own_heads = key_heads // share
    experts = w_gate.shape[1] // share
    tokens_all = rows * chips * share
    query_block = min(QUERY_BLOCK, rows)
    key_block = min(KEY_BLOCK, tokens_all)
    token_block = rows // columns

    places = jnp.stack(
        [(chip ^ j) * share + (core ^ h) for j in range(chips) for h in range(share)]
    ).astype(i32)
    token_offsets = places * rows
    feature_offsets = places * weight_rows

    def both(values):
        return jnp.stack([values] + ([swap_core(values)] if share == 2 else []))

    def gather_parts(own, other):
        halves = [chip_gather(own, chips, False)]
        if share == 2:
            halves.append(chip_gather(other, chips, True))
        return [halves[h][j] for j in range(chips) for h in range(share)]

    def reduce_parts(parts):
        own = chip_reduce(parts[0::share], chips, False)
        other = chip_reduce(parts[1::share], chips, True) if share == 2 else None
        return own, other

    x_full = lax.all_gather(layer_input, "col", axis=1, tiled=True)
    own_all = lax.all_gather(ancestry[:, 0], row_axes, axis=0, tiled=True)
    project = lax.all_gather(
        jnp.concatenate([w_query, w_key, w_value], axis=1), row_axes, axis=0, tiled=True
    )
    gains = lax.all_gather(jnp.stack([gain_attention, gain_mixture]), "col", axis=1, tiled=True)
    cotangent_full = lax.all_gather(cotangent, "col", axis=1, tiled=True)
    out_columns = lax.all_gather(w_out, "col", axis=1, tiled=True)
    out_router = lax.all_gather(
        jnp.concatenate([out_columns, w_router], axis=1), row_axes, axis=0, tiled=True
    )
    index_arrays = both(jnp.concatenate([routes, priority, ancestry], axis=1))
    all_routes = index_arrays[:, :, :TOPK]
    all_priority = index_arrays[:, :, TOPK : 2 * TOPK]
    all_ancestry = index_arrays[:, :, 2 * TOPK :]

    stacked = jnp.stack([w_gate, w_up, w_down]).transpose(2, 0, 1, 3)
    stacked = stacked.reshape(share, experts, 3, weight_rows, H)
    own_weights, other_weights = own_and_other(stacked, core, share)
    weight_parts = gather_parts(
        own_weights, swap_core(other_weights) if share == 2 else None
    )

    token_starts = jnp.stack([(chip * share + (core ^ g)) * rows for g in range(share)]).astype(i32)
    position, path_bits, query_starts, codes = tree_tables(
        all_ancestry, own_all, token_starts, query_block, key_block
    )
    key_bits = (jnp.int32(1) << own_all)[:, None]
    frequency = rope_base ** (-(jnp.arange(HD // 2, dtype=f32) * 2.0) / HD)
    angle = position.astype(f32)[:, None, :] * frequency[None, :, None]
    cosine, sine = jnp.cos(angle), jnp.sin(angle)
    first_expert = (column * (experts * share) + core * experts).astype(i32)
    ranks = slot_ranks(first_expert, all_routes, all_priority, experts)
    rank_columns = ranks.transpose(0, 2, 1)
    expert_ids = jnp.arange(EXPERTS, dtype=i32)
    chosen = jnp.any(all_routes[:, None, :, :] == expert_ids[None, :, None, None], axis=3)

    x_wide = x_full.astype(f32)
    inverse_one = lax.rsqrt(jnp.mean(x_wide * x_wide, axis=1, keepdims=True) + epsilon)
    h_one = (x_wide * inverse_one * gains[0][None, :]).astype(bf16)
    projected = dot_dims(project, h_one, 0, 1)
    query_width, key_width = query_heads * HD, key_heads * HD
    query = rotate(
        projected[:query_width].reshape(share, own_heads, group, HD, rows), cosine[0], sine[0]
    )
    query = (query.astype(bf16).astype(f32) * score_scale).astype(bf16)
    keys = rotate(
        projected[query_width : query_width + key_width].reshape(share, own_heads, HD, rows),
        cosine[0],
        sine[0],
    ).astype(bf16)
    values = projected[query_width + key_width :].reshape(share, own_heads, HD, rows).astype(bf16)
    sent = jnp.concatenate(
        [keys[:, :, None], values[:, :, None], query], axis=2
    )
    own_sent, other_sent = own_and_other(sent, core, share)
    received = [own_sent] + ([swap_core(other_sent)] if share == 2 else [])
    query_groups = jnp.stack([r[:, 2:] for r in received], axis=1)
    pairs = [r[:, :2].reshape(own_heads, 2 * HD, rows) for r in received]
    kv_parts = gather_parts(pairs[0], pairs[-1])

    attend_outs = [
        attend_forward(
            token_offsets,
            query_starts,
            codes,
            query_groups[head],
            path_bits[:, None, :],
            key_bits,
            [p[head] for p in kv_parts],
        )
        for head in range(own_heads)
    ]
    mixed_f = jnp.stack([o[0] for o in attend_outs])
    mixed_b = mixed_f.astype(bf16)
    mixed_own = mixed_b[:, 0]
    mixed_other = swap_core(mixed_b[:, 1]) if share == 2 else None
    mixed = in_core_order(mixed_own, mixed_other, core).reshape(query_width, rows)
    mixed_full = lax.all_gather(mixed, "col", axis=0, tiled=True)
    full_out = out_router[:, :D]
    full_router = out_router[:, D:]
    branch = dot_dims(mixed_full, full_out, 0, 1)
    x_middle = x_wide + branch_scale * branch
    inverse_two = lax.rsqrt(jnp.mean(x_middle * x_middle, axis=1, keepdims=True) + epsilon)
    h_two = (x_middle * inverse_two * gains[1][None, :]).astype(bf16)
    h_two_groups = both(h_two)
    grad_out = cotangent_full.astype(f32)
    mix_grads = both((branch_scale * grad_out).astype(bf16))

    logits = lax.dot_general(
        full_router, h_two_groups, (((0,), (2,)), ((), ())), preferred_element_type=f32
    ).transpose(1, 0, 2)
    shown = jnp.where(chosen, logits, masked_score)
    raised = jnp.where(chosen, jnp.exp(logits - jnp.max(shown, axis=1, keepdims=True)), 0.0)
    gates = raised / jnp.sum(raised, axis=1, keepdims=True)
    own_gates = lax.dynamic_slice_in_dim(gates, first_expert, experts, 1)
    weighted_out, slot_token_grads, inputs, slot_grads, hidden, pair_rows = run_experts(
        feature_offsets,
        h_two_groups,
        mix_grads,
        ranks.transpose(1, 0, 2)[:, :, None, :],
        own_gates.transpose(1, 0, 2)[:, :, None, :],
        weight_parts,
    )

    def combine_groups(slot_rows):
        if share == 1:
            return combine(rank_columns[0], slot_rows[0])
        received = swap_core(combine(rank_columns[1], slot_rows[1]))
        own = combine(rank_columns[0], slot_rows[0])
        return (own.astype(f32) + received.astype(f32)).astype(bf16)

    token_sum = combine_groups(slot_token_grads)
    token_grads = lax.psum_scatter(token_sum, "col", scatter_dimension=0, tiled=True).astype(f32)
    grad_parts = expert_grads(
        feature_offsets, inputs, slot_grads, hidden, chips * share, weight_rows
    )
    own_sums, other_sums = reduce_parts(grad_parts)
    returned = swap_core(other_sums) if share == 2 else None
    matrix_sums = in_core_order(own_sums, returned, core).reshape(
        share * experts, 3, weight_rows, H
    )
    matrix_grads = matrix_sums.astype(f32).transpose(1, 2, 0, 3)
    mix_sum = combine_groups(weighted_out)
    mix_slice = lax.psum_scatter(mix_sum, "col", scatter_dimension=1, tiled=True).astype(f32)
    feature_start = column * width
    x_middle_slice = lax.dynamic_slice_in_dim(x_middle, feature_start, width, 1)
    result = (x_middle_slice + branch_scale * mix_slice).astype(bf16)

    pair_rows = pair_rows[:, :, 0]
    pair_other = swap_core(pair_rows[:, 1]) if share == 2 else None
    pair_columns = in_core_order(pair_rows[:, 0], pair_other, core).reshape(share * experts, rows)
    pair_grad = lax.all_gather(pair_columns, "col", axis=0, tiled=True)
    picked_grad = gates[0] * (pair_grad - jnp.sum(gates[0] * pair_grad, axis=0, keepdims=True))
    logit_grad = picked_grad.astype(bf16)

    token_start = column * token_block

    def own_tokens(array):
        return lax.dynamic_slice_in_dim(array, token_start, token_block, 0)

    h_two_grad = token_grads + dot_dims(
        lax.dynamic_slice_in_dim(logit_grad, token_start, token_block, 1), full_router, 0, 1
    )
    x_part, inverse_part = own_tokens(x_middle), own_tokens(inverse_two)
    scaled_two = h_two_grad * gains[1][None, :]
    inner_two = jnp.sum(scaled_two * x_part, axis=1, keepdims=True)
    x_middle_grad = (
        own_tokens(grad_out) + inverse_part * scaled_two - x_part * inverse_part**3 * inner_two / D
    )
    gain_mixture_part = jnp.sum(h_two_grad * x_part * inverse_part, axis=0)
    branch_grad = lax.all_gather(
        (branch_scale * x_middle_grad).astype(bf16), "col", axis=0, tiled=True
    )

    own_out = lax.dynamic_slice_in_dim(full_out, column * query_width, query_width, 1)
    mixed_grad = dot_dims(own_out, branch_grad, 0, 1).astype(bf16)
    own_grad, other_grad = own_and_other(
        mixed_grad.reshape(share, own_heads, group, HD, rows), core, share
    )
    grad_groups = jnp.stack(
        [own_grad] + ([swap_core(other_grad)] if share == 2 else []), axis=1
    )
    backward_outs = [
        attend_backward(
            token_offsets,
            query_starts,
            codes,
            query_groups[head],
            grad_groups[head],
            attend_outs[head][0],
            attend_outs[head][1],
            path_bits[:, None, :],
            key_bits,
            [p[head] for p in kv_parts],
        )
        for head in range(own_heads)
    ]
    query_grad = jnp.stack([o[0] for o in backward_outs])
    query_grad = rotate(
        query_grad, cosine[None, :, None], -sine[None, :, None]
    ).astype(bf16)
    query_other = swap_core(query_grad[:, 1]) if share == 2 else None
    query_pre_grad = in_core_order(query_grad[:, 0], query_other, core).reshape(query_width, rows)
    kv_own, kv_other = reduce_parts(
        [jnp.stack([o[1][n] for o in backward_outs]) for n in range(chips * share)]
    )
    kv_other = swap_core(kv_other) if share == 2 else None
    kv_grad = in_core_order(kv_own, kv_other, core).astype(f32)
    kv_grad = kv_grad.transpose(0, 1, 3, 2).reshape(key_heads, 2 * HD, rows)
    key_pre_grad = (
        rotate(kv_grad[:, :HD], cosine[0], -sine[0]).astype(bf16).reshape(key_width, rows)
    )
    value_pre_grad = kv_grad[:, HD:].astype(bf16).reshape(key_width, rows)
    project_grad = jnp.concatenate([query_pre_grad, key_pre_grad, value_pre_grad], axis=0)

    h_one_part = dot_dims(project_grad, project, 0, 1)
    inner_one = lax.psum(
        jnp.sum(h_one_part * gains[0][None, :] * x_wide, axis=1), "col"
    )[:, None]
    h_one_grad = lax.psum_scatter(
        h_one_part.astype(bf16), "col", scatter_dimension=1, tiled=True
    ).astype(f32)
    x_slice = layer_input.astype(f32)
    middle_slice = lax.dynamic_slice_in_dim(branch_grad, feature_start, width, 1).astype(f32)
    input_grad = (
        middle_slice * (1.0 / branch_scale)
        + inverse_one * h_one_grad * gain_attention[None, :]
        - x_slice * inverse_one**3 * inner_one / D
    )
    gain_attention_part = jnp.sum(h_one_grad * x_slice * inverse_one, axis=0)

    early = jnp.concatenate(
        [dot_dims(branch_grad, mixed, 0, 1), dot_dims(h_two, logit_grad, 0, 1)], axis=1
    )
    early_sums = lax.psum_scatter(
        early.astype(bf16), row_axes, scatter_dimension=0, tiled=True
    ).astype(f32)
    late_sums = lax.psum_scatter(
        dot_dims(h_one, project_grad, 0, 1).astype(bf16), row_axes, scatter_dimension=0, tiled=True
    ).astype(f32)
    gain_parts = jnp.stack(
        [
            lax.dynamic_update_slice_in_dim(
                jnp.zeros((D,), f32), gain_attention_part, feature_start, 0
            ),
            gain_mixture_part,
        ]
    )
    gain_sums = lax.dynamic_slice_in_dim(
        lax.psum(gain_parts, ("chip", "core", "col")), feature_start, width, 1
    )
    return (
        result,
        input_grad,
        gain_sums[0],
        gain_sums[1],
        late_sums[:, :query_width],
        late_sums[:, query_width : query_width + key_width],
        late_sums[:, query_width + key_width :],
        early_sums[:, :query_width],
        early_sums[:, query_width:],
        matrix_grads[0],
        matrix_grads[1],
        matrix_grads[2],
    )


def solution(mesh):
    rows, columns = mesh.shape["row"], mesh.shape["col"]
    halves = rows % 2 == 0 and EXPERTS // columns % 2 == 0 and KVH // columns % 2 == 0
    share = 2 if halves else 1
    split = Mesh(mesh.devices.reshape(rows // share, share, columns), ("chip", "core", "col"))
    row = ("chip", "core")
    return jax.shard_map(
        body,
        mesh=split,
        in_specs=(
            P(row, "col"),
            P(row, "col"),
            P("col"),
            P("col"),
            P(row, "col"),
            P(row, "col"),
            P(row, "col"),
            P(row, "col"),
            P(row, None),
            P(row, "col", None),
            P(row, "col", None),
            P(row, "col", None),
            P(row, None),
            P(row, None),
            P(row, None),
        ),
        out_specs=(
            P(row, "col"),
            P(row, "col"),
            P("col"),
            P("col"),
            P(row, "col"),
            P(row, "col"),
            P(row, "col"),
            P(row, "col"),
            P(row, None),
            P(row, "col", None),
            P(row, "col", None),
            P(row, "col", None),
        ),
        check_vma=False,
    )
```

time: 3200 us -> 1100 us (0.34)
  waiting for transfers between devices: 1550 us -> 366 us
  matrix products: 543 us -> 34.1 us
  local copies, waits for them, and re-layouts: 524 us -> 89.5 us
  other arithmetic: 411 us -> 111 us
  Pallas kernels: 0 us -> 193 us
  starting transfers between devices: 3.25 us -> 171 us
    all_gather x37 -> x6, waiting for transfers between devices: 706 us -> 84.5 us  [the longest x1 49.2 us: body(): mixed_full = lax.all_gather(mixed, 'col', axis=0, tiled=True)]
    dot_general x205 -> x9, matrix products: 543 us -> 34.1 us  [the longest x8 30.5 us: dot_dims(): lax.dot_general(left, right, (((left_dim,), (right_dim,)), ((), ())), pre...]
    unnamed x64 -> x14, waiting for transfers between devices: 503 us -> 1.53 us
    reduce_scatter x5 -> x2, waiting for transfers between devices: 340 us -> 32.3 us  [the longest x1 32.3 us: body(): lax.psum_scatter(token_sum, 'col', scatter_dimension=0, tiled=True)]
    ppermute x0 -> x37, waiting for transfers between devices: none -> 248 us  [swap(): return lax.ppermute(values, axis, [(i, i ^ bit) for i in range(size)])]
    pallas_call x0 -> x9, Pallas kernels: none -> 193 us  [the longest x1 57.5 us: run_experts(): pl.pallas_call(functools.partial(expert_kernel, parts=len(weight_parts),...]
    scatter-add x30 -> x0, other arithmetic: 189 us -> none  [the longest x10 87.1 us: body(): token_grads.at[tokens_e]]
    ppermute x0 -> x37, starting transfers between devices: none -> 169 us  [swap(): return lax.ppermute(values, axis, [(i, i ^ bit) for i in range(size)])]
  transfers between devices with their start and end apart: 53 -> 48, of which waited for: 42 -> 21; matrix products, arithmetic and copies ran while one was open for 28% -> 19% of each run, Pallas kernels for 0% -> 12%
where the time goes in v1:
time: 1100 us; the launch traced here: 1090 us
  waiting for transfers between devices  366 us (33%)
  Pallas kernels  193 us (18%)
  starting transfers between devices  171 us (16%)
  blocking collectives  115 us (10%)
  other arithmetic  111 us (10%)
  local copies, waits for them, and re-layouts  89.5 us (8%)
  matrix products  34.1 us (3%)
  between operations  15.1 us (1%)
    ppermute x37, waiting for transfers between devices, swap(): return lax.ppermute(values, axis, [(i, i ^ bit) for i in range(size)])  248 us
    ppermute x37, starting transfers between devices, swap(): return lax.ppermute(values, axis, [(i, i ^ bit) for i in range(size)])  169 us
    pallas_call x1, Pallas kernels, run_experts(): pl.pallas_call(functools.partial(expert_kernel, parts=len(weight_parts),...  57.5 us
    all_gather x1, waiting for transfers between devices, body(): mixed_full = lax.all_gather(mixed, 'col', axis=0, tiled=True)  49.2 us
    psum x1, blocking collectives, body(): lax.psum(gain_parts, ('chip', 'core', 'col'))  38.9 us
    pallas_call x1, Pallas kernels, attend_backward(): pl.pallas_call(kernel, name='attend_backward', grid_spec=pltpu.PrefetchSc...  38.2 us
    pallas_call x1, Pallas kernels, attend_forward(): pl.pallas_call(kernel, name='attend_forward', grid_spec=pltpu.PrefetchSca...  33.5 us
    pallas_call x4, Pallas kernels, combine(): pl.pallas_call(functools.partial(combine_kernel, experts=experts), name='...  32.5 us
  transfers between devices with their start and end apart: 48, of which 21 were waited for; matrix products, arithmetic and copies ran while one was open for 19% of the time, Pallas kernels for 12%

profile of v1, /device:TPU:0, one launch (start us, length us, event | category | flops | bytes accessed | tf_op | source)
XLA Modules:
  0.0 1093.6 jit_solution(16567244700585747132)
XLA Ops:
  11.4 24.3 %all_gather.35 = bf16[192,1536]{1,0:T(8,128)(2,1)S(1)} all-gather(bf16[192,384]{1,0:T(8,128)(2,1)} %param.22), channel_id=1, replica_groups=mesh['chip'=4,'core'=2,'col'=4] {'col'}, dimensions={1}, use_global_device_ids=true | all-gather | bytes 737280 | tf_op jit(solution)/shard_map/all_gather | solution.py:637
  50.4 15.0 %all_gather.33 = f32[2,1536]{1,0:T(2,128)S(1)} all-gather(f32[2,384]{1,0:T(2,128)S(1)} %pad_maximum_fusion.17), channel_id=1, replica_groups=mesh['chip'=4,'core'=2,'col'=4] {'col'}, dimensions={1}, use_global_device_ids=true | all-gather | bytes 15360 | tf_op jit(solution)/shard_map/all_gather | solution.py:635
  70.8 9.5 all-gather.9.cloned.1.call-done
  83.7 25.7 %all-gather.11.cloned.1.call-done = bf16[1536,640]{1,0:T(8,128)(2,1)} async-done(((bf16[192,640]{1,0:T(8,128)(2,1)}), bf16[1536,640]{1,0:T(8,128)(2,1)}) %all-gather.11.cloned.1.call-update) | async-done | bytes 1966096 | tf_op jit(solution)/shard_map/all_gather | solution.py:632
  141.4 33.5 %attend_forward.1 = (f32[2,3,64,1024]{3,2,1,0:T(8,128)}, f32[2,3,1,1024]{3,2,1,0:T(1,128)}) custom-call(s32[8]{0:T(128)} %get-tuple-element.216.offsets, s32[8]{0:T(128)} %get-tuple-element.159.starts, s32[128]{0:T(128)} %select_n.117.codes, bf16[2,3,64,1024]{3,2,1,0:T(8,128)(2,1)} %maximum_bitcast_fusion.query, s32[2,1,1024]{2,1,0:T(1,128)} %broadcast_in_dim.50.path, ...), custom_call_target="tpu_custom_call" | custom-call | flops 6442450944 | bytes 8388608 | tf_op jit(solution)/shard_map/attend_forward/pallas_call | solution.py:277
  189.5 41.1 %collective-permute-start.12 = (bf16[5,3,192,512]{3,2,1,0:T(8,128)(2,1)}, bf16[5,3,192,512]{3,2,1,0:T(8,128)(2,1)}, u32[]{:S(2)}, u32[]{:S(2)}) collective-permute-start(bf16[5,3,192,512]{3,2,1,0:T(8,128)(2,1)} %bitcast.232.rest_0_), channel_id=1, source_target_pairs={{0,8},{8,0},{16,24},{24,16},{1,9},{9,1},{17,25},{25,17},{2,10},{10... | collective-permute-start | bytes 8847368 | tf_op jit(solution)/shard_map/ppermute | solution.py:48
  230.6 31.1 %collective-permute-start.15 = (bf16[5,3,192,512]{3,2,1,0:T(8,128)(2,1)}, bf16[5,3,192,512]{3,2,1,0:T(8,128)(2,1)}, u32[]{:S(2)}, u32[]{:S(2)}) collective-permute-start(bf16[5,3,192,512]{3,2,1,0:T(8,128)(2,1)} %collective-permute-done.11.rest_1_), channel_id=1, source_target_pairs={{0,16},{8,24},{16,0},{24,8},{1,17},{9,25},{17,1},{25,9},{2,18},{10... | collective-permute-start | bytes 8847368 | tf_op jit(solution)/shard_map/ppermute | solution.py:48
  267.2 49.2 %all-gather.13.cloned.1.call-done = bf16[1536,1024]{1,0:T(8,128)(2,1)} async-done(((bf16[384,1024]{1,0:T(8,128)(2,1)}), bf16[1536,1024]{1,0:T(8,128)(2,1)}) %all-gather.13.cloned.1.call-update) | async-done | bytes 3145744 | tf_op jit(solution)/shard_map/all_gather | solution.py:708
  374.6 19.9 %collective-permute-done.14.rest_4_ = bf16[5,3,192,512]{3,2,1,0:T(8,128)(2,1)} collective-permute-done((bf16[5,3,192,512]{3,2,1,0:T(8,128)(2,1)}, bf16[5,3,192,512]{3,2,1,0:T(8,128)(2,1)}, u32[]{:S(2)}, u32[]{:S(2)}) %collective-permute-start.14) | collective-permute-done | bytes 2949152 | tf_op jit(solution)/shard_map/ppermute | solution.py:48
  394.5 62.8 %collective-permute-done.16.rest_6_ = bf16[5,3,192,512]{3,2,1,0:T(8,128)(2,1)} collective-permute-done((bf16[5,3,192,512]{3,2,1,0:T(8,128)(2,1)}, bf16[5,3,192,512]{3,2,1,0:T(8,128)(2,1)}, u32[]{:S(2)}, u32[]{:S(2)}) %collective-permute-start.16) | collective-permute-done | bytes 2949152 | tf_op jit(solution)/shard_map/ppermute | solution.py:48
  457.3 25.8 %collective-permute-done.17.rest_7_ = bf16[5,3,192,512]{3,2,1,0:T(8,128)(2,1)} collective-permute-done((bf16[5,3,192,512]{3,2,1,0:T(8,128)(2,1)}, bf16[5,3,192,512]{3,2,1,0:T(8,128)(2,1)}, u32[]{:S(2)}, u32[]{:S(2)}) %collective-permute-start.17) | collective-permute-done | bytes 2949152 | tf_op jit(solution)/shard_map/ppermute | solution.py:48
  483.1 57.5 %experts.1 = (bf16[2,5,256,1536]{3,2,1,0:T(8,128)(2,1)}, bf16[2,5,256,1536]{3,2,1,0:T(8,128)(2,1)}, bf16[5,512,1536]{2,1,0:T(8,128)(2,1)}, bf16[5,512,1536]{2,1,...) custom-call(s32[8]{0:T(128)} %get-tuple-element.217.offsets, ...), custom_call_target="tpu_custom_call" | custom-call | flops 40265318400 | bytes 67108864 | tf_op jit(solution)/shard_map/experts/pallas_call | solution.py:445
  576.4 17.9 %all-gather.1 = f32[4,10,1024]{2,1,0:T(8,128)} all-gather(f32[1,10,1024]{2,1,0:T(8,128)S(1)} %reshape.404), channel_id=1, replica_groups=mesh['chip'=4,'core'=2,'col'=4] {'col'}, dimensions={0}, use_global_device_ids=true | all-gather | bytes 204800 | tf_op jit(solution)/shard_map/all_gather | solution.py:762
  597.8 32.3 %reduce-scatter.12.cloned.1.call-done = bf16[256,1536]{1,0:T(8,128)(2,1)} async-done(((bf16[1024,1536]{1,0:T(8,128)(2,1)}), bf16[256,1536]{1,0:T(8,128)(2,1)}) %reduce-scatter.12.cloned.1.call-update) | async-done | bytes 786448 | tf_op jit(solution)/shard_map/reduce_scatter | solution.py:743
  675.1 22.4 %expert_grads.1 = (bf16[5,3,192,512]{3,2,1,0:T(8,128)(2,1)}, bf16[5,3,192,512]{3,2,1,0:T(8,128)(2,1)}, bf16[5,3,192,512]{3,2,1,0:T(8,128)(2,1)}, bf16[5,3,192,51...) custom-call(s32[8]{0:T(128)} %get-tuple-element.217.offsets, ...), custom_call_target="tpu_custom_call" | custom-call | flops 12079595520 | bytes 50331648 | tf_op jit(solution)/shard_map/expert_grads/pallas_call | solution.py:494
  709.6 38.2 %attend_backward.1 = (f32[2,3,64,1024]{3,2,1,0:T(8,128)}, bf16[1024,128]{1,0:T(8,128)(2,1)}, bf16[1024,128]{1,0:T(8,128)(2,1)}, bf16[1024,128]{1,0:T(8,128)(2,1)...) custom-call(s32[8]{0:T(128)} %get-tuple-element.216.offsets, ...), custom_call_target="tpu_custom_call" | custom-call | flops 16106127360 | bytes 16777216 | tf_op jit(solution)/shard_map/attend_backward/pallas_call | solution.py:322
  747.9 42.5 %collective-permute-start.24 = (bf16[1,1024,128]{2,1,0:T(8,128)(2,1)}, bf16[1,1024,128]{2,1,0:T(8,128)(2,1)S(1)}, u32[]{:S(2)}, u32[]{:S(2)}) collective-permute-start(bf16[1,1024,128]{2,1,0:T(8,128)(2,1)} %bitcast.291), channel_id=1, source_target_pairs={{0,8},{8,0},{16,24},{24,16},{1,9},{9,1},{17,25},{25,17},{2,10},{10... | collective-permute-start | bytes 786440 | tf_op jit(solution)/shard_map/ppermute | solution.py:48
  790.4 33.4 %collective-permute-start.27 = (bf16[1,1024,128]{2,1,0:T(8,128)(2,1)}, bf16[1,1024,128]{2,1,0:T(8,128)(2,1)S(1)}, u32[]{:S(2)}, u32[]{:S(2)}) collective-permute-start(bf16[1,1024,128]{2,1,0:T(8,128)(2,1)} %bitcast.292), channel_id=1, source_target_pairs={{0,16},{8,24},{16,0},{24,8},{1,17},{9,25},{17,1},{25,9},{2,18},{10... | collective-permute-start | bytes 786440 | tf_op jit(solution)/shard_map/ppermute | solution.py:48
  883.3 37.0 %collective-permute-done.33 = bf16[5,3,192,512]{3,2,1,0:T(8,128)(2,1)} collective-permute-done((bf16[5,3,192,512]{3,2,1,0:T(8,128)(2,1)}, bf16[5,3,192,512]{3,2,1,0:T(8,128)(2,1)}, u32[]{:S(2)}, u32[]{:S(2)}) %collective-permute-start.33) | collective-permute-done | bytes 2949152 | tf_op jit(solution)/shard_map/ppermute | solution.py:48
  920.3 20.9 %collective-permute-done.35 = bf16[5,3,192,512]{3,2,1,0:T(8,128)(2,1)} collective-permute-done((bf16[5,3,192,512]{3,2,1,0:T(8,128)(2,1)}, bf16[5,3,192,512]{3,2,1,0:T(8,128)(2,1)}, u32[]{:S(2)}, u32[]{:S(2)}) %collective-permute-start.35) | collective-permute-done | bytes 2949152 | tf_op jit(solution)/shard_map/ppermute | solution.py:48
  948.0 53.8 %collective-permute-done.30 = bf16[5,3,192,512]{3,2,1,0:T(8,128)(2,1)} collective-permute-done((bf16[5,3,192,512]{3,2,1,0:T(8,128)(2,1)}, bf16[5,3,192,512]{3,2,1,0:T(8,128)(2,1)}, u32[]{:S(2)}, u32[]{:S(2)}) %collective-permute-start.30) | collective-permute-done | bytes 2949152 | tf_op jit(solution)/shard_map/ppermute | solution.py:48
  1013.3 9.4 slice_bitcast_fusion
  1026.7 9.4 psum.14
  1047.3 38.9 %psum.15 = f32[2,1536]{1,0:T(2,128)S(1)} all-reduce(f32[2,1536]{1,0:T(2,128)S(1)} %pad_maximum_fusion.16), channel_id=1, replica_groups=mesh['chip'=4,'core'=2,'col'=4] {'chip','core','col'}, use_global_device_ids=true, to_apply=%region_24.25 | all-reduce | flops 3072 | bytes 24576 | tf_op jit(solution)/shard_map/psum | solution.py:860
  (348 shorter events, 326.8 us)
Async XLA Ops:
  7.2 73.1 %all-gather.9.cloned.1.call-start = ((), (), s32[]{:S(2)}) async-start(), calls=%async_computation.5 | async-start | bytes 3932160 | tf_op jit(solution)/shard_map/all_gather | solution.py:630
  8.0 101.4 %all-gather.11.cloned.1.call-start = ((), (), s32[]{:S(2)}) async-start(), calls=%async_computation.6 | async-start | bytes 2211840 | tf_op jit(solution)/shard_map/all_gather | solution.py:632
  9.7 252.0 %all-gather.17.cloned.1.call-start = ((), (), s32[]{:S(2)}) async-start(), calls=%async_computation.9 | async-start | bytes 3932160 | tf_op jit(solution)/shard_map/all_gather | solution.py:636
  10.5 256.8 %all-gather.15.cloned.1.call-start = ((), (), s32[]{:S(2)}) async-start(), calls=%async_computation.8 | async-start | bytes 5750784 | tf_op jit(solution)/shard_map/all_gather | solution.py:638
  36.6 279.9 %all-gather.13.cloned.1.call-start = ((), (), s32[]{:S(2)}) async-start(), calls=%async_computation.7 | async-start | bytes 3932160 | tf_op jit(solution)/shard_map/all_gather | solution.py:708
  182.4 447.7 %reduce-scatter.12.cloned.1.call-start = ((), (), s32[]{:S(2)}) async-start(), calls=%async_computation.10 | async-start | bytes 3932160 | tf_op jit(solution)/shard_map/reduce_scatter | solution.py:743
  189.5 164.0 %collective-permute-start.12 = (bf16[5,3,192,512]{3,2,1,0:T(8,128)(2,1)}, bf16[5,3,192,512]{3,2,1,0:T(8,128)(2,1)}, u32[]{:S(2)}, u32[]{:S(2)}) collective-permute-start(bf16[5,3,192,512]{3,2,1,0:T(8,128)(2,1)} %bitcast.232.rest_0_), channel_id=1, source_target_pairs={{0,8},{8,0},{16,24},{24,16},{1,9},{9,1},{17,25},{25,17},{2,10},{10... | collective-permute-start | bytes 8847368 | tf_op jit(solution)/shard_map/ppermute | solution.py:48
  230.6 124.4 %collective-permute-start.15 = (bf16[5,3,192,512]{3,2,1,0:T(8,128)(2,1)}, bf16[5,3,192,512]{3,2,1,0:T(8,128)(2,1)}, u32[]{:S(2)}, u32[]{:S(2)}) collective-permute-start(bf16[5,3,192,512]{3,2,1,0:T(8,128)(2,1)} %collective-permute-done.11.rest_1_), channel_id=1, source_target_pairs={{0,16},{8,24},{16,0},{24,8},{1,17},{9,25},{17,1},{25,9},{2,18},{10... | collective-permute-start | bytes 8847368 | tf_op jit(solution)/shard_map/ppermute | solution.py:48
  267.2 88.3 %collective-permute-start.10 = (bf16[1024,1536]{1,0:T(8,128)(2,1)}, bf16[1024,1536]{1,0:T(8,128)(2,1)}, u32[]{:S(2)}, u32[]{:S(2)}) collective-permute-start(bf16[1024,1536]{1,0:T(8,128)(2,1)} %get-tuple-element.175), channel_id=1, source_target_pairs={{0,4},{4,0},{1,5},{5,1},{2,6},{6,2},{3,7},{7,3},{8,12},{12,8},{9,1... | collective-permute-start | bytes 9437192 | tf_op jit(solution)/shard_map/ppermute | solution.py:48
  353.5 103.8 %collective-permute-start.13 = (bf16[5,3,192,512]{3,2,1,0:T(8,128)(2,1)}, bf16[5,3,192,512]{3,2,1,0:T(8,128)(2,1)}, u32[]{:S(2)}, u32[]{:S(2)}) collective-permute-start(bf16[5,3,192,512]{3,2,1,0:T(8,128)(2,1)} %collective-permute-done.11.rest_1_), channel_id=1, source_target_pairs={{0,8},{8,0},{16,24},{24,16},{1,9},{9,1},{17,25},{25,17},{2,10},{10... | collective-permute-start | bytes 8847368 | tf_op jit(solution)/shard_map/ppermute | solution.py:48
  355.0 102.3 %collective-permute-start.16 = (bf16[5,3,192,512]{3,2,1,0:T(8,128)(2,1)}, bf16[5,3,192,512]{3,2,1,0:T(8,128)(2,1)}, u32[]{:S(2)}, u32[]{:S(2)}) collective-permute-start(bf16[5,3,192,512]{3,2,1,0:T(8,128)(2,1)} %collective-permute-done.12.rest_2_), channel_id=1, source_target_pairs={{0,16},{8,24},{16,0},{24,8},{1,17},{9,25},{17,1},{25,9},{2,18},{10... | collective-permute-start | bytes 8847368 | tf_op jit(solution)/shard_map/ppermute | solution.py:48
  355.6 127.5 %collective-permute-start.17 = (bf16[5,3,192,512]{3,2,1,0:T(8,128)(2,1)}, bf16[5,3,192,512]{3,2,1,0:T(8,128)(2,1)}, u32[]{:S(2)}, u32[]{:S(2)}) collective-permute-start(bf16[5,3,192,512]{3,2,1,0:T(8,128)(2,1)} %collective-permute-done.15.rest_5_), channel_id=1, source_target_pairs={{0,8},{8,0},{16,24},{24,16},{1,9},{9,1},{17,25},{25,17},{2,10},{10... | collective-permute-start | bytes 8847368 | tf_op jit(solution)/shard_map/ppermute | solution.py:48
  567.7 133.4 %all-gather.19.cloned.1.call-start = ((), (), s32[]{:S(2)}) async-start(), calls=%async_computation.11 | async-start | bytes 3932160 | tf_op jit(solution)/shard_map/all_gather | solution.py:781
  636.1 386.6 %reduce-scatter.16.cloned.1.call-start = ((), (), s32[]{:S(2)}) async-start(), calls=%async_computation.13 | async-start | bytes 3932160
  668.3 367.9 %reduce-scatter.20.cloned.1.call-start = ((), (), s32[]{:S(2)}) async-start(), calls=%async_computation.15 | async-start | bytes 1769472
  697.6 170.6 %collective-permute-start.31 = (bf16[5,3,192,512]{3,2,1,0:T(8,128)(2,1)}, bf16[5,3,192,512]{3,2,1,0:T(8,128)(2,1)}, u32[]{:S(2)}, u32[]{:S(2)}) collective-permute-start(bf16[5,3,192,512]{3,2,1,0:T(8,128)(2,1)} %get-tuple-element.57), channel_id=1, source_target_pairs={{0,8},{8,0},{16,24},{24,16},{1,9},{9,1},{17,25},{25,17},{2,10},{10... | collective-permute-start | bytes 8847368 | tf_op jit(solution)/shard_map/ppermute | solution.py:48
  699.0 161.7 %collective-permute-start.34 = (bf16[5,3,192,512]{3,2,1,0:T(8,128)(2,1)}, bf16[5,3,192,512]{3,2,1,0:T(8,128)(2,1)}, u32[]{:S(2)}, u32[]{:S(2)}) collective-permute-start(bf16[5,3,192,512]{3,2,1,0:T(8,128)(2,1)} %get-tuple-element.61), channel_id=1, source_target_pairs={{0,16},{8,24},{16,0},{24,8},{1,17},{9,25},{17,1},{25,9},{2,18},{10... | collective-permute-start | bytes 8847368 | tf_op jit(solution)/shard_map/ppermute | solution.py:48
  708.2 331.4 %reduce-scatter.14.cloned.1.call-start = ((), (), s32[]{:S(2)}) async-start(), calls=%async_computation.12 | async-start | bytes 2211840 | tf_op jit(solution)/shard_map/reduce_scatter | solution.py:848
  747.9 84.4 %collective-permute-start.24 = (bf16[1,1024,128]{2,1,0:T(8,128)(2,1)}, bf16[1,1024,128]{2,1,0:T(8,128)(2,1)S(1)}, u32[]{:S(2)}, u32[]{:S(2)}) collective-permute-start(bf16[1,1024,128]{2,1,0:T(8,128)(2,1)} %bitcast.291), channel_id=1, source_target_pairs={{0,8},{8,0},{16,24},{24,16},{1,9},{9,1},{17,25},{25,17},{2,10},{10... | collective-permute-start | bytes 786440 | tf_op jit(solution)/shard_map/ppermute | solution.py:48
  845.3 75.0 %collective-permute-start.33 = (bf16[5,3,192,512]{3,2,1,0:T(8,128)(2,1)}, bf16[5,3,192,512]{3,2,1,0:T(8,128)(2,1)}, u32[]{:S(2)}, u32[]{:S(2)}) collective-permute-start(bf16[5,3,192,512]{3,2,1,0:T(8,128)(2,1)} %get-tuple-element.59), channel_id=1, source_target_pairs={{0,16},{8,24},{16,0},{24,8},{1,17},{9,25},{17,1},{25,9},{2,18},{10... | collective-permute-start | bytes 8847368 | tf_op jit(solution)/shard_map/ppermute | solution.py:48
  860.5 182.3 %reduce-scatter.18.cloned.1.call-start = ((), (), s32[]{:S(2)}) async-start(), calls=%async_computation.14 | async-start | bytes 3932160
  866.1 75.0 %collective-permute-start.35 = (bf16[5,3,192,512]{3,2,1,0:T(8,128)(2,1)}, bf16[5,3,192,512]{3,2,1,0:T(8,128)(2,1)}, u32[]{:S(2)}, u32[]{:S(2)}) collective-permute-start(bf16[5,3,192,512]{3,2,1,0:T(8,128)(2,1)} %add_convert_fusion.3), channel_id=1, source_target_pairs={{0,8},{8,0},{16,24},{24,16},{1,9},{9,1},{17,25},{25,17},{2,10},{10... | collective-permute-start | bytes 8847368 | tf_op jit(solution)/shard_map/ppermute | solution.py:48
  866.7 135.1 %collective-permute-start.30 = (bf16[5,3,192,512]{3,2,1,0:T(8,128)(2,1)}, bf16[5,3,192,512]{3,2,1,0:T(8,128)(2,1)}, u32[]{:S(2)}, u32[]{:S(2)}) collective-permute-start(bf16[5,3,192,512]{3,2,1,0:T(8,128)(2,1)} %get-tuple-element.55), channel_id=1, source_target_pairs={{0,8},{8,0},{16,24},{24,16},{1,9},{9,1},{17,25},{25,17},{2,10},{10... | collective-permute-start | bytes 8847368 | tf_op jit(solution)/shard_map/ppermute | solution.py:48
  872.8 129.0 %collective-permute-start.32 = (bf16[5,3,192,512]{3,2,1,0:T(8,128)(2,1)}, bf16[5,3,192,512]{3,2,1,0:T(8,128)(2,1)}, u32[]{:S(2)}, u32[]{:S(2)}) collective-permute-start(bf16[5,3,192,512]{3,2,1,0:T(8,128)(2,1)} %add_convert_fusion.6), channel_id=1, source_target_pairs={{0,16},{8,24},{16,0},{24,8},{1,17},{9,25},{17,1},{25,9},{2,18},{10... | collective-permute-start | bytes 8847368 | tf_op jit(solution)/shard_map/ppermute | solution.py:48
  (69 other events, 1486.7 us)
Sparse Core Ops, SparseCore 0:
  9.6 70.6 all-gather.8
  82.8 26.5 all-gather.10
  110.9 63.4 all-gather.16
  176.1 39.1 all-gather.14
  216.7 99.7 all-gather.12
  567.8 62.2 reduce-scatter.11
  636.2 63.5 all-gather.18
  702.1 58.8 reduce-scatter.15
  764.3 38.4 reduce-scatter.19
  860.6 46.8 reduce-scatter.13
  909.9 60.2 reduce-scatter.17

commit v2 on v1

v2 whole, which is shorter than its diff:
```python
import functools

import jax
import jax.numpy as jnp
from jax import lax
from jax.experimental.layout import Layout, with_layout_constraint
from jax.experimental import pallas as pl
from jax.experimental.pallas import tpu as pltpu
from jax.sharding import Mesh
from jax.sharding import PartitionSpec as P

D = 1536
HD = 64
H = 512
KVH = 8
EXPERTS = 40
TOPK = 8
SEGS = 13
CAP = 230
SLOTS = 256

epsilon = 1e-06
branch_scale = 0.22
score_scale = 0.015625
rope_base = 10000.0
masked_score = -1e30

bf16 = jnp.bfloat16
f32 = jnp.float32
i32 = jnp.int32

QUERY_BLOCK = 512
KEY_BLOCK = 512
VMEM_LIMIT = 60 * 1024 * 1024


def dot(left, right):
    return jnp.dot(left, right, preferred_element_type=f32)


def dot_dims(left, right, left_dim, right_dim):
    return lax.dot_general(
        left, right, (((left_dim,), (right_dim,)), ((), ())), preferred_element_type=f32
    )


def swap(values, axis, bit):
    size = lax.axis_size(axis)
    return lax.ppermute(values, axis, [(i, i ^ bit) for i in range(size)])


def swap_core(values):
    return swap(values, "core", 1)


def chip_bits(chips):
    return [1 << b for b in range(chips.bit_length() - 1)]


def half_bits(chips, half):
    bits = chip_bits(chips)
    return bits if half == 0 else bits[::-1]


def gather_rounds(chips, halves):
    rounds = []
    for level in range(len(chip_bits(chips))):
        moves = []
        for half in range(halves):
            bits = half_bits(chips, half)
            held = [0]
            for bit in bits[:level]:
                held += [j ^ bit for j in held]
            moves.append([(half, j, bits[level]) for j in sorted(held)])
        rounds += [list(r) for r in zip(*moves)]
    return rounds


def run_gather(held, rounds):
    held = dict(held)
    for moves in rounds:
        for half, j, bit in moves:
            held[half, j ^ bit] = swap(held[half, j], "chip", bit)
    return held


def gather_parts(values, chips):
    held = run_gather(
        {(h, 0): v for h, v in enumerate(values)}, gather_rounds(chips, len(values))
    )
    return listed(held, chips)


def listed(held, chips):
    halves = len(held) // chips
    return [held[h, j] for j in range(chips) for h in range(halves)]


def reduce_levels(chips, halves):
    levels = []
    for level in range(len(chip_bits(chips))):
        moves = []
        for half in range(halves):
            bits = half_bits(chips, half)
            done = sum(bits[: level + 1])
            moves.append([(half, j, bits[level]) for j in range(chips) if not j & done])
        levels.append([list(r) for r in zip(*moves)])
    return levels


def take(held, moves):
    return {(h, j): swap(held[h, j ^ bit], "chip", bit) for h, j, bit in moves}


def add_taken(held, taken):
    sums = {k: (held[k].astype(f32) + v.astype(f32)).astype(v.dtype) for k, v in taken.items()}
    return {**held, **sums}


def reduce_parts(parts, chips, share):
    held = {(h, j): parts[j * share + h] for j in range(chips) for h in range(share)}
    for rounds in reduce_levels(chips, share):
        taken = {}
        for moves in rounds:
            taken.update(take(held, moves))
        held = add_taken(held, taken)
    return [held[h, 0] for h in range(share)]


def column_shifts(values_for):
    size = lax.axis_size("col")
    me = lax.axis_index("col")
    return [
        (
            (me - d) % size,
            lax.ppermute(values_for((me + d) % size), "col", [(i, (i + d) % size) for i in range(size)]),
        )
        for d in range(1, size)
    ]


def column_sum(values):
    for _, other in column_shifts(lambda _: values):
        values = values + other
    return values


def column_rows(values):
    rows = values.shape[0]
    size = lax.axis_size("col")
    out = jnp.zeros((size * rows,) + values.shape[1:], values.dtype)
    for c, part in [(lax.axis_index("col"), values)] + column_shifts(lambda _: values):
        out = lax.dynamic_update_slice_in_dim(out, part, c * rows, 0)
    return out


def row_sum(values):
    chips, share = lax.axis_size("chip"), lax.axis_size("core")
    size = chips * share
    total = values
    for n in range(1, size):
        total = total + lax.ppermute(values, ("chip", "core"), [(i, i ^ n) for i in range(size)])
    return total


def tie(*trees):
    return lax.optimization_barrier(trees)


def own_and_other(values, core, share):
    if share == 1:
        return values[0], None
    mine = lax.dynamic_index_in_dim(values, core, 0, keepdims=False)
    other = lax.dynamic_index_in_dim(values, 1 - core, 0, keepdims=False)
    return mine, other


def in_core_order(mine, other, core):
    if other is None:
        return mine[None]
    first = core == 0
    return jnp.stack([jnp.where(first, mine, other), jnp.where(first, other, mine)])


def column_of(row):
    return jnp.broadcast_to(row, (8, row.shape[1])).T[:, :1]


def attend_forward_kernel(
    offsets, starts, codes, query, path, key_bits, *rest, parts, key_blocks, key_block
):
    kv_parts = rest[:parts]
    out, rounded, log_total, key_columns, value_rows, query_rows, peak, mixed, paths = rest[parts:]
    step = pl.program_id(0)
    heads, width, count = query.shape[1:]

    @pl.when(step == 0)
    def _():
        for n, part in enumerate(kv_parts):
            rows = part.shape[1]
            start = pl.multiple_of(offsets[n], rows)
            key_columns[:, pl.ds(start, rows)] = part[:width, :]
            turned = pltpu.roll(part[...].astype(f32).T, width, 1)
            lane = lax.broadcasted_iota(i32, turned.shape, 1)
            value_rows[pl.ds(start, rows), :] = jnp.where(lane < width, turned, 1.0).astype(bf16)

    for head in range(heads):
        query_rows[head * count : (head + 1) * count] = query[0, head].astype(f32).T.astype(bf16)
    paths[...] = jnp.broadcast_to(path[0], (8, count)).T
    peak[...] = jnp.full_like(peak, masked_score)
    mixed[...] = jnp.zeros_like(mixed)

    def block(number, masked):
        start = pl.multiple_of(number * key_block, key_block)
        scores = dot(query_rows[...], key_columns[:, pl.ds(start, key_block)])
        if masked:
            keys = start + lax.broadcasted_iota(i32, (count, key_block), 1)
            queries = starts[step] + lax.broadcasted_iota(i32, (count, key_block), 0)
            on_path = (paths[:, :1] & key_bits[:, pl.ds(start, key_block)]) != 0
            allowed = on_path & (keys <= queries)
            scores = jnp.where(
                allowed[None], scores.reshape(heads, count, key_block), masked_score
            ).reshape(heads * count, key_block)
        old = peak[...]
        new = jnp.maximum(old, jnp.max(scores, axis=1, keepdims=True))
        weights = jnp.exp(scores - jnp.tile(new, (1, key_block // 128))).astype(bf16)
        mixed[...] = mixed[...] * jnp.exp(old - new) + dot(
            weights, value_rows[pl.ds(start, key_block), :]
        )
        peak[...] = new

    @pl.loop(0, key_blocks)
    def _(number):
        code = codes[step * key_blocks + number]

        @pl.when(code == 1)
        def _():
            block(number, True)

        @pl.when(code == 2)
        def _():
            block(number, False)

    lane = lax.broadcasted_iota(i32, (count, 2 * width), 1)
    for head in range(heads):
        at = slice(head * count, (head + 1) * count)
        sums = mixed[at]
        turned = jnp.where(
            lane < width, sums / pltpu.roll(sums, width, 1), peak[at] + jnp.log(sums)
        ).T
        out[0, head] = turned[:width]
        rounded[0, head] = turned[:width].astype(bf16)
        log_total[0, head] = turned[width : width + 1]


def attend_backward_kernel(
    offsets,
    starts,
    codes,
    query,
    mixed_grad,
    mixed,
    log_total,
    path,
    key_bits,
    *rest,
    parts,
    key_blocks,
    key_block,
):
    kv_parts = rest[:parts]
    query_grad = rest[parts]
    grad_parts = rest[parts + 1 : 2 * parts + 1]
    (kv_rows, key_columns, padded, padded_grad, query_rows, grad_rows, row_terms, query_sum, kv_sum) = (
        rest[2 * parts + 1 :]
    )
    step = pl.program_id(0)
    heads, width, count = query.shape[1:]

    @pl.when(step == 0)
    def _():
        for n, part in enumerate(kv_parts):
            rows = part.shape[1]
            start = pl.multiple_of(offsets[n], rows)
            key_columns[:, pl.ds(start, rows)] = part[:width, :]
            kv_rows[pl.ds(start, rows), :] = part[...].astype(f32).T.astype(bf16)
        padded[...] = jnp.zeros_like(padded)
        padded_grad[...] = jnp.zeros_like(padded_grad)
        kv_sum[...] = jnp.zeros_like(kv_sum)

    for head in range(heads):
        at = slice(head * count, (head + 1) * count)
        padded[:width, at] = query[0, head]
        padded_grad[width:, at] = mixed_grad[0, head]
        row_terms[0:1, at] = log_total[0, head]
        row_terms[1:2, at] = jnp.sum(
            mixed_grad[0, head].astype(f32) * mixed[0, head], axis=0, keepdims=True
        )
    query_rows[...] = padded[...].astype(f32).T.astype(bf16)
    grad_rows[...] = padded_grad[...].astype(f32).T.astype(bf16)
    query_sum[...] = jnp.zeros_like(query_sum)

    def block(number, masked):
        start = pl.multiple_of(number * key_block, key_block)
        rows = kv_rows[pl.ds(start, key_block), :]
        scores = dot(rows, padded[...])
        if masked:
            keys = start + lax.broadcasted_iota(i32, (key_block, count), 0)
            queries = starts[step] + lax.broadcasted_iota(i32, (key_block, count), 1)
            on_path = (path[0] & column_of(key_bits[:, pl.ds(start, key_block)])) != 0
            allowed = on_path & (keys <= queries)
            scores = jnp.where(jnp.concatenate([allowed] * heads, axis=1), scores, masked_score)
        weights = jnp.exp(scores - row_terms[0:1, :])
        weight_grad = dot(rows, padded_grad[...])
        score_grad = (weights * (weight_grad - row_terms[1:2, :])).astype(bf16)
        kv_sum[pl.ds(start, key_block), :] += dot(score_grad, query_rows[...]) + dot(
            weights.astype(bf16), grad_rows[...]
        )
        query_sum[...] += dot(key_columns[:, pl.ds(start, key_block)], score_grad)

    @pl.loop(0, key_blocks)
    def _(number):
        code = codes[step * key_blocks + number]

        @pl.when(code == 1)
        def _():
            block(number, True)

        @pl.when(code == 2)
        def _():
            block(number, False)

    for head in range(heads):
        query_grad[0, head] = score_scale * query_sum[:, head * count : (head + 1) * count]

    @pl.when(step == pl.num_programs(0) - 1)
    def _():
        for n, part in enumerate(grad_parts):
            rows = part.shape[0]
            part[...] = kv_sum[pl.ds(pl.multiple_of(offsets[n], rows), rows), :].astype(part.dtype)


def whole(shape):
    return pl.BlockSpec(shape, lambda *_: (0,) * len(shape), pipeline_mode=pl.Buffered(1))


def attention_specs(heads, rows, block):
    per_group = rows // block

    def four(step, *_):
        return (step // per_group, 0, 0, step % per_group)

    return pl.BlockSpec((1, heads, HD, block), four), pl.BlockSpec((1, heads, 1, block), four)


def attend_forward(offsets, starts, codes, query, path_bits, key_bits, kv_parts):
    groups, heads, _, rows = query.shape
    block = min(QUERY_BLOCK, rows)
    per_group = rows // block
    tokens = key_bits.shape[1]
    key_block = min(KEY_BLOCK, tokens)
    wide, row = attention_specs(heads, rows, block)
    kernel = functools.partial(
        attend_forward_kernel,
        parts=len(kv_parts),
        key_blocks=tokens // key_block,
        key_block=key_block,
    )
    return pl.pallas_call(
        kernel,
        name="attend_forward",
        grid_spec=pltpu.PrefetchScalarGridSpec(
            num_scalar_prefetch=3,
            grid=(groups * per_group,),
            in_specs=[
                wide,
                pl.BlockSpec((1, 1, block), lambda s, *_: (s // per_group, 0, s % per_group)),
                whole(key_bits.shape),
            ]
            + [whole(p.shape) for p in kv_parts],
            out_specs=[wide, wide, row],
            scratch_shapes=[
                pltpu.VMEM((HD, tokens), bf16),
                pltpu.VMEM((tokens, 2 * HD), bf16),
                pltpu.VMEM((heads * block, HD), bf16),
                pltpu.VMEM((heads * block, 2 * HD), f32),
                pltpu.VMEM((heads * block, 2 * HD), f32),
                pltpu.VMEM((block, 8), i32),
            ],
        ),
        out_shape=[
            jax.ShapeDtypeStruct(query.shape, f32),
            jax.ShapeDtypeStruct(query.shape, bf16),
            jax.ShapeDtypeStruct((groups, heads, 1, rows), f32),
        ],
        compiler_params=pltpu.CompilerParams(
            dimension_semantics=("arbitrary",), vmem_limit_bytes=VMEM_LIMIT
        ),
    )(offsets, starts, codes, query, path_bits[:, None, :], key_bits, *kv_parts)


def attend_backward(
    offsets, starts, codes, query, mixed_grad, mixed, log_total, path_bits, key_bits, kv_parts
):
    groups, heads, _, rows = query.shape
    block = min(QUERY_BLOCK, rows)
    per_group = rows // block
    tokens = key_bits.shape[1]
    key_block = min(KEY_BLOCK, tokens)
    wide, row = attention_specs(heads, rows, block)
    grad_shape = (kv_parts[0].shape[1], 2 * HD)
    kernel = functools.partial(
        attend_backward_kernel,
        parts=len(kv_parts),
        key_blocks=tokens // key_block,
        key_block=key_block,
    )
    outs = pl.pallas_call(
        kernel,
        name="attend_backward",
        grid_spec=pltpu.PrefetchScalarGridSpec(
            num_scalar_prefetch=3,
            grid=(groups * per_group,),
            in_specs=[
                wide,
                wide,
                wide,
                row,
                pl.BlockSpec((1, 1, block), lambda s, *_: (s // per_group, 0, s % per_group)),
                whole(key_bits.shape),
            ]
            + [whole(p.shape) for p in kv_parts],
            out_specs=[wide] + [whole(grad_shape) for _ in kv_parts],
            scratch_shapes=[
                pltpu.VMEM((tokens, 2 * HD), bf16),
                pltpu.VMEM((HD, tokens), bf16),
                pltpu.VMEM((2 * HD, heads * block), bf16),
                pltpu.VMEM((2 * HD, heads * block), bf16),
                pltpu.VMEM((heads * block, 2 * HD), bf16),
                pltpu.VMEM((heads * block, 2 * HD), bf16),
                pltpu.VMEM((8, heads * block), f32),
                pltpu.VMEM((HD, heads * block), f32),
                pltpu.VMEM((tokens, 2 * HD), f32),
            ],
        ),
        out_shape=[jax.ShapeDtypeStruct(query.shape, f32)]
        + [jax.ShapeDtypeStruct(grad_shape, bf16) for _ in kv_parts],
        compiler_params=pltpu.CompilerParams(
            dimension_semantics=("arbitrary",), vmem_limit_bytes=VMEM_LIMIT
        ),
    )(
        offsets,
        starts,
        codes,
        query,
        mixed_grad,
        mixed,
        log_total,
        path_bits[:, None, :],
        key_bits,
        *kv_parts,
    )
    return outs[0], outs[1:]


def rank_kernel(first, route_rows, priority_rows, route_columns, priority_columns, out, *, experts):
    rows = route_rows.shape[2]
    never = rows * TOPK
    for e in range(experts):
        expert = first[0] + e
        along = jnp.min(
            jnp.where(route_rows[0] == expert, priority_rows[0], never), axis=0, keepdims=True
        )
        down = jnp.min(
            jnp.where(route_columns[0] == expert, priority_columns[0], never), axis=1, keepdims=True
        )
        count = jnp.zeros((8, rows), i32)
        for begin in range(0, rows, 8):
            count += (down[begin : begin + 8] < along).astype(i32)
        rank = jnp.sum(count, axis=0, keepdims=True)
        out[0, e : e + 1, :] = jnp.where((along < never) & (rank < CAP), rank, -1)
    if out.shape[1] > experts:
        out[0, experts:, :] = jnp.full((out.shape[1] - experts, rows), -1, i32)


def slot_ranks(first, routes, priority, experts):
    groups, rows, _ = routes.shape
    tall = pl.BlockSpec((1, rows, TOPK), lambda g, *_: (g, 0, 0))
    flat = pl.BlockSpec((1, TOPK, rows), lambda g, *_: (g, 0, 0))
    padded = -(-experts // 8) * 8
    return pl.pallas_call(
        functools.partial(rank_kernel, experts=experts),
        name="slot_ranks",
        grid_spec=pltpu.PrefetchScalarGridSpec(
            num_scalar_prefetch=1,
            grid=(groups,),
            in_specs=[flat, flat, tall, tall],
            out_specs=pl.BlockSpec((1, padded, rows), lambda g, *_: (g, 0, 0)),
        ),
        out_shape=jax.ShapeDtypeStruct((groups, padded, rows), i32),
        compiler_params=pltpu.CompilerParams(vmem_limit_bytes=VMEM_LIMIT),
    )(
        first.reshape(1),
        routes.transpose(0, 2, 1),
        priority.transpose(0, 2, 1),
        routes,
        priority,
    )


def expert_kernel(offsets, first, ranks, *rest, parts, groups):
    gates, rest = rest[:groups], rest[groups:]
    tokens, rest = rest[:groups], rest[groups:]
    grads, rest = rest[:groups], rest[groups:]
    weights = rest[:parts]
    weighted_out, token_grad, inputs, slot_grads, hidden, pair_grads, matrices = rest[parts:]
    rows = tokens[0].shape[0]
    e = pl.program_id(0)
    for n, part in enumerate(weights):
        count = part.shape[2]
        for m in range(3):
            matrices[m, pl.ds(pl.multiple_of(offsets[n], count), count), :] = part[m, 0]
    slot = lax.broadcasted_iota(i32, (SLOTS, rows), 0)
    for g in range(groups):
        at = slice(g * SLOTS, (g + 1) * SLOTS)
        inside = slot == ranks[g, pl.ds(e, 1), :]
        pick = inside.astype(bf16)
        gate = gates[g][pl.ds(first[0] + e, 1), :]
        weight = jnp.sum(jnp.where(inside, gate, 0.0), axis=1, keepdims=True)
        picked = dot(pick, tokens[g][...]).astype(bf16)
        inputs[0, at, :] = picked
        gate_pre = dot(picked, matrices[0])
        up_pre = dot(picked, matrices[1])
        sigma = jax.nn.sigmoid(gate_pre)
        silu = gate_pre * sigma
        active = (silu * up_pre).astype(bf16)
        out = dot_dims(active, matrices[2], 1, 1)
        weighted_out[g, 0] = (out * weight).astype(bf16)
        upstream = dot(pick, grads[g][...])
        pair = jnp.sum(upstream * out, axis=1, keepdims=True)
        pair_grads[g, pl.ds(e, 1), :] = jnp.sum(jnp.where(inside, pair, 0.0), axis=0, keepdims=True)
        slot_grad = (weight * upstream).astype(bf16)
        slot_grads[0, at, :] = slot_grad
        act_grad = dot(slot_grad, matrices[2])
        gate_grad = (act_grad * up_pre * sigma * (1.0 + gate_pre * (1.0 - sigma))).astype(bf16)
        up_grad = (act_grad * silu).astype(bf16)
        hidden[0, 0, at, :] = gate_grad
        hidden[0, 1, at, :] = up_grad
        hidden[0, 2, at, :] = active
        token_grad[g, 0] = (
            dot_dims(gate_grad, matrices[0], 1, 1) + dot_dims(up_grad, matrices[1], 1, 1)
        ).astype(bf16)


def run_experts(offsets, first, ranks, gates, tokens, grads, weight_parts):
    groups = len(tokens)
    rows = tokens[0].shape[0]
    _, experts, part_rows, _ = weight_parts[0].shape
    parts = len(weight_parts)
    slots = groups * SLOTS
    by_group = pl.BlockSpec((groups, 1, SLOTS, D), lambda e, *_: (0, e, 0, 0))
    stash = pl.BlockSpec((1, slots, D), lambda e, *_: (e, 0, 0))
    return pl.pallas_call(
        functools.partial(expert_kernel, parts=parts, groups=groups),
        name="experts",
        grid_spec=pltpu.PrefetchScalarGridSpec(
            num_scalar_prefetch=2,
            grid=(experts,),
            in_specs=[whole(ranks.shape)]
            + [whole((EXPERTS, rows)) for _ in range(groups)]
            + [whole((rows, D)) for _ in range(2 * groups)]
            + [pl.BlockSpec((3, 1, part_rows, H), lambda e, *_: (0, e, 0, 0)) for _ in weight_parts],
            out_specs=[
                by_group,
                by_group,
                stash,
                stash,
                pl.BlockSpec((1, 3, slots, H), lambda e, *_: (e, 0, 0, 0)),
                whole(ranks.shape),
            ],
            scratch_shapes=[pltpu.VMEM((3, D, H), bf16)],
        ),
        out_shape=[
            jax.ShapeDtypeStruct((groups, experts, SLOTS, D), bf16),
            jax.ShapeDtypeStruct((groups, experts, SLOTS, D), bf16),
            jax.ShapeDtypeStruct((experts, slots, D), bf16),
            jax.ShapeDtypeStruct((experts, slots, D), bf16),
            jax.ShapeDtypeStruct((experts, 3, slots, H), bf16),
            jax.ShapeDtypeStruct(ranks.shape, f32),
        ],
        compiler_params=pltpu.CompilerParams(
            dimension_semantics=("arbitrary",), vmem_limit_bytes=VMEM_LIMIT
        ),
    )(
        offsets,
        first.reshape(1),
        ranks,
        *gates,
        *tokens,
        *grads,
        *weight_parts,
    )


def expert_grad_kernel(offsets, inputs, slot_grads, hidden, *rest):
    outs, total = rest[:-1], rest[-1]
    for m in range(3):
        left = inputs if m < 2 else slot_grads
        total[...] = dot_dims(left[0], hidden[0, m], 0, 0)
        for n, out in enumerate(outs):
            count = out.shape[2]
            out[m, 0] = total[pl.ds(pl.multiple_of(offsets[n], count), count), :].astype(bf16)


def expert_grads(offsets, inputs, slot_grads, hidden, parts, part_rows):
    experts, slots, _ = inputs.shape
    stash = pl.BlockSpec((1, slots, D), lambda e, *_: (e, 0, 0))
    return pl.pallas_call(
        expert_grad_kernel,
        name="expert_grads",
        grid_spec=pltpu.PrefetchScalarGridSpec(
            num_scalar_prefetch=1,
            grid=(experts,),
            in_specs=[stash, stash, pl.BlockSpec((1, 3, slots, H), lambda e, *_: (e, 0, 0, 0))],
            out_specs=[
                pl.BlockSpec((3, 1, part_rows, H), lambda e, *_: (0, e, 0, 0)) for _ in range(parts)
            ],
            scratch_shapes=[pltpu.VMEM((D, H), f32)],
        ),
        out_shape=[jax.ShapeDtypeStruct((3, experts, part_rows, H), bf16) for _ in range(parts)],
        compiler_params=pltpu.CompilerParams(
            dimension_semantics=("arbitrary",), vmem_limit_bytes=VMEM_LIMIT
        ),
    )(offsets, inputs, slot_grads, hidden)


def combine_kernel(ranks, rows_in, out, *, experts):
    count = out.shape[0]
    slot = lax.broadcasted_iota(i32, (count, SLOTS), 1)
    pick = jnp.concatenate(
        [(ranks[0, :, e : e + 1] == slot).astype(bf16) for e in range(experts)], axis=1
    )
    out[...] = dot(pick, rows_in[0]).astype(bf16)


def combine(ranks, slot_rows, g):
    groups, rows, columns = ranks.shape
    experts = slot_rows.shape[1]
    block = min(256, rows)
    return pl.pallas_call(
        functools.partial(combine_kernel, experts=experts),
        name="combine",
        grid=(rows // block,),
        in_specs=[
            pl.BlockSpec((1, block, columns), lambda i: (g, i, 0)),
            pl.BlockSpec(
                (1, experts * SLOTS, D), lambda i: (g, 0, 0), pipeline_mode=pl.Buffered(1)
            ),
        ],
        out_specs=pl.BlockSpec((block, D), lambda i: (i, 0)),
        out_shape=jax.ShapeDtypeStruct((rows, D), bf16),
        compiler_params=pltpu.CompilerParams(vmem_limit_bytes=VMEM_LIMIT),
    )(ranks, slot_rows.reshape(groups, experts * SLOTS, D))


def project_kernel(mixed, x, gain, matrix, middle, normed, inverse):
    branch = dot_dims(mixed[...].astype(f32).T.astype(bf16), matrix[:, :D], 1, 1)
    total = x[...].astype(f32) + branch_scale * branch
    scale = lax.rsqrt(jnp.mean(total * total, axis=1, keepdims=True) + epsilon)
    middle[...] = total
    inverse[...] = scale
    normed[...] = (total * scale * gain[...]).astype(bf16)


def project_out(mixed, x, gain, matrix):
    rows = x.shape[0]
    block = min(256, rows)
    tall = pl.BlockSpec((block, D), lambda i: (i, 0))
    return pl.pallas_call(
        project_kernel,
        name="project_out",
        grid=(rows // block,),
        in_specs=[
            pl.BlockSpec((D, block), lambda i: (0, i)),
            tall,
            whole(gain.shape),
            whole(matrix.shape),
        ],
        out_specs=[tall, tall, pl.BlockSpec((block, 1), lambda i: (i, 0))],
        out_shape=[
            jax.ShapeDtypeStruct((rows, D), f32),
            jax.ShapeDtypeStruct((rows, D), bf16),
            jax.ShapeDtypeStruct((rows, 1), f32),
        ],
        compiler_params=pltpu.CompilerParams(
            dimension_semantics=("arbitrary",), vmem_limit_bytes=VMEM_LIMIT
        ),
    )(mixed, x, gain, matrix)


def rotate(values, cosine, sine):
    first = values[..., : HD // 2, :]
    second = values[..., HD // 2 :, :]
    return jnp.concatenate([first * cosine - second * sine, second * cosine + first * sine], axis=-2)


def rotate_back(values, cosine, sine):
    first = values[..., : HD // 2, :]
    second = values[..., HD // 2 :, :]
    return jnp.concatenate([first * cosine + second * sine, second * cosine - first * sine], axis=-2)


def tree_tables(ancestry, own_all, token_starts, query_block, key_block):
    groups, rows, _ = ancestry.shape
    tokens = own_all.shape[0]
    segments = jnp.arange(SEGS, dtype=i32)
    index = jnp.arange(tokens, dtype=i32)
    member = own_all[None, :] == segments[:, None]
    begin = jnp.min(jnp.where(member, index[None, :], tokens), axis=1)
    length = jnp.sum(member.astype(i32), axis=1)
    on_path = jnp.any(ancestry[:, :, :, None] == segments, axis=2)
    at = token_starts[:, None] + jnp.arange(rows, dtype=i32)[None, :]
    before = jnp.clip(at[:, :, None] - begin, 0, length)
    position = jnp.sum(jnp.where(on_path, before, 0), axis=2)
    bits = jnp.sum(on_path.astype(i32) << segments, axis=2)
    blocked = on_path.reshape(groups * rows // query_block, query_block, SEGS)
    path_any = jnp.any(blocked, axis=1)
    path_all = jnp.all(blocked, axis=1)
    keys = jnp.any(member.reshape(SEGS, tokens // key_block, key_block), axis=2).T
    some = jnp.any(path_any[:, None, :] & keys[None, :, :], axis=2)
    every = jnp.all(path_all[:, None, :] | ~keys[None, :, :], axis=2)
    query_start = at.reshape(-1, query_block)[:, 0]
    key_start = jnp.arange(tokens // key_block, dtype=i32) * key_block
    some &= key_start[None, :] < query_start[:, None] + query_block
    every &= key_start[None, :] + key_block <= query_start[:, None] + 1
    codes = jnp.where(some, jnp.where(every, 2, 1), 0).astype(i32)
    return position, bits, query_start, codes.reshape(-1)


def body(
    layer_input,
    cotangent,
    gain_attention,
    gain_mixture,
    w_query,
    w_key,
    w_value,
    w_out,
    w_router,
    w_gate,
    w_up,
    w_down,
    routes,
    priority,
    ancestry,
):
    chips, share, columns = lax.axis_size("chip"), lax.axis_size("core"), lax.axis_size("col")
    chip, core, column = lax.axis_index("chip"), lax.axis_index("core"), lax.axis_index("col")
    row_axes = ("chip", "core")
    rows, width = layer_input.shape
    weight_rows = w_query.shape[0]
    query_heads = w_query.shape[1] // HD
    key_heads = w_key.shape[1] // HD
    group = query_heads // key_heads
    own_heads = key_heads // share
    experts = w_gate.shape[1] // share
    tokens_all = rows * chips * share
    query_block = min(QUERY_BLOCK, rows)
    key_block = min(KEY_BLOCK, tokens_all)
    token_block = rows // columns

    places = [(chip ^ j) * share + (core ^ h) for j in range(chips) for h in range(share)]
    token_offsets = jnp.stack([p * rows for p in places]).astype(i32)
    feature_offsets = jnp.stack([p * weight_rows for p in places]).astype(i32)

    def groups_of(values):
        return [values] + ([swap_core(values)] if share == 2 else [])

    x_full = lax.all_gather(layer_input, "col", axis=1, tiled=True)
    cotangent_full = lax.all_gather(cotangent, "col", axis=1, tiled=True)
    index_groups = groups_of(jnp.concatenate([routes, priority, ancestry], axis=1))
    index_arrays = jnp.stack(index_groups)
    all_routes = index_arrays[:, :, :TOPK]
    all_priority = index_arrays[:, :, TOPK : 2 * TOPK]
    all_ancestry = index_arrays[:, :, 2 * TOPK :]

    stacked = jnp.stack([m.transpose(1, 0, 2) for m in (w_gate, w_up, w_down)])
    stacked = stacked.reshape(3, share, experts, weight_rows, H).transpose(1, 0, 2, 3, 4)
    own_weights, other_weights = own_and_other(stacked, core, share)
    starts = [own_weights] + ([swap_core(other_weights)] if share == 2 else [])

    local_project = jnp.concatenate([w_query, w_key, w_value], axis=1)
    local_project, segments_here, starts[0] = tie(local_project, ancestry[:, 0], starts[0])
    own_all = lax.all_gather(segments_here, row_axes, axis=0, tiled=True)
    project = jnp.concatenate(
        [
            lax.all_gather(local_project[:, n : n + 256], row_axes, axis=0, tiled=True)
            for n in range(0, local_project.shape[1], 256)
        ],
        axis=1,
    )
    gain_rows = column_rows(jnp.concatenate([gain_attention, gain_mixture])[None, :])
    gains = gain_rows.reshape(columns, 2, width).transpose(1, 0, 2).reshape(2, D)
    out_columns = jnp.zeros((weight_rows, D), bf16)
    for c, part in [(column, w_out)] + column_shifts(lambda _: w_out):
        out_columns = lax.dynamic_update_slice_in_dim(out_columns, part, c * part.shape[1], 1)
    out_columns, project, own_all = tie(out_columns, project, own_all)
    out_router = lax.all_gather(
        jnp.concatenate([out_columns, w_router], axis=1), row_axes, axis=0, tiled=True
    )

    rounds = gather_rounds(chips, share)
    project, own_all, starts = tie(project, own_all, starts)
    weights_held = run_gather({(h, 0): v for h, v in enumerate(starts)}, rounds[:1])

    token_starts = jnp.stack([(chip * share + (core ^ g)) * rows for g in range(share)]).astype(i32)
    position, path_bits, query_starts, codes = tree_tables(
        all_ancestry, own_all, token_starts, query_block, key_block
    )
    frequency = rope_base ** (-(jnp.arange(HD // 2, dtype=f32) * 2.0) / HD)
    angle = position.astype(f32)[:, None, :] * frequency[None, :, None]
    by_rows = Layout(major_to_minor=(0, 1, 2))
    cosine = with_layout_constraint(jnp.cos(angle), by_rows)
    sine = with_layout_constraint(jnp.sin(angle), by_rows)
    first_expert = (column * (experts * share) + core * experts).astype(i32)
    ranks = slot_ranks(first_expert, all_routes, all_priority, experts)
    rank_columns = ranks.transpose(0, 2, 1)
    expert_ids = jnp.arange(EXPERTS, dtype=i32)
    chosen = jnp.any(all_routes[:, None, :, :] == expert_ids[None, :, None, None], axis=3)

    x_full, weights_held = tie(x_full, weights_held)
    x_wide = x_full.astype(f32)
    inverse_one = lax.rsqrt(jnp.mean(x_wide * x_wide, axis=1, keepdims=True) + epsilon)
    h_one = (x_wide * inverse_one * gains[0][None, :]).astype(bf16)
    key_bits = (jnp.int32(1) << own_all)[None, :]
    h_one, ranks, rank_columns, cosine, sine, path_bits, codes, chosen, key_bits = tie(
        h_one, ranks, rank_columns, cosine, sine, path_bits, codes, chosen, key_bits
    )
    projected = dot_dims(project, h_one, 0, 1)
    query_width, key_width = query_heads * HD, key_heads * HD
    query = rotate(
        projected[:query_width].reshape(share, own_heads, group, HD, rows), cosine[0], sine[0]
    )
    query = (query.astype(bf16).astype(f32) * score_scale).astype(bf16)
    keys = rotate(
        projected[query_width : query_width + key_width].reshape(share, own_heads, HD, rows),
        cosine[0],
        sine[0],
    ).astype(bf16)
    values = projected[query_width + key_width :].reshape(share, own_heads, HD, rows).astype(bf16)
    sent = jnp.concatenate([keys[:, :, None], values[:, :, None], query], axis=2)
    own_sent, other_sent = own_and_other(sent, core, share)
    received = [own_sent] + ([swap_core(other_sent)] if share == 2 else [])
    query_groups = jnp.stack([r[:, 2:] for r in received], axis=1)
    pairs = [r[:, :2].reshape(own_heads, 2 * HD, rows) for r in received]
    pairs, weights_held = tie(pairs, weights_held)
    kv_parts = gather_parts(pairs, chips)
    kv_parts, weights_held = tie(kv_parts, weights_held)
    weights_held = run_gather(weights_held, rounds[1 : len(rounds) - 1])

    attend_outs = [
        attend_forward(
            token_offsets,
            query_starts,
            codes,
            query_groups[head],
            path_bits,
            key_bits,
            [p[head] for p in kv_parts],
        )
        for head in range(own_heads)
    ]
    mixed_b = jnp.stack([o[1] for o in attend_outs])
    mixed_b, weights_held, cotangent_full, out_router = tie(
        mixed_b, weights_held, cotangent_full, out_router
    )
    weights_held = run_gather(weights_held, rounds[len(rounds) - 1 :])
    mixed_other = swap_core(mixed_b[:, 1]) if share == 2 else None
    mixed = in_core_order(mixed_b[:, 0], mixed_other, core).reshape(query_width, rows)
    mixed_full = lax.all_gather(mixed, "col", axis=0, tiled=True)
    mixed_full, weights_held = tie(mixed_full, weights_held)
    mix_grads = groups_of((branch_scale * cotangent_full.astype(f32)).astype(bf16))
    x_middle, h_two, inverse_two = project_out(
        mixed_full, x_full, gains[1:2], out_router
    )
    full_router = out_router[:, D:]
    h_two_groups = groups_of(h_two)

    def gates_of(tokens, picks):
        logits = dot_dims(full_router, tokens, 0, 1)
        shown = jnp.where(picks, logits, masked_score)
        raised = jnp.where(picks, jnp.exp(logits - jnp.max(shown, axis=0, keepdims=True)), 0.0)
        return raised / jnp.sum(raised, axis=0, keepdims=True)

    gates = [gates_of(h_two_groups[g], chosen[g]) for g in range(share)]
    weighted_out, slot_token_grads, inputs, slot_grads, hidden, pair_rows = run_experts(
        feature_offsets,
        first_expert,
        ranks,
        gates,
        h_two_groups,
        mix_grads,
        listed(weights_held, chips),
    )

    def combine_groups(slot_rows):
        if share == 1:
            return combine(rank_columns, slot_rows, 0)
        received = swap_core(combine(rank_columns, slot_rows, 1))
        own = combine(rank_columns, slot_rows, 0)
        return (own.astype(f32) + received.astype(f32)).astype(bf16)

    token_sum = combine_groups(slot_token_grads)
    token_grads = lax.psum_scatter(token_sum, "col", scatter_dimension=0, tiled=True)
    pair_other = swap_core(pair_rows[1, :experts]) if share == 2 else None
    pair_columns = in_core_order(pair_rows[0, :experts], pair_other, core)
    pair_columns = pair_columns.reshape(share * experts, rows)
    pair_grad = column_rows(pair_columns)
    picked_grad = gates[0] * (pair_grad - jnp.sum(gates[0] * pair_grad, axis=0, keepdims=True))
    logit_grad = picked_grad.astype(bf16)
    mix_sum = combine_groups(weighted_out)

    levels = reduce_levels(chips, share)
    first = [[m for m in moves if m[1]] for moves in levels[0]]
    last = [[m for m in moves if not m[1]] for moves in levels[0]]
    parts = expert_grads(feature_offsets, inputs, slot_grads, hidden, chips * share, weight_rows)
    sums_held = {(h, j): parts[j * share + h] for j in range(chips) for h in range(share)}
    first_taken = {}
    for moves in first:
        first_taken.update(take(sums_held, moves))
    staying = [sums_held.pop((h, 0)) for h in range(share)]
    token_grads, staying, mix_sum, logit_grad = tie(token_grads, staying, mix_sum, logit_grad)
    token_grads = token_grads.astype(f32)

    token_start = column * token_block

    def own_tokens(array):
        return lax.dynamic_slice_in_dim(array, token_start, token_block, 0)

    h_two_grad = token_grads + dot_dims(
        lax.dynamic_slice_in_dim(logit_grad, token_start, token_block, 1), full_router, 0, 1
    )
    x_part, inverse_part = own_tokens(x_middle), own_tokens(inverse_two)
    scaled_two = h_two_grad * gains[1][None, :]
    inner_two = jnp.sum(scaled_two * x_part, axis=1, keepdims=True)
    x_middle_grad = (
        own_tokens(cotangent_full).astype(f32)
        + inverse_part * scaled_two
        - x_part * inverse_part**3 * inner_two / D
    )
    gain_mixture_part = jnp.sum(h_two_grad * x_part * inverse_part, axis=0)
    branch_grad = lax.all_gather(
        (branch_scale * x_middle_grad).astype(bf16), "col", axis=0, tiled=True
    )
    sums_held = add_taken(sums_held, first_taken)
    branch_grad, mix_sum, sums_held = tie(branch_grad, mix_sum, sums_held)
    arrived = [[part] for part in staying]
    for rounds_here in levels[1:]:
        passed = {}
        for moves in rounds_here:
            passed.update(take(sums_held, moves))
        for h in range(share):
            if (h, 0) in passed:
                arrived[h].append(passed.pop((h, 0)))
        sums_held = add_taken(sums_held, passed)
    for moves in last:
        for (h, _), part in take(sums_held, moves).items():
            arrived[h].append(part)

    own_out = lax.dynamic_slice_in_dim(out_router, column * query_width, query_width, 1)
    mixed_grad = dot_dims(own_out, branch_grad, 0, 1).astype(bf16)
    own_grad, other_grad = own_and_other(
        mixed_grad.reshape(share, own_heads, group, HD, rows), core, share
    )
    grad_groups = jnp.stack(
        [own_grad] + ([swap_core(other_grad)] if share == 2 else []), axis=1
    )
    backward_outs = [
        attend_backward(
            token_offsets,
            query_starts,
            codes,
            query_groups[head],
            grad_groups[head],
            attend_outs[head][0],
            attend_outs[head][2],
            path_bits,
            key_bits,
            [p[head] for p in kv_parts],
        )
        for head in range(own_heads)
    ]
    mix_slice = lax.psum_scatter(mix_sum, "col", scatter_dimension=1, tiled=True).astype(f32)
    feature_start = column * width
    x_middle_slice = lax.dynamic_slice_in_dim(x_middle, feature_start, width, 1)
    result = (x_middle_slice + branch_scale * mix_slice).astype(bf16)
    backward_outs, arrived, branch_later = tie(backward_outs, arrived, branch_grad)
    query_grad = jnp.stack([o[0] for o in backward_outs])
    query_grad = rotate_back(query_grad, cosine[None, :, None], sine[None, :, None]).astype(bf16)
    query_other = swap_core(query_grad[:, 1]) if share == 2 else None
    query_pre_grad = in_core_order(query_grad[:, 0], query_other, core).reshape(query_width, rows)
    kv_sums = reduce_parts(
        [jnp.stack([o[1][n] for o in backward_outs]) for n in range(chips * share)], chips, share
    )
    kv_other = swap_core(kv_sums[1]) if share == 2 else None
    kv_grad = in_core_order(kv_sums[0], kv_other, core).astype(f32)
    kv_grad = kv_grad.transpose(0, 1, 3, 2).reshape(key_heads, 2 * HD, rows)
    key_pre_grad = (
        rotate_back(kv_grad[:, :HD], cosine[0], sine[0]).astype(bf16).reshape(key_width, rows)
    )
    value_pre_grad = kv_grad[:, HD:].astype(bf16).reshape(key_width, rows)
    project_grad = jnp.concatenate([query_pre_grad, key_pre_grad, value_pre_grad], axis=0)

    (project_grad,) = tie(project_grad)
    h_one_part = dot(project, project_grad).astype(bf16)
    h_one_part, project_grad = tie(h_one_part, project_grad)
    h_one_grad = lax.psum_scatter(h_one_part, "col", scatter_dimension=0, tiled=True)
    inner_one = column_sum(jnp.sum(project_grad.astype(f32) * projected, axis=0))[:, None]
    sums = [functools.reduce(jnp.add, [p.astype(f32) for p in own]).astype(bf16) for own in arrived]
    returned = swap_core(sums[1]) if share == 2 else None
    late = dot_dims(h_one, project_grad, 0, 1)
    early = [dot_dims(branch_later, mixed, 0, 1), dot_dims(h_two, logit_grad, 0, 1)]
    small_grads = jnp.concatenate([late] + early, axis=1).astype(bf16)
    gain_attention_part = jnp.sum(late * project.astype(f32), axis=1) / gains[0]
    gain_parts = jnp.stack([gain_attention_part, gain_mixture_part])

    def own_features(array, c):
        return lax.dynamic_slice_in_dim(array, c * width, width, 1)

    gain_sums = own_features(gain_parts, column)
    for _, other in column_shifts(lambda c: own_features(gain_parts, c)):
        gain_sums = gain_sums + other
    small_held = {
        (h, j): lax.dynamic_slice_in_dim(
            small_grads, places[j * share + h] * weight_rows, weight_rows, 0
        )
        for j in range(chips)
        for h in range(share)
    }
    for rounds_here in levels:
        taken = {}
        for moves in rounds_here:
            taken.update(take(small_held, moves))
        small_held = add_taken(small_held, taken)
    gain_sums = row_sum(gain_sums)
    small_sum = small_held[0, 0].astype(f32)
    if share == 2:
        small_sum = small_sum + swap_core(small_held[1, 0]).astype(f32)
    matrix_grads = [
        in_core_order(sums[0][m], None if returned is None else returned[m], core)
        .astype(f32)
        .reshape(share * experts, weight_rows, H)
        .transpose(1, 0, 2)
        for m in range(3)
    ]
    h_one_grad, matrix_grads, small_sum, gain_sums, inner_one = tie(
        h_one_grad, matrix_grads, small_sum, gain_sums, inner_one
    )
    x_slice = layer_input.astype(f32)
    middle_slice = lax.dynamic_slice_in_dim(branch_grad, feature_start, width, 1).astype(f32)
    input_grad = (
        middle_slice * (1.0 / branch_scale)
        + inverse_one * h_one_grad.astype(f32).T * gain_attention[None, :]
        - x_slice * inverse_one**2 * inner_one / D
    )
    kv_width = query_width + 2 * key_width
    return (
        result,
        input_grad,
        gain_sums[0],
        gain_sums[1],
        small_sum[:, :query_width],
        small_sum[:, query_width : query_width + key_width],
        small_sum[:, query_width + key_width : kv_width],
        small_sum[:, kv_width : kv_width + query_width],
        small_sum[:, kv_width + query_width :],
        *matrix_grads,
    )


def solution(mesh):
    rows, columns = mesh.shape["row"], mesh.shape["col"]
    halves = rows % 2 == 0 and EXPERTS // columns % 2 == 0 and KVH // columns % 2 == 0
    share = 2 if halves else 1
    split = Mesh(mesh.devices.reshape(rows // share, share, columns), ("chip", "core", "col"))
    row = ("chip", "core")
    return jax.shard_map(
        body,
        mesh=split,
        in_specs=(
            P(row, "col"),
            P(row, "col"),
            P("col"),
            P("col"),
            P(row, "col"),
            P(row, "col"),
            P(row, "col"),
            P(row, "col"),
            P(row, None),
            P(row, "col", None),
            P(row, "col", None),
            P(row, "col", None),
            P(row, None),
            P(row, None),
            P(row, None),
        ),
        out_specs=(
            P(row, "col"),
            P(row, "col"),
            P("col"),
            P("col"),
            P(row, "col"),
            P(row, "col"),
            P(row, "col"),
            P(row, "col"),
            P(row, None),
            P(row, "col", None),
            P(row, "col", None),
            P(row, "col", None),
        ),
        check_vma=False,
    )
```

time: 1100 us -> 825 us (0.75)
  starting transfers between devices: 171 us -> 63.3 us
  blocking collectives: 115 us -> 38.4 us
  local copies, waits for them, and re-layouts: 89.5 us -> 39.9 us
  other arithmetic: 111 us -> 82.6 us
    ppermute x37 -> x44, starting transfers between devices: 169 us -> 32.6 us  [swap(): return lax.ppermute(values, axis, [(i, i ^ bit) for i in range(size)])]
    ppermute x37 -> x44, waiting for transfers between devices: 248 us -> 343 us  [swap(): return lax.ppermute(values, axis, [(i, i ^ bit) for i in range(size)])]
    all_gather x1, waiting for transfers between devices: 49.2 us -> 0.01 us  [body(): mixed_full = lax.all_gather(mixed, 'col', axis=0, tiled=True)]
    psum x2 -> x0, blocking collectives: 48.3 us -> none  [the longest x1 38.9 us: body(): lax.psum(gain_parts, ('chip', 'core', 'col'))]
    ppermute x0 -> x22, starting transfers between devices: none -> 29.4 us  [the longest x15 23.3 us: column_shifts(): lax.ppermute(values_for((me + d) % size), 'col', [(i, (i + d) % size) for...]
    all_gather x4, blocking collectives: 66.2 us -> 38.4 us  [the longest x3 29.4 us: body(): lax.all_gather(local_project[:, n:n + 256], row_axes, axis=0, tiled=True)]
    all_gather x1 -> x0, waiting for transfers between devices: 25.7 us -> none  [body(): lax.all_gather(jnp.concatenate([w_query, w_key, w_value], axis=1), row_ax...]
    reduce_scatter x1, waiting for transfers between devices: 32.3 us -> 7.25 us  [body(): lax.psum_scatter(token_sum, 'col', scatter_dimension=0, tiled=True)]
  transfers between devices with their start and end apart: 48 -> 74, of which waited for: 21 -> 31; matrix products, arithmetic and copies ran while one was open for 19% -> 16% of each run, Pallas kernels for 12% -> 13%
where the time goes in v2:
time: 825 us; the launch traced here: 819 us
  waiting for transfers between devices  364 us (44%)
  Pallas kernels  184 us (22%)
  other arithmetic  82.6 us (10%)
  starting transfers between devices  63.3 us (8%)
  local copies, waits for them, and re-layouts  39.9 us (5%)
  blocking collectives  38.4 us (5%)
  matrix products  30.1 us (4%)
  between operations  15.8 us (2%)
    ppermute x44, waiting for transfers between devices, swap(): return lax.ppermute(values, axis, [(i, i ^ bit) for i in range(size)])  343 us
    pallas_call x1, Pallas kernels, run_experts(): pl.pallas_call(functools.partial(expert_kernel, parts=parts, groups=group...  57 us
    ppermute x44, starting transfers between devices, swap(): return lax.ppermute(values, axis, [(i, i ^ bit) for i in range(size)])  32.6 us
    pallas_call x4, Pallas kernels, combine(): pl.pallas_call(functools.partial(combine_kernel, experts=experts), name='...  32.4 us
    pallas_call x1, Pallas kernels, attend_backward(): pl.pallas_call(kernel, name='attend_backward', grid_spec=pltpu.PrefetchSc...  30.6 us
    all_gather x3, blocking collectives, body(): lax.all_gather(local_project[:, n:n + 256], row_axes, axis=0, tiled=True)  29.4 us
    dot_general x8, matrix products, dot_dims(): lax.dot_general(left, right, (((left_dim,), (right_dim,)), ((), ())), pre...  24.4 us
    ppermute x15, starting transfers between devices, column_shifts(): lax.ppermute(values_for((me + d) % size), 'col', [(i, (i + d) % size) for...  23.3 us
  transfers between devices with their start and end apart: 74, of which 31 were waited for; matrix products, arithmetic and copies ran while one was open for 16% of the time, Pallas kernels for 13%

profile of v2, /device:TPU:0, one launch (start us, length us, event | category | flops | bytes accessed | tf_op | source)
XLA Modules:
  0.0 818.8 jit_solution(11112364265779659988)
XLA Ops:
  23.3 9.6 %all_gather.30 = bf16[1536,128]{1,0:T(8,128)(2,1)S(1)} all-gather(bf16[192,128]{1,0:T(8,128)(2,1)S(1)} %slice.169), channel_id=1, replica_groups=mesh['chip'=4,'core'=2,'col'=4] {'chip','core'}, dimensions={0}, use_global_device_ids=true | all-gather | bytes 442368 | tf_op jit(solution)/shard_map/all_gather | solution.py:797
  33.8 10.4 %all_gather.29 = bf16[1536,256]{1,0:T(8,128)(2,1)S(1)} all-gather(bf16[192,256]{1,0:T(8,128)(2,1)S(1)} %get-tuple-element.406), channel_id=1, replica_groups=mesh['chip'=4,'core'=2,'col'=4] {'chip','core'}, dimensions={0}, use_global_device_ids=true | all-gather | bytes 884736 | tf_op jit(solution)/shard_map/all_gather | solution.py:797
  44.5 9.4 %all_gather.28 = bf16[1536,256]{1,0:T(8,128)(2,1)S(1)} all-gather(bf16[192,256]{1,0:T(8,128)(2,1)S(1)} %get-tuple-element.405), channel_id=1, replica_groups=mesh['chip'=4,'core'=2,'col'=4] {'chip','core'}, dimensions={0}, use_global_device_ids=true | all-gather | bytes 884736 | tf_op jit(solution)/shard_map/all_gather | solution.py:797
  57.8 9.0 %all_gather.31 = s32[8192]{0:T(1024)S(1)} all-gather(s32[1024]{0:T(1024)S(1)} %bitcast.281), channel_id=1, replica_groups=mesh['chip'=4,'core'=2,'col'=4] {'chip','core'}, dimensions={0}, use_global_device_ids=true | all-gather | bytes 36864 | tf_op jit(solution)/shard_map/all_gather | solution.py:794
  80.4 8.5 %slot_ranks.1.ranks = s32[2,8,1024]{2,1,0:T(8,128)} custom-call(s32[1]{0:T(128)} %bitcast.22.first, s32[2,8,1024]{2,1,0:T(8,128)} %copy.240.route_rows, s32[2,8,1024]{2,1,0:T(8,128)} %copy.241.priority_rows, s32[2,1024,8]{2,1,0:T(8,128)} %copy-done.1, s32[2,1024,8]{2,1,0:T(8,128)} %copy-done.6), custom_call_target="tpu_custom_call" | custom-call | tf_op jit(solution)/shard_map/slot_ranks/pallas_call | solution.py:491
  99.7 37.6 %collective-permute-done.4.rest_8_ = bf16[3,5,192,512]{3,2,1,0:T(8,128)(2,1)} collective-permute-done((bf16[3,5,192,512]{3,2,1,0:T(8,128)(2,1)}, bf16[3,5,192,512]{3,2,1,0:T(8,128)(2,1)}, u32[]{:S(2)}, u32[]{:S(2)}) %collective-permute-start.4) | collective-permute-done | bytes 2949152 | tf_op jit(solution)/shard_map/ppermute | solution.py:49
  168.7 8.0 collective-permute-done.15
  183.2 21.0 %attend_forward.1 = (f32[2,3,64,1024]{3,2,1,0:T(8,128)}, bf16[2,3,64,1024]{3,2,1,0:T(8,128)(2,1)}, f32[2,3,1,1024]{3,2,1,0:T(1,128)}) custom-call(s32[8]{0:T(128)} %stack.184.offsets, s32[4]{0:T(128)} %get-tuple-element.361.starts, s32[64]{0:T(128)} %select_n.264.codes, bf16[2,3,64,1024]{3,2,1,0:T(8,128)(2,1)} %maximum_bitcast_fusion.query, ...), custom_call_target="tpu_custom_call" | custom-call | tf_op jit(solution)/shard_map/attend_forward/pallas_call | solution.py:369
  204.2 7.3 all-gather.10.cloned.1.call-done.matrix
  211.5 43.9 %collective-permute-done.17.rest_10_ = bf16[3,5,192,512]{3,2,1,0:T(8,128)(2,1)S(1)} collective-permute-done((bf16[3,5,192,512]{3,2,1,0:T(8,128)(2,1)}, bf16[3,5,192,512]{3,2,1,0:T(8,128)(2,1)S(1)}, u32[]{:S(2)}, u32[]{:S(2)}) %collective-permute-start.17) | collective-permute-done | bytes 2949152 | tf_op jit(solution)/shard_map/ppermute | solution.py:49
  264.5 63.6 %collective-permute-done.20.rest_12_ = bf16[3,5,192,512]{3,2,1,0:T(8,128)(2,1)} collective-permute-done((bf16[3,5,192,512]{3,2,1,0:T(8,128)(2,1)}, bf16[3,5,192,512]{3,2,1,0:T(8,128)(2,1)}, u32[]{:S(2)}, u32[]{:S(2)}) %collective-permute-start.20) | collective-permute-done | bytes 2949152 | tf_op jit(solution)/shard_map/ppermute | solution.py:49
  328.7 11.4 %project_out.1 = (f32[1024,1536]{1,0:T(8,128)}, bf16[1024,1536]{1,0:T(8,128)(2,1)}, f32[1024,1]{1,0:T(8,128)}) custom-call(bf16[1536,1024]{1,0:T(8,128)(2,1)} %all-gather.12.cloned.1.call-done.mixed, bf16[1024,1536]{1,0:T(8,128)(2,1)} %all-gather.6.cloned.1.call-done.x, f32[1,1536]{1,0:T(1,128)} %bitcast.282, ...), custom_call_target="tpu_custom_call" | custom-call | tf_op jit(solution)/shard_map/project_out/pallas_call | solution.py:679
  351.6 57.0 %experts.1 = (bf16[2,5,256,1536]{3,2,1,0:T(8,128)(2,1)}, bf16[2,5,256,1536]{3,2,1,0:T(8,128)(2,1)}, bf16[5,512,1536]{2,1,0:T(8,128)(2,1)}, bf16[5,512,1536]{2,1,...) custom-call(s32[8]{0:T(128)} %stack.208.offsets, s32[1]{0:T(128)} %bitcast.22.first, ...), custom_call_target="tpu_custom_call" | custom-call | tf_op jit(solution)/shard_map/experts/pallas_call | solution.py:563
  408.7 8.3 %combine.5 = bf16[1024,1536]{1,0:T(8,128)(2,1)} custom-call(s32[2,1024,8]{2,1,0:T(8,128)} %bitcast.231, bf16[2,1280,1536]{2,1,0:T(8,128)(2,1)} %bitcast.229), custom_call_target="tpu_custom_call" | custom-call | tf_op jit(solution)/shard_map/combine/pallas_call | solution.py:650
  417.1 8.0 combine.4
  429.5 8.1 combine.7
  447.5 8.0 combine.6
  455.5 23.2 %expert_grads.1 = (bf16[3,5,192,512]{3,2,1,0:T(8,128)(2,1)}, bf16[3,5,192,512]{3,2,1,0:T(8,128)(2,1)}, bf16[3,5,192,512]{3,2,1,0:T(8,128)(2,1)}, bf16[3,5,192,51...) custom-call(s32[8]{0:T(128)} %stack.208.offsets, ...), custom_call_target="tpu_custom_call" | custom-call | tf_op jit(solution)/shard_map/expert_grads/pallas_call | solution.py:618
  484.5 7.2 reduce-scatter.8.cloned.1.call-done
  501.1 62.7 %collective-permute-done.30 = bf16[3,5,192,512]{3,2,1,0:T(8,128)(2,1)S(1)} collective-permute-done((bf16[3,5,192,512]{3,2,1,0:T(8,128)(2,1)}, bf16[3,5,192,512]{3,2,1,0:T(8,128)(2,1)S(1)}, u32[]{:S(2)}, u32[]{:S(2)}) %collective-permute-start.30) | collective-permute-done | bytes 2949152 | tf_op jit(solution)/shard_map/ppermute | solution.py:49
  589.3 30.6 %attend_backward.1 = (f32[2,3,64,1024]{3,2,1,0:T(8,128)}, bf16[1024,128]{1,0:T(8,128)(2,1)}, bf16[1024,128]{1,0:T(8,128)(2,1)}, bf16[1024,128]{1,0:T(8,128)(2,1)...) custom-call(s32[8]{0:T(128)} %stack.184.offsets, ...), custom_call_target="tpu_custom_call" | custom-call | tf_op jit(solution)/shard_map/attend_backward/pallas_call | solution.py:418
  619.9 18.1 %collective-permute-done.33 = bf16[3,5,192,512]{3,2,1,0:T(8,128)(2,1)} collective-permute-done((bf16[3,5,192,512]{3,2,1,0:T(8,128)(2,1)}, bf16[3,5,192,512]{3,2,1,0:T(8,128)(2,1)}, u32[]{:S(2)}, u32[]{:S(2)}) %collective-permute-start.33) | collective-permute-done | bytes 2949152 | tf_op jit(solution)/shard_map/ppermute | solution.py:49
  639.5 60.7 %collective-permute-done.35 = bf16[3,5,192,512]{3,2,1,0:T(8,128)(2,1)} collective-permute-done((bf16[3,5,192,512]{3,2,1,0:T(8,128)(2,1)}, bf16[3,5,192,512]{3,2,1,0:T(8,128)(2,1)}, u32[]{:S(2)}, u32[]{:S(2)}) %collective-permute-start.35) | collective-permute-done | bytes 2949152 | tf_op jit(solution)/shard_map/ppermute | solution.py:49
  778.6 7.5 collective-permute-done.46
  (431 shorter events, 263.7 us)
Async XLA Ops:
  7.2 92.5 %all-gather.6.cloned.1.call-start = ((), (), s32[]{:S(2)}) async-start(), calls=%async_computation.3 | async-start | bytes 3932160 | tf_op jit(solution)/shard_map/all_gather | solution.py:779
  7.9 196.3 %all-gather.8.cloned.1.call-start = ((), (), s32[]{:S(2)}) async-start(), calls=%async_computation.4 | async-start | bytes 3932160 | tf_op jit(solution)/shard_map/all_gather | solution.py:780
  8.7 202.8 %all-gather.10.cloned.1.call-start = ((), (), s32[]{:S(2)}) async-start(), calls=%async_computation.5 | async-start | bytes 5750784 | tf_op jit(solution)/shard_map/all_gather | solution.py:808
  15.5 55.6 %collective-permute-start.3 = (bf16[3,5,192,512]{3,2,1,0:T(8,128)(2,1)}, bf16[3,5,192,512]{3,2,1,0:T(8,128)(2,1)}, u32[]{:S(2)}, u32[]{:S(2)}) collective-permute-start(bf16[3,5,192,512]{3,2,1,0:T(8,128)(2,1)} %get-tuple-element.371), channel_id=1, source_target_pairs={{0,4},{4,0},{1,5},{5,1},{2,6},{6,2},{3,7},{7,3},{8,12},{12,8},{9,1... | collective-permute-start | bytes 8847368 | tf_op jit(solution)/shard_map/ppermute | solution.py:49
  16.0 50.9 %collective-permute-start = (bf16[192,384]{1,0:T(8,128)(2,1)S(1)}, bf16[192,384]{1,0:T(8,128)(2,1)}, u32[]{:S(2)}, u32[]{:S(2)}) collective-permute-start(bf16[192,384]{1,0:T(8,128)(2,1)S(1)} %copy-done.43), channel_id=1, source_target_pairs={{0,1},{1,2},{2,3},{3,0},{4,5},{5,6},{6,7},{7,4},{8,9},{9,10},{10,1... | collective-permute-start | bytes 442376 | tf_op jit(solution)/shard_map/ppermute | solution.py:136
  22.5 51.2 %collective-permute-start.6 = (f32[1,768]{1,0:T(1,128)S(1)}, f32[1,768]{1,0:T(1,128)S(1)}, u32[]{:S(2)}, u32[]{:S(2)}) collective-permute-start(f32[1,768]{1,0:T(1,128)S(1)} %broadcast_in_dim.51), channel_id=1, source_target_pairs={{0,1},{1,2},{2,3},{3,0},{4,5},{5,6},{6,7},{7,4},{8,9},{9,10},{10,1... | collective-permute-start | bytes 9224 | tf_op jit(solution)/shard_map/ppermute | solution.py:136
  71.1 66.2 %collective-permute-start.4 = (bf16[3,5,192,512]{3,2,1,0:T(8,128)(2,1)}, bf16[3,5,192,512]{3,2,1,0:T(8,128)(2,1)}, u32[]{:S(2)}, u32[]{:S(2)}) collective-permute-start(bf16[3,5,192,512]{3,2,1,0:T(8,128)(2,1)} %get-tuple-element.193.rest_6_), channel_id=1, source_target_pairs={{0,8},{8,0},{16,24},{24,16},{1,9},{9,1},{17,25},{25,17},{2,10},{10... | collective-permute-start | bytes 8847368 | tf_op jit(solution)/shard_map/ppermute | solution.py:49
  71.7 65.9 %collective-permute-start.5 = (bf16[3,5,192,512]{3,2,1,0:T(8,128)(2,1)}, bf16[3,5,192,512]{3,2,1,0:T(8,128)(2,1)}, u32[]{:S(2)}, u32[]{:S(2)}) collective-permute-start(bf16[3,5,192,512]{3,2,1,0:T(8,128)(2,1)} %collective-permute-done.3.rest_7_), channel_id=1, source_target_pairs={{0,16},{8,24},{16,0},{24,8},{1,17},{9,25},{17,1},{25,9},{2,18},{10... | collective-permute-start | bytes 8847368 | tf_op jit(solution)/shard_map/ppermute | solution.py:49
  96.0 232.7 %all-gather.12.cloned.1.call-start = ((), (), s32[]{:S(2)}) async-start(), calls=%async_computation.6 | async-start | bytes 3932160 | tf_op jit(solution)/shard_map/all_gather | solution.py:880
  176.7 78.7 %collective-permute-start.17 = (bf16[3,5,192,512]{3,2,1,0:T(8,128)(2,1)}, bf16[3,5,192,512]{3,2,1,0:T(8,128)(2,1)S(1)}, u32[]{:S(2)}, u32[]{:S(2)}) collective-permute-start(bf16[3,5,192,512]{3,2,1,0:T(8,128)(2,1)} %get-tuple-element.193.rest_6_), channel_id=1, source_target_pairs={{0,16},{8,24},{16,0},{24,8},{1,17},{9,25},{17,1},{25,9},{2,18},{10... | collective-permute-start | bytes 8847368 | tf_op jit(solution)/shard_map/ppermute | solution.py:49
  177.5 78.7 %collective-permute-start.18 = (bf16[3,5,192,512]{3,2,1,0:T(8,128)(2,1)}, bf16[3,5,192,512]{3,2,1,0:T(8,128)(2,1)}, u32[]{:S(2)}, u32[]{:S(2)}) collective-permute-start(bf16[3,5,192,512]{3,2,1,0:T(8,128)(2,1)} %collective-permute-done.3.rest_7_), channel_id=1, source_target_pairs={{0,8},{8,0},{16,24},{24,16},{1,9},{9,1},{17,25},{25,17},{2,10},{10... | collective-permute-start | bytes 8847368 | tf_op jit(solution)/shard_map/ppermute | solution.py:49
  261.5 230.2 %reduce-scatter.8.cloned.1.call-start = ((), (), s32[]{:S(2)}) async-start(), calls=%async_computation.7 | async-start | bytes 3932160 | tf_op jit(solution)/shard_map/reduce_scatter | solution.py:914
  261.8 66.3 %collective-permute-start.20 = (bf16[3,5,192,512]{3,2,1,0:T(8,128)(2,1)}, bf16[3,5,192,512]{3,2,1,0:T(8,128)(2,1)}, u32[]{:S(2)}, u32[]{:S(2)}) collective-permute-start(bf16[3,5,192,512]{3,2,1,0:T(8,128)(2,1)} %collective-permute-done.4.rest_8_), channel_id=1, source_target_pairs={{0,16},{8,24},{16,0},{24,8},{1,17},{9,25},{17,1},{25,9},{2,18},{10... | collective-permute-start | bytes 8847368 | tf_op jit(solution)/shard_map/ppermute | solution.py:49
  262.8 66.0 %collective-permute-start.21 = (bf16[3,5,192,512]{3,2,1,0:T(8,128)(2,1)}, bf16[3,5,192,512]{3,2,1,0:T(8,128)(2,1)}, u32[]{:S(2)}, u32[]{:S(2)}) collective-permute-start(bf16[3,5,192,512]{3,2,1,0:T(8,128)(2,1)} %collective-permute-done.5.rest_11_), channel_id=1, source_target_pairs={{0,8},{8,0},{16,24},{24,16},{1,9},{9,1},{17,25},{25,17},{2,10},{10... | collective-permute-start | bytes 8847368 | tf_op jit(solution)/shard_map/ppermute | solution.py:49
  429.5 141.4 %all-gather.14.cloned.1.call-start = ((), (), s32[]{:S(2)}) async-start(), calls=%async_computation.8 | async-start | bytes 3932160 | tf_op jit(solution)/shard_map/all_gather | solution.py:952
  497.6 302.8 %reduce-scatter.10.cloned.1.call-start = ((), (), s32[]{:S(2)}) async-start(), calls=%async_computation.9 | async-start | bytes 3932160
  498.1 65.7 %collective-permute-start.30 = (bf16[3,5,192,512]{3,2,1,0:T(8,128)(2,1)}, bf16[3,5,192,512]{3,2,1,0:T(8,128)(2,1)S(1)}, u32[]{:S(2)}, u32[]{:S(2)}) collective-permute-start(bf16[3,5,192,512]{3,2,1,0:T(8,128)(2,1)} %get-tuple-element.214), channel_id=1, source_target_pairs={{0,8},{8,0},{16,24},{24,16},{1,9},{9,1},{17,25},{25,17},{2,10},{10... | collective-permute-start | bytes 8847368 | tf_op jit(solution)/shard_map/ppermute | solution.py:49
  499.6 68.7 %collective-permute-start.31 = (bf16[3,5,192,512]{3,2,1,0:T(8,128)(2,1)}, bf16[3,5,192,512]{3,2,1,0:T(8,128)(2,1)S(1)}, u32[]{:S(2)}, u32[]{:S(2)}) collective-permute-start(bf16[3,5,192,512]{3,2,1,0:T(8,128)(2,1)} %get-tuple-element.216), channel_id=1, source_target_pairs={{0,16},{8,24},{16,0},{24,8},{1,17},{9,25},{17,1},{25,9},{2,18},{10... | collective-permute-start | bytes 8847368 | tf_op jit(solution)/shard_map/ppermute | solution.py:49
  570.9 67.1 %collective-permute-start.33 = (bf16[3,5,192,512]{3,2,1,0:T(8,128)(2,1)}, bf16[3,5,192,512]{3,2,1,0:T(8,128)(2,1)}, u32[]{:S(2)}, u32[]{:S(2)}) collective-permute-start(bf16[3,5,192,512]{3,2,1,0:T(8,128)(2,1)} %add_convert_fusion.5), channel_id=1, source_target_pairs={{0,16},{8,24},{16,0},{24,8},{1,17},{9,25},{17,1},{25,9},{2,18},{10... | collective-permute-start | bytes 8847368 | tf_op jit(solution)/shard_map/ppermute | solution.py:49
  572.4 67.1 %collective-permute-start.34 = (bf16[3,5,192,512]{3,2,1,0:T(8,128)(2,1)}, bf16[3,5,192,512]{3,2,1,0:T(8,128)(2,1)}, u32[]{:S(2)}, u32[]{:S(2)}) collective-permute-start(bf16[3,5,192,512]{3,2,1,0:T(8,128)(2,1)} %get-tuple-element.233), channel_id=1, source_target_pairs={{0,8},{8,0},{16,24},{24,16},{1,9},{9,1},{17,25},{25,17},{2,10},{10... | collective-permute-start | bytes 8847368 | tf_op jit(solution)/shard_map/ppermute | solution.py:49
  573.8 126.3 %collective-permute-start.35 = (bf16[3,5,192,512]{3,2,1,0:T(8,128)(2,1)}, bf16[3,5,192,512]{3,2,1,0:T(8,128)(2,1)}, u32[]{:S(2)}, u32[]{:S(2)}) collective-permute-start(bf16[3,5,192,512]{3,2,1,0:T(8,128)(2,1)} %add_convert_fusion.4), channel_id=1, source_target_pairs={{0,8},{8,0},{16,24},{24,16},{1,9},{9,1},{17,25},{25,17},{2,10},{10... | collective-permute-start | bytes 8847368 | tf_op jit(solution)/shard_map/ppermute | solution.py:49
  574.4 125.8 %collective-permute-start.36 = (bf16[3,5,192,512]{3,2,1,0:T(8,128)(2,1)}, bf16[3,5,192,512]{3,2,1,0:T(8,128)(2,1)}, u32[]{:S(2)}, u32[]{:S(2)}) collective-permute-start(bf16[3,5,192,512]{3,2,1,0:T(8,128)(2,1)} %get-tuple-element.236), channel_id=1, source_target_pairs={{0,16},{8,24},{16,0},{24,8},{1,17},{9,25},{17,1},{25,9},{2,18},{10... | collective-permute-start | bytes 8847368 | tf_op jit(solution)/shard_map/ppermute | solution.py:49
  577.9 226.6 %reduce-scatter.12.cloned.1.call-start = ((), (), s32[]{:S(2)}) async-start(), calls=%async_computation.10 | async-start | bytes 3932160
  716.4 73.4 %collective-permute-start.45 = (bf16[3,5,192,512]{3,2,1,0:T(8,128)(2,1)}, bf16[3,5,192,512]{3,2,1,0:T(8,128)(2,1)}, u32[]{:S(2)}, u32[]{:S(2)}) collective-permute-start(bf16[3,5,192,512]{3,2,1,0:T(8,128)(2,1)} %add_convert_fusion.2), channel_id=1, source_target_pairs={{0,4},{4,0},{1,5},{5,1},{2,6},{6,2},{3,7},{7,3},{8,12},{12,8},{9,1... | collective-permute-start | bytes 8847368 | tf_op jit(solution)/shard_map/ppermute | solution.py:49
  (109 other events, 1708.7 us)
Sparse Core Ops, SparseCore 0:
  9.6 76.3 all-gather.5
  87.6 62.6 all-gather.7
  152.7 58.7 all-gather.9
  261.7 61.1 all-gather.11
  429.6 62.1 reduce-scatter.7
  497.7 63.6 all-gather.13
  578.0 60.6 reduce-scatter.9
  745.1 58.0 reduce-scatter.11

commit v3 on v2

--- a/solution.py
+++ b/solution.py
@@ -127,6 +127,69 @@
     return [held[h, 0] for h in range(share)]
 
 
+def pick(core, values):
+    return jnp.where(core == 0, values[0], values[-1])
+
+
+def shared_places(chips, share, core):
+    chip = lax.axis_index("chip")
+    places = []
+    for p in range(chips):
+        jumps = [
+            sum(b for t, b in enumerate(half_bits(chips, k)) if p >> t & 1) for k in range(share)
+        ]
+        places.append((chip ^ pick(core, jumps)) * share + core)
+    return places
+
+
+def shared_swap(values, level):
+    chips, share = lax.axis_size("chip"), lax.axis_size("core")
+    pairs = [
+        (c * share + k, (c ^ half_bits(chips, k)[level]) * share + k)
+        for c in range(chips)
+        for k in range(share)
+    ]
+    return lax.ppermute(values, ("chip", "core"), pairs)
+
+
+def shared_level(blocks, level):
+    return blocks + [shared_swap(b, level) for b in blocks]
+
+
+def shared_rows(blocks):
+    chips, share, core = lax.axis_size("chip"), lax.axis_size("core"), lax.axis_index("core")
+    places = shared_places(chips, share, core)
+    parts = list(blocks)
+    if share == 2:
+        parts += [swap_core(b) for b in blocks]
+        places = places + shared_places(chips, share, 1 - core)
+    rows = blocks[0].shape[0]
+    return place_rows(jnp.stack([p * rows for p in places]).astype(i32), parts)
+
+
+def shared_reduce(values, rows):
+    chips, share, core = lax.axis_size("chip"), lax.axis_size("core"), lax.axis_index("core")
+
+    def blocks_of(k):
+        return jnp.stack(
+            [
+                lax.dynamic_slice_in_dim(values, p * rows, rows, 0)
+                for p in shared_places(chips, share, k)
+            ]
+        )
+
+    def add(left, right):
+        return (left.astype(f32) + right.astype(f32)).astype(left.dtype)
+
+    held = blocks_of(core)
+    if share == 2:
+        held = add(held, swap_core(blocks_of(1 - core)))
+    for level in reversed(range(len(chip_bits(chips)))):
+        half = 1 << level
+        held = add(held[:half], shared_swap(held[half:], level))
+    return held[0].astype(f32)
+
+
 def column_shifts(values_for):
     size = lax.axis_size("col")
     me = lax.axis_index("col")
@@ -155,12 +218,10 @@
 
 
 def row_sum(values):
-    chips, share = lax.axis_size("chip"), lax.axis_size("core")
-    size = chips * share
-    total = values
-    for n in range(1, size):
-        total = total + lax.ppermute(values, ("chip", "core"), [(i, i ^ n) for i in range(size)])
-    return total
+    for axis in ("core", "chip"):
+        for bit in chip_bits(lax.axis_size(axis)):
+            values = values + swap(values, axis, bit)
+    return values
 
 
 def tie(*trees):
@@ -461,6 +522,29 @@
         *kv_parts,
     )
     return outs[0], outs[1:]
+
+
+def place_kernel(offsets, *rest):
+    parts, out = rest[:-1], rest[-1]
+    for n, part in enumerate(parts):
+        rows = part.shape[0]
+        out[pl.ds(pl.multiple_of(offsets[n], rows), rows), :] = part[...]
+
+
+def place_rows(offsets, parts):
+    rows, width = parts[0].shape
+    return pl.pallas_call(
+        place_kernel,
+        name="place_rows",
+        grid_spec=pltpu.PrefetchScalarGridSpec(
+            num_scalar_prefetch=1,
+            grid=(1,),
+            in_specs=[whole(p.shape) for p in parts],
+            out_specs=whole((rows * len(parts), width)),
+        ),
+        out_shape=jax.ShapeDtypeStruct((rows * len(parts), width), parts[0].dtype),
+        compiler_params=pltpu.CompilerParams(vmem_limit_bytes=VMEM_LIMIT),
+    )(offsets, *parts)
 
 
 def rank_kernel(first, route_rows, priority_rows, route_columns, priority_columns, out, *, experts):
@@ -602,36 +686,48 @@
     )
 
 
-def expert_grad_kernel(offsets, inputs, slot_grads, hidden, *rest):
+def expert_grad_kernel(offsets, inputs, slot_grads, hidden, *rest, pieces):
     outs, total = rest[:-1], rest[-1]
     for m in range(3):
         left = inputs if m < 2 else slot_grads
         total[...] = dot_dims(left[0], hidden[0, m], 0, 0)
-        for n, out in enumerate(outs):
-            count = out.shape[2]
-            out[m, 0] = total[pl.ds(pl.multiple_of(offsets[n], count), count), :].astype(bf16)
-
-
-def expert_grads(offsets, inputs, slot_grads, hidden, parts, part_rows):
+        for (n, begin), out in zip(pieces, outs):
+            if begin <= m < begin + out.shape[0]:
+                count = out.shape[2]
+                at = pl.ds(pl.multiple_of(offsets[n], count), count)
+                out[m - begin, 0] = total[at, :].astype(bf16)
+
+
+def expert_grads(offsets, inputs, slot_grads, hidden, parts, cut_parts, part_rows):
     experts, slots, _ = inputs.shape
     stash = pl.BlockSpec((1, slots, D), lambda e, *_: (e, 0, 0))
-    return pl.pallas_call(
-        expert_grad_kernel,
+    pieces = []
+    for n in range(parts):
+        pieces += [(n, 0, 1), (n, 1, 2)] if n in cut_parts else [(n, 0, 3)]
+    outs = pl.pallas_call(
+        functools.partial(expert_grad_kernel, pieces=[(n, begin) for n, begin, _ in pieces]),
         name="expert_grads",
         grid_spec=pltpu.PrefetchScalarGridSpec(
             num_scalar_prefetch=1,
             grid=(experts,),
             in_specs=[stash, stash, pl.BlockSpec((1, 3, slots, H), lambda e, *_: (e, 0, 0, 0))],
             out_specs=[
-                pl.BlockSpec((3, 1, part_rows, H), lambda e, *_: (0, e, 0, 0)) for _ in range(parts)
+                pl.BlockSpec((held, 1, part_rows, H), lambda e, *_: (0, e, 0, 0))
+                for _, _, held in pieces
             ],
             scratch_shapes=[pltpu.VMEM((D, H), f32)],
         ),
-        out_shape=[jax.ShapeDtypeStruct((3, experts, part_rows, H), bf16) for _ in range(parts)],
+        out_shape=[
+            jax.ShapeDtypeStruct((held, experts, part_rows, H), bf16) for _, _, held in pieces
+        ],
         compiler_params=pltpu.CompilerParams(
             dimension_semantics=("arbitrary",), vmem_limit_bytes=VMEM_LIMIT
         ),
     )(offsets, inputs, slot_grads, hidden)
+    found = {}
+    for (n, _, _), out in zip(pieces, outs):
+        found.setdefault(n, []).append(out)
+    return [found[n] for n in range(parts)]
 
 
 def combine_kernel(ranks, rows_in, out, *, experts):
@@ -777,41 +873,36 @@
         return [values] + ([swap_core(values)] if share == 2 else [])
 
     x_full = lax.all_gather(layer_input, "col", axis=1, tiled=True)
-    cotangent_full = lax.all_gather(cotangent, "col", axis=1, tiled=True)
+    x_full, w_out_here = tie(x_full, w_out)
+    out_columns = jnp.zeros((weight_rows, D), bf16)
+    for c, part in [(column, w_out_here)] + column_shifts(lambda _: w_out_here):
+        out_columns = lax.dynamic_update_slice_in_dim(out_columns, part, c * part.shape[1], 1)
+    cotangent_here, out_columns = tie(cotangent, out_columns)
+    cotangent_full = lax.all_gather(cotangent_here, "col", axis=1, tiled=True)
     index_groups = groups_of(jnp.concatenate([routes, priority, ancestry], axis=1))
     index_arrays = jnp.stack(index_groups)
-    all_routes = index_arrays[:, :, :TOPK]
-    all_priority = index_arrays[:, :, TOPK : 2 * TOPK]
-    all_ancestry = index_arrays[:, :, 2 * TOPK :]
+
+    own_all = lax.all_gather(ancestry[:, 0], row_axes, axis=0, tiled=True)
+    project_part = jnp.concatenate([w_query, w_key, w_value], axis=1)
+    own_all, project_part = tie(own_all, project_part)
+    levels_here = range(len(chip_bits(chips)))
+    project_parts = [project_part]
+    for level in levels_here:
+        project_parts = shared_level(project_parts, level)
 
     stacked = jnp.stack([m.transpose(1, 0, 2) for m in (w_gate, w_up, w_down)])
     stacked = stacked.reshape(3, share, experts, weight_rows, H).transpose(1, 0, 2, 3, 4)
     own_weights, other_weights = own_and_other(stacked, core, share)
     starts = [own_weights] + ([swap_core(other_weights)] if share == 2 else [])
-
-    local_project = jnp.concatenate([w_query, w_key, w_value], axis=1)
-    local_project, segments_here, starts[0] = tie(local_project, ancestry[:, 0], starts[0])
-    own_all = lax.all_gather(segments_here, row_axes, axis=0, tiled=True)
-    project = jnp.concatenate(
-        [
-            lax.all_gather(local_project[:, n : n + 256], row_axes, axis=0, tiled=True)
-            for n in range(0, local_project.shape[1], 256)
-        ],
-        axis=1,
-    )
-    gain_rows = column_rows(jnp.concatenate([gain_attention, gain_mixture])[None, :])
-    gains = gain_rows.reshape(columns, 2, width).transpose(1, 0, 2).reshape(2, D)
-    out_columns = jnp.zeros((weight_rows, D), bf16)
-    for c, part in [(column, w_out)] + column_shifts(lambda _: w_out):
-        out_columns = lax.dynamic_update_slice_in_dim(out_columns, part, c * part.shape[1], 1)
-    out_columns, project, own_all = tie(out_columns, project, own_all)
-    out_router = lax.all_gather(
-        jnp.concatenate([out_columns, w_router], axis=1), row_axes, axis=0, tiled=True
-    )
-
+    project_parts, starts, index_arrays = tie(project_parts, starts, index_arrays)
+    all_routes = index_arrays[:, :, :TOPK]
+    all_priority = index_arrays[:, :, TOPK : 2 * TOPK]
+    all_ancestry = index_arrays[:, :, 2 * TOPK :]
+    project = shared_rows(project_parts)
     rounds = gather_rounds(chips, share)
-    project, own_all, starts = tie(project, own_all, starts)
     weights_held = run_gather({(h, 0): v for h, v in enumerate(starts)}, rounds[:1])
+    gains = column_rows(jnp.concatenate([gain_attention, gain_mixture])[None, :])
+    gains = gains.reshape(columns, 2, width).transpose(1, 0, 2).reshape(2, D)
 
     token_starts = jnp.stack([(chip * share + (core ^ g)) * rows for g in range(share)]).astype(i32)
     position, path_bits, query_starts, codes = tree_tables(
@@ -828,14 +919,15 @@
     expert_ids = jnp.arange(EXPERTS, dtype=i32)
     chosen = jnp.any(all_routes[:, None, :, :] == expert_ids[None, :, None, None], axis=3)
 
-    x_full, weights_held = tie(x_full, weights_held)
+    key_bits = (jnp.int32(1) << own_all)[None, :]
+    tables = (ranks, rank_columns, cosine, sine, path_bits, codes, chosen, key_bits, project, gains)
+    out_parts = [jnp.concatenate([out_columns, w_router], axis=1)]
+    out_parts = shared_level(out_parts, 0)
+    x_full, weights_held, tables, out_parts = tie(x_full, weights_held, tables, out_parts)
+    ranks, rank_columns, cosine, sine, path_bits, codes, chosen, key_bits, project, gains = tables
     x_wide = x_full.astype(f32)
     inverse_one = lax.rsqrt(jnp.mean(x_wide * x_wide, axis=1, keepdims=True) + epsilon)
     h_one = (x_wide * inverse_one * gains[0][None, :]).astype(bf16)
-    key_bits = (jnp.int32(1) << own_all)[None, :]
-    h_one, ranks, rank_columns, cosine, sine, path_bits, codes, chosen, key_bits = tie(
-        h_one, ranks, rank_columns, cosine, sine, path_bits, codes, chosen, key_bits
-    )
     projected = dot_dims(project, h_one, 0, 1)
     query_width, key_width = query_heads * HD, key_heads * HD
     query = rotate(
@@ -853,7 +945,9 @@
     received = [own_sent] + ([swap_core(other_sent)] if share == 2 else [])
     query_groups = jnp.stack([r[:, 2:] for r in received], axis=1)
     pairs = [r[:, :2].reshape(own_heads, 2 * HD, rows) for r in received]
-    pairs, weights_held = tie(pairs, weights_held)
+    for level in levels_here[1:]:
+        out_parts = shared_level(out_parts, level)
+    pairs, weights_held, out_parts = tie(pairs, weights_held, out_parts)
     kv_parts = gather_parts(pairs, chips)
     kv_parts, weights_held = tie(kv_parts, weights_held)
     weights_held = run_gather(weights_held, rounds[1 : len(rounds) - 1])
@@ -871,14 +965,15 @@
         for head in range(own_heads)
     ]
     mixed_b = jnp.stack([o[1] for o in attend_outs])
-    mixed_b, weights_held, cotangent_full, out_router = tie(
-        mixed_b, weights_held, cotangent_full, out_router
-    )
+    mixed_b, weights_held, cotangent_full, out_parts = tie(
+        mixed_b, weights_held, cotangent_full, out_parts
+    )
+    out_router = shared_rows(out_parts)
     weights_held = run_gather(weights_held, rounds[len(rounds) - 1 :])
     mixed_other = swap_core(mixed_b[:, 1]) if share == 2 else None
     mixed = in_core_order(mixed_b[:, 0], mixed_other, core).reshape(query_width, rows)
     mixed_full = lax.all_gather(mixed, "col", axis=0, tiled=True)
-    mixed_full, weights_held = tie(mixed_full, weights_held)
+    mixed_full, weights_held, out_router = tie(mixed_full, weights_held, out_router)
     mix_grads = groups_of((branch_scale * cotangent_full.astype(f32)).astype(bf16))
     x_middle, h_two, inverse_two = project_out(
         mixed_full, x_full, gains[1:2], out_router
@@ -923,14 +1018,32 @@
     levels = reduce_levels(chips, share)
     first = [[m for m in moves if m[1]] for moves in levels[0]]
     last = [[m for m in moves if not m[1]] for moves in levels[0]]
-    parts = expert_grads(feature_offsets, inputs, slot_grads, hidden, chips * share, weight_rows)
+    sent = {(h, j ^ bit) for moves in first for h, j, bit in moves}
+    last_sent = {(h, j ^ bit) for moves in last for h, j, bit in moves}
+    parts = expert_grads(
+        feature_offsets,
+        inputs,
+        slot_grads,
+        hidden,
+        chips * share,
+        {j * share + h for h, j in sent | last_sent},
+        weight_rows,
+    )
     sums_held = {(h, j): parts[j * share + h] for j in range(chips) for h in range(share)}
-    first_taken = {}
-    for moves in first:
-        first_taken.update(take(sums_held, moves))
-    staying = [sums_held.pop((h, 0)) for h in range(share)]
-    token_grads, staying, mix_sum, logit_grad = tie(token_grads, staying, mix_sum, logit_grad)
+
+    def take_piece(rounds_here, held):
+        taken = {}
+        for moves in rounds_here:
+            taken.update(take(held, moves))
+        return taken
+
+    first_taken = take_piece(first, {k: sums_held[k][0] for k in sent})
+    staying = [sums_held[h, 0][0] for h in range(share)]
+    token_grads, staying, mix_sum, logit_grad, first_taken = tie(
+        token_grads, staying, mix_sum, logit_grad, first_taken
+    )
     token_grads = token_grads.astype(f32)
+    second_taken = take_piece(first, {k: sums_held[k][1] for k in sent})
 
     token_start = column * token_block
 
@@ -949,29 +1062,37 @@
         - x_part * inverse_part**3 * inner_two / D
     )
     gain_mixture_part = jnp.sum(h_two_grad * x_part * inverse_part, axis=0)
-    branch_grad = lax.all_gather(
-        (branch_scale * x_middle_grad).astype(bf16), "col", axis=0, tiled=True
-    )
-    sums_held = add_taken(sums_held, first_taken)
-    branch_grad, mix_sum, sums_held = tie(branch_grad, mix_sum, sums_held)
+    branch_part = (branch_scale * x_middle_grad).astype(bf16)
+    mixed_parts = dot(branch_part, out_router[:, :D]).astype(bf16)
+    mixed_parts = mixed_parts.reshape(token_block, columns, query_width).transpose(1, 0, 2)
+    mixed_grad = lax.all_to_all(mixed_parts, "col", split_axis=0, concat_axis=0, tiled=True)
+    mixed_grad, branch_part, mix_sum, second_taken = tie(
+        mixed_grad, branch_part, mix_sum, second_taken
+    )
+    branch_grad = lax.all_gather(branch_part, "col", axis=0, tiled=True)
+    sums_here = {}
+    for k, part in first_taken.items():
+        taken = jnp.concatenate([part, second_taken[k]])
+        sums_here[k] = (sums_held[k][0].astype(f32) + taken.astype(f32)).astype(bf16)
+
+    mixed_grad = mixed_grad.reshape(rows, query_width).T
+    mixed_grad, sums_here = tie(mixed_grad, sums_here)
+    own_grad, other_grad = own_and_other(
+        mixed_grad.reshape(share, own_heads, group, HD, rows), core, share
+    )
     arrived = [[part] for part in staying]
     for rounds_here in levels[1:]:
         passed = {}
         for moves in rounds_here:
-            passed.update(take(sums_held, moves))
+            passed.update(take(sums_here, moves))
         for h in range(share):
             if (h, 0) in passed:
                 arrived[h].append(passed.pop((h, 0)))
-        sums_held = add_taken(sums_held, passed)
-    for moves in last:
-        for (h, _), part in take(sums_held, moves).items():
-            arrived[h].append(part)
-
-    own_out = lax.dynamic_slice_in_dim(out_router, column * query_width, query_width, 1)
-    mixed_grad = dot_dims(own_out, branch_grad, 0, 1).astype(bf16)
-    own_grad, other_grad = own_and_other(
-        mixed_grad.reshape(share, own_heads, group, HD, rows), core, share
-    )
+        sums_here = add_taken(sums_here, passed)
+    last_begin = {k: sums_held[k][0] for k in last_sent}
+    last_rest = {k: sums_held[k][1] for k in last_sent}
+    last_rest, own_grad = tie(last_rest, own_grad)
+    last_rest = take_piece(last, last_rest)
     grad_groups = jnp.stack(
         [own_grad] + ([swap_core(other_grad)] if share == 2 else []), axis=1
     )
@@ -994,7 +1115,9 @@
     feature_start = column * width
     x_middle_slice = lax.dynamic_slice_in_dim(x_middle, feature_start, width, 1)
     result = (x_middle_slice + branch_scale * mix_slice).astype(bf16)
-    backward_outs, arrived, branch_later = tie(backward_outs, arrived, branch_grad)
+    backward_outs, arrived, branch_later, last_rest = tie(
+        backward_outs, arrived, branch_grad, last_rest
+    )
     query_grad = jnp.stack([o[0] for o in backward_outs])
     query_grad = rotate_back(query_grad, cosine[None, :, None], sine[None, :, None]).astype(bf16)
     query_other = swap_core(query_grad[:, 1]) if share == 2 else None
@@ -1004,6 +1127,12 @@
     )
     kv_other = swap_core(kv_sums[1]) if share == 2 else None
     kv_grad = in_core_order(kv_sums[0], kv_other, core).astype(f32)
+    kv_grad, last_begin = tie(kv_grad, last_begin)
+    last_begin = take_piece(last, last_begin)
+    for h in range(share):
+        for k in last_rest:
+            if k[0] == h:
+                arrived[h].append(jnp.concatenate([last_begin[k], last_rest[k]]))
     kv_grad = kv_grad.transpose(0, 1, 3, 2).reshape(key_heads, 2 * HD, rows)
     key_pre_grad = (
         rotate_back(kv_grad[:, :HD], cosine[0], sine[0]).astype(bf16).reshape(key_width, rows)
@@ -1030,22 +1159,8 @@
     gain_sums = own_features(gain_parts, column)
     for _, other in column_shifts(lambda c: own_features(gain_parts, c)):
         gain_sums = gain_sums + other
-    small_held = {
-        (h, j): lax.dynamic_slice_in_dim(
-            small_grads, places[j * share + h] * weight_rows, weight_rows, 0
-        )
-        for j in range(chips)
-        for h in range(share)
-    }
-    for rounds_here in levels:
-        taken = {}
-        for moves in rounds_here:
-            taken.update(take(small_held, moves))
-        small_held = add_taken(small_held, taken)
+    small_sum = shared_reduce(small_grads, weight_rows)
     gain_sums = row_sum(gain_sums)
-    small_sum = small_held[0, 0].astype(f32)
-    if share == 2:
-        small_sum = small_sum + swap_core(small_held[1, 0]).astype(f32)
     matrix_grads = [
         in_core_order(sums[0][m], None if returned is None else returned[m], core)
         .astype(f32)

time: 825 us -> 794 us (0.962)
  waiting for transfers between devices: 364 us -> 311 us
  blocking collectives: 38.4 us -> 10.1 us
  local copies, waits for them, and re-layouts: 39.9 us -> 60.2 us
  starting transfers between devices: 63.3 us -> 73.8 us
  Pallas kernels: 184 us -> 194 us
    ppermute x44 -> x53, waiting for transfers between devices: 343 us -> 247 us  [swap(): return lax.ppermute(values, axis, [(i, i ^ bit) for i in range(size)])]
    all_gather x4 -> x1, blocking collectives: 38.4 us -> 10.1 us  [body(): own_all = lax.all_gather(ancestry[:, 0], row_axes, axis=0, tiled=True)]
    ppermute x7 -> x8, waiting for transfers between devices: 0.02 us -> 24.3 us  [shared_swap(): return lax.ppermute(values, ('chip', 'core'), pairs)]
    all_gather x1, waiting for transfers between devices: 0.02 us -> 24.2 us  [body(): x_full = lax.all_gather(layer_input, 'col', axis=1, tiled=True)]
    convert_element_type x2 -> x7, other arithmetic: 4.01 us -> 16.7 us  [the longest x2 9.84 us: body(): (sums_held[k][0].astype(f32) + taken.astype(f32)).astype(bf16)]
    pallas_call x1 -> x3, Pallas kernels: 23.2 us -> 32.6 us  [the longest x1 23.2 us: expert_grads(): pl.pallas_call(functools.partial(expert_grad_kernel, pieces=[(n, begin) f...]
    dynamic_slice x2 -> x9, local copies, waits for them, and re-layouts: 1.18 us -> 10.4 us  [blocks_of(): lax.dynamic_slice_in_dim(values, p * rows, rows, 0)]
    ppermute x15, waiting for transfers between devices: 4.9 us -> 13.8 us  [column_shifts(): lax.ppermute(values_for((me + d) % size), 'col', [(i, (i + d) % size) for...]
  transfers between devices with their start and end apart: 74 -> 84, of which waited for: 31 -> 37; matrix products, arithmetic and copies ran while one was open for 16% -> 20% of each run, Pallas kernels for 13% -> 15%
where the time goes in v3:
time: 794 us; the launch traced here: 783 us
  waiting for transfers between devices  311 us (39%)
  Pallas kernels  194 us (24%)
  other arithmetic  89.9 us (11%)
  starting transfers between devices  73.8 us (9%)
  local copies, waits for them, and re-layouts  60.2 us (8%)
  matrix products  29.3 us (4%)
  between operations  15.9 us (2%)
  blocking collectives  10.1 us (1%)
    ppermute x53, waiting for transfers between devices, swap(): return lax.ppermute(values, axis, [(i, i ^ bit) for i in range(size)])  247 us
    pallas_call x1, Pallas kernels, run_experts(): pl.pallas_call(functools.partial(expert_kernel, parts=parts, groups=group...  57.1 us
    ppermute x53, starting transfers between devices, swap(): return lax.ppermute(values, axis, [(i, i ^ bit) for i in range(size)])  39.7 us
    pallas_call x4, Pallas kernels, combine(): pl.pallas_call(functools.partial(combine_kernel, experts=experts), name='...  32.4 us
    pallas_call x1, Pallas kernels, attend_backward(): pl.pallas_call(kernel, name='attend_backward', grid_spec=pltpu.PrefetchSc...  30.4 us
    ppermute x8, waiting for transfers between devices, shared_swap(): return lax.ppermute(values, ('chip', 'core'), pairs)  24.3 us
    all_gather x1, waiting for transfers between devices, body(): x_full = lax.all_gather(layer_input, 'col', axis=1, tiled=True)  24.2 us
    pallas_call x1, Pallas kernels, expert_grads(): pl.pallas_call(functools.partial(expert_grad_kernel, pieces=[(n, begin) f...  23.2 us
  transfers between devices with their start and end apart: 84, of which 37 were waited for; matrix products, arithmetic and copies ran while one was open for 20% of the time, Pallas kernels for 15%

profile of v3, /device:TPU:0, one launch (start us, length us, event | category | flops | bytes accessed | tf_op | source)
XLA Modules:
  0.0 783.4 jit_solution(7940013570536021258)
XLA Ops:
  14.2 10.1 %all-gather = s32[8192,1]{0,1:T(1,128)S(1)} all-gather(s32[1024,1]{0,1:T(1,128)S(1)} %slice-done), channel_id=2, replica_groups=mesh['chip'=4,'core'=2,'col'=4] {'chip','core'}, dimensions={0}, use_global_device_ids=true | all-gather | bytes 36864 | tf_op jit(solution)/shard_map/all_gather | solution.py:885
  51.6 24.2 %all-gather.6.cloned.1.call-done.x = bf16[1024,1536]{1,0:T(8,128)(2,1)} async-done(((bf16[1024,384]{1,0:T(8,128)(2,1)}), bf16[1024,1536]{1,0:T(8,128)(2,1)}) %all-gather.6.cloned.1.call-update) | async-done | bytes 3145744 | tf_op jit(solution)/shard_map/all_gather | solution.py:875
  99.8 8.5 %slot_ranks.1.ranks = s32[2,8,1024]{2,1,0:T(8,128)} custom-call(s32[1]{0:T(128)} %bitcast.22.first, s32[2,8,1024]{2,1,0:T(8,128)} %copy.203.route_rows, s32[2,8,1024]{2,1,0:T(8,128)} %copy.204.priority_rows, s32[2,1024,8]{2,1,0:T(8,128)} %copy-done.6, s32[2,1024,8]{2,1,0:T(8,128)} %get-tuple-element.453.priority_columns), custom_call_target="tpu_custom_call" | custom-call | tf_op jit(solution)/shard_map/slot_ranks/pallas_call | solution.py:575
  125.8 8.5 %collective-permute-done.19.rest_2_ = bf16[192,1576]{1,0:T(8,128)(2,1)S(1)} collective-permute-done((bf16[192,1576]{1,0:T(8,128)(2,1)}, bf16[192,1576]{1,0:T(8,128)(2,1)S(1)}, u32[]{:S(2)}, u32[]{:S(2)}) %collective-permute-start.19) | collective-permute-done | bytes 605216 | tf_op jit(solution)/shard_map/ppermute | solution.py:152
  134.3 6.8 collective-permute-done.20.rest_3_
  167.9 21.0 %attend_forward.1 = (f32[2,3,64,1024]{3,2,1,0:T(8,128)}, bf16[2,3,64,1024]{3,2,1,0:T(8,128)(2,1)}, f32[2,3,1,1024]{3,2,1,0:T(1,128)}) custom-call(s32[8]{0:T(128)} %stack.248.offsets, s32[4]{0:T(128)} %get-tuple-element.419.starts, s32[64]{0:T(128)} %select_n.283.codes, bf16[2,3,64,1024]{3,2,1,0:T(8,128)(2,1)} %maximum_bitcast_fusion.query, ...), custom_call_target="tpu_custom_call" | custom-call | tf_op jit(solution)/shard_map/attend_forward/pallas_call | solution.py:430
  188.9 36.3 %collective-permute-done.27.rest_10_ = bf16[3,5,192,512]{3,2,1,0:T(8,128)(2,1)S(1)} collective-permute-done((bf16[3,5,192,512]{3,2,1,0:T(8,128)(2,1)}, bf16[3,5,192,512]{3,2,1,0:T(8,128)(2,1)S(1)}, u32[]{:S(2)}, u32[]{:S(2)}) %collective-permute-start.27) | collective-permute-done | bytes 2949152 | tf_op jit(solution)/shard_map/ppermute | solution.py:49
  239.3 5.7 place_rows.3.matrix
  245.0 52.8 %collective-permute-done.30.rest_12_ = bf16[3,5,192,512]{3,2,1,0:T(8,128)(2,1)} collective-permute-done((bf16[3,5,192,512]{3,2,1,0:T(8,128)(2,1)}, bf16[3,5,192,512]{3,2,1,0:T(8,128)(2,1)}, u32[]{:S(2)}, u32[]{:S(2)}) %collective-permute-start.30) | collective-permute-done | bytes 2949152 | tf_op jit(solution)/shard_map/ppermute | solution.py:49
  298.7 11.8 %project_out.1 = (f32[1024,1536]{1,0:T(8,128)}, bf16[1024,1536]{1,0:T(8,128)(2,1)}, f32[1024,1]{1,0:T(8,128)}) custom-call(bf16[1536,1024]{1,0:T(8,128)(2,1)} %all-gather.10.cloned.1.call-done.mixed, bf16[1024,1536]{1,0:T(8,128)(2,1)} %all-gather.6.cloned.1.call-done.x, f32[1,1536]{1,0:T(1,128)} %get-tuple-element.472.gain, bf16[1536,1576]{1,0:T(8,128)(2,1)} %place_rows.3.matrix), custom_call_target="tpu_custom_call" | custom-call | tf_op jit(solution)/shard_map/project_out/pallas_call | solution.py:775
  321.9 57.1 %experts.1 = (bf16[2,5,256,1536]{3,2,1,0:T(8,128)(2,1)}, bf16[2,5,256,1536]{3,2,1,0:T(8,128)(2,1)}, bf16[5,512,1536]{2,1,0:T(8,128)(2,1)}, bf16[5,512,1536]{2,1,...) custom-call(s32[8]{0:T(128)} %stack.279.offsets, s32[1]{0:T(128)} %bitcast.22.first, ...), custom_call_target="tpu_custom_call" | custom-call | tf_op jit(solution)/shard_map/experts/pallas_call | solution.py:647
  378.9 8.2 %combine.5 = bf16[1024,1536]{1,0:T(8,128)(2,1)} custom-call(s32[2,1024,8]{2,1,0:T(8,128)} %bitcast.256, bf16[2,1280,1536]{2,1,0:T(8,128)(2,1)} %bitcast.254), custom_call_target="tpu_custom_call" | custom-call | tf_op jit(solution)/shard_map/combine/pallas_call | solution.py:746
  387.3 8.0 %combine.4 = bf16[1024,1536]{1,0:T(8,128)(2,1)} custom-call(s32[2,1024,8]{2,1,0:T(8,128)} %bitcast.257, bf16[2,1280,1536]{2,1,0:T(8,128)(2,1)} %bitcast.255), custom_call_target="tpu_custom_call" | custom-call | tf_op jit(solution)/shard_map/combine/pallas_call | solution.py:746
  399.8 8.1 %combine.7 = bf16[1024,1536]{1,0:T(8,128)(2,1)} custom-call(s32[2,1024,8]{2,1,0:T(8,128)} %bitcast.258, bf16[2,1280,1536]{2,1,0:T(8,128)(2,1)} %bitcast.252), custom_call_target="tpu_custom_call" | custom-call | tf_op jit(solution)/shard_map/combine/pallas_call | solution.py:746
  417.8 8.0 %combine.6 = bf16[1024,1536]{1,0:T(8,128)(2,1)} custom-call(s32[2,1024,8]{2,1,0:T(8,128)} %bitcast.259, bf16[2,1280,1536]{2,1,0:T(8,128)(2,1)} %bitcast.253), custom_call_target="tpu_custom_call" | custom-call | tf_op jit(solution)/shard_map/combine/pallas_call | solution.py:746
  425.9 23.2 %expert_grads.1 = (bf16[3,5,192,512]{3,2,1,0:T(8,128)(2,1)}, bf16[3,5,192,512]{3,2,1,0:T(8,128)(2,1)}, bf16[1,5,192,512]{3,2,1,0:T(8,128)(2,1)}, bf16[2,5,192,51...) custom-call(s32[8]{0:T(128)} %stack.279.offsets, ...), custom_call_target="tpu_custom_call" | custom-call | tf_op jit(solution)/shard_map/expert_grads/pallas_call | solution.py:707
  459.0 15.2 %collective-permute-done.44 = bf16[1,5,192,512]{3,2,1,0:T(8,128)(2,1)} collective-permute-done((bf16[1,5,192,512]{3,2,1,0:T(8,128)(2,1)}, bf16[1,5,192,512]{3,2,1,0:T(8,128)(2,1)}, u32[]{:S(2)}, u32[]{:S(2)}) %collective-permute-start.44) | collective-permute-done | bytes 983072 | tf_op jit(solution)/shard_map/ppermute | solution.py:49
  491.6 23.2 %collective-permute-done.46 = bf16[2,5,192,512]{3,2,1,0:T(8,128)(2,1)} collective-permute-done((bf16[2,5,192,512]{3,2,1,0:T(8,128)(2,1)}, bf16[2,5,192,512]{3,2,1,0:T(8,128)(2,1)}, u32[]{:S(2)}, u32[]{:S(2)}) %collective-permute-start.46) | collective-permute-done | bytes 1966112 | tf_op jit(solution)/shard_map/ppermute | solution.py:49
  543.2 30.4 %attend_backward.1 = (f32[2,3,64,1024]{3,2,1,0:T(8,128)}, bf16[1024,128]{1,0:T(8,128)(2,1)}, bf16[1024,128]{1,0:T(8,128)(2,1)}, bf16[1024,128]{1,0:T(8,128)(2,1)...) custom-call(s32[8]{0:T(128)} %stack.248.offsets, ...), custom_call_target="tpu_custom_call" | custom-call | tf_op jit(solution)/shard_map/attend_backward/pallas_call | solution.py:479
  573.6 59.8 %collective-permute-done.51 = bf16[2,5,192,512]{3,2,1,0:T(8,128)(2,1)} collective-permute-done((bf16[2,5,192,512]{3,2,1,0:T(8,128)(2,1)}, bf16[2,5,192,512]{3,2,1,0:T(8,128)(2,1)}, u32[]{:S(2)}, u32[]{:S(2)}) %collective-permute-start.51) | collective-permute-done | bytes 1966112 | tf_op jit(solution)/shard_map/ppermute | solution.py:49
  651.2 6.9 collective-permute-done.59
  663.3 5.8 convolution_convert_fusion
  703.7 7.3 collective-permute-done.62
  742.0 7.0 collective-permute-done.61
  (491 shorter events, 313.5 us)
Async XLA Ops:
  7.2 68.7 %all-gather.6.cloned.1.call-start = ((), (), s32[]{:S(2)}) async-start(), calls=%async_computation.4 | async-start | bytes 3932160 | tf_op jit(solution)/shard_map/all_gather | solution.py:875
  7.9 181.0 %all-gather.8.cloned.1.call-start = ((), (), s32[]{:S(2)}) async-start(), calls=%async_computation.5 | async-start | bytes 3932160 | tf_op jit(solution)/shard_map/all_gather | solution.py:881
  40.1 76.8 %collective-permute-start.5 = (bf16[3,5,192,512]{3,2,1,0:T(8,128)(2,1)}, bf16[3,5,192,512]{3,2,1,0:T(8,128)(2,1)}, u32[]{:S(2)}, u32[]{:S(2)}) collective-permute-start(bf16[3,5,192,512]{3,2,1,0:T(8,128)(2,1)} %get-tuple-element.235.rest_6_), channel_id=1, source_target_pairs={{0,8},{8,0},{16,24},{24,16},{1,9},{9,1},{17,25},{25,17},{2,10},{10... | collective-permute-start | bytes 8847368 | tf_op jit(solution)/shard_map/ppermute | solution.py:49
  41.0 76.0 %collective-permute-start.6 = (bf16[3,5,192,512]{3,2,1,0:T(8,128)(2,1)}, bf16[3,5,192,512]{3,2,1,0:T(8,128)(2,1)}, u32[]{:S(2)}, u32[]{:S(2)}) collective-permute-start(bf16[3,5,192,512]{3,2,1,0:T(8,128)(2,1)} %collective-permute-done.3.rest_7_), channel_id=1, source_target_pairs={{0,16},{8,24},{16,0},{24,8},{1,17},{9,25},{17,1},{25,9},{2,18},{10... | collective-permute-start | bytes 8847368 | tf_op jit(solution)/shard_map/ppermute | solution.py:49
  116.7 182.0 %all-gather.10.cloned.1.call-start = ((), (), s32[]{:S(2)}) async-start(), calls=%async_computation.6 | async-start | bytes 3932160 | tf_op jit(solution)/shard_map/all_gather | solution.py:975
  160.6 64.6 %collective-permute-start.27 = (bf16[3,5,192,512]{3,2,1,0:T(8,128)(2,1)}, bf16[3,5,192,512]{3,2,1,0:T(8,128)(2,1)S(1)}, u32[]{:S(2)}, u32[]{:S(2)}) collective-permute-start(bf16[3,5,192,512]{3,2,1,0:T(8,128)(2,1)} %get-tuple-element.235.rest_6_), channel_id=1, source_target_pairs={{0,16},{8,24},{16,0},{24,8},{1,17},{9,25},{17,1},{25,9},{2,18},{10... | collective-permute-start | bytes 8847368 | tf_op jit(solution)/shard_map/ppermute | solution.py:49
  162.2 64.5 %collective-permute-start.28 = (bf16[3,5,192,512]{3,2,1,0:T(8,128)(2,1)}, bf16[3,5,192,512]{3,2,1,0:T(8,128)(2,1)}, u32[]{:S(2)}, u32[]{:S(2)}) collective-permute-start(bf16[3,5,192,512]{3,2,1,0:T(8,128)(2,1)} %collective-permute-done.3.rest_7_), channel_id=1, source_target_pairs={{0,8},{8,0},{16,24},{24,16},{1,9},{9,1},{17,25},{25,17},{2,10},{10... | collective-permute-start | bytes 8847368 | tf_op jit(solution)/shard_map/ppermute | solution.py:49
  231.5 244.5 %reduce-scatter.8.cloned.1.call-start = ((), (), s32[]{:S(2)}) async-start(), calls=%async_computation.7 | async-start | bytes 3932160 | tf_op jit(solution)/shard_map/reduce_scatter | solution.py:1009
  231.5 66.3 %collective-permute-start.30 = (bf16[3,5,192,512]{3,2,1,0:T(8,128)(2,1)}, bf16[3,5,192,512]{3,2,1,0:T(8,128)(2,1)}, u32[]{:S(2)}, u32[]{:S(2)}) collective-permute-start(bf16[3,5,192,512]{3,2,1,0:T(8,128)(2,1)} %collective-permute-done.5.rest_8_), channel_id=1, source_target_pairs={{0,16},{8,24},{16,0},{24,8},{1,17},{9,25},{17,1},{25,9},{2,18},{10... | collective-permute-start | bytes 8847368 | tf_op jit(solution)/shard_map/ppermute | solution.py:49
  232.7 66.0 %collective-permute-start.31 = (bf16[3,5,192,512]{3,2,1,0:T(8,128)(2,1)}, bf16[3,5,192,512]{3,2,1,0:T(8,128)(2,1)}, u32[]{:S(2)}, u32[]{:S(2)}) collective-permute-start(bf16[3,5,192,512]{3,2,1,0:T(8,128)(2,1)} %collective-permute-done.6.rest_11_), channel_id=1, source_target_pairs={{0,8},{8,0},{16,24},{24,16},{1,9},{9,1},{17,25},{25,17},{2,10},{10... | collective-permute-start | bytes 8847368 | tf_op jit(solution)/shard_map/ppermute | solution.py:49
  407.8 47.4 %collective-permute-start.39 = (bf16[1024,1536]{1,0:T(8,128)(2,1)}, bf16[1024,1536]{1,0:T(8,128)(2,1)}, u32[]{:S(2)}, u32[]{:S(2)}) collective-permute-start(bf16[1024,1536]{1,0:T(8,128)(2,1)} %combine.7), channel_id=1, source_target_pairs={{0,4},{4,0},{1,5},{5,1},{2,6},{6,2},{3,7},{7,3},{8,12},{12,8},{9,1... | collective-permute-start | bytes 9437192 | tf_op jit(solution)/shard_map/ppermute | solution.py:49
  412.5 38.4 %collective-permute-start.41 = (f32[10,1024]{1,0:T(8,128)S(1)}, f32[10,1024]{1,0:T(8,128)S(1)}, u32[]{:S(2)}, u32[]{:S(2)}) collective-permute-start(f32[10,1024]{1,0:T(8,128)S(1)} %reshape.401), channel_id=1, source_target_pairs={{0,1},{1,2},{2,3},{3,0},{4,5},{5,6},{6,7},{7,4},{8,9},{9,10},{10,1... | collective-permute-start | bytes 122888 | tf_op jit(solution)/shard_map/ppermute | solution.py:199
  414.3 37.9 %collective-permute-start.42 = (f32[10,1024]{1,0:T(8,128)S(1)}, f32[10,1024]{1,0:T(8,128)S(1)}, u32[]{:S(2)}, u32[]{:S(2)}) collective-permute-start(f32[10,1024]{1,0:T(8,128)S(1)} %reshape.401), channel_id=1, source_target_pairs={{0,2},{1,3},{2,0},{3,1},{4,6},{5,7},{6,4},{7,5},{8,10},{9,11},{10,... | collective-permute-start | bytes 122888 | tf_op jit(solution)/shard_map/ppermute | solution.py:199
  414.8 38.7 %collective-permute-start.43 = (f32[10,1024]{1,0:T(8,128)S(1)}, f32[10,1024]{1,0:T(8,128)S(1)}, u32[]{:S(2)}, u32[]{:S(2)}) collective-permute-start(f32[10,1024]{1,0:T(8,128)S(1)} %reshape.401), channel_id=1, source_target_pairs={{0,3},{1,0},{2,1},{3,2},{4,7},{5,4},{6,5},{7,6},{8,11},{9,8},{10,9... | collective-permute-start | bytes 122888 | tf_op jit(solution)/shard_map/ppermute | solution.py:199
  452.2 62.6 %collective-permute-start.46 = (bf16[2,5,192,512]{3,2,1,0:T(8,128)(2,1)}, bf16[2,5,192,512]{3,2,1,0:T(8,128)(2,1)}, u32[]{:S(2)}, u32[]{:S(2)}) collective-permute-start(bf16[2,5,192,512]{3,2,1,0:T(8,128)(2,1)} %get-tuple-element.256), channel_id=1, source_target_pairs={{0,8},{8,0},{16,24},{24,16},{1,9},{9,1},{17,25},{25,17},{2,10},{10... | collective-permute-start | bytes 5898248 | tf_op jit(solution)/shard_map/ppermute | solution.py:49
  453.5 62.9 %collective-permute-start.47 = (bf16[2,5,192,512]{3,2,1,0:T(8,128)(2,1)}, bf16[2,5,192,512]{3,2,1,0:T(8,128)(2,1)}, u32[]{:S(2)}, u32[]{:S(2)}) collective-permute-start(bf16[2,5,192,512]{3,2,1,0:T(8,128)(2,1)} %get-tuple-element.257), channel_id=1, source_target_pairs={{0,16},{8,24},{16,0},{24,8},{1,17},{9,25},{17,1},{25,9},{2,18},{10... | collective-permute-start | bytes 5898248 | tf_op jit(solution)/shard_map/ppermute | solution.py:49
  491.6 141.9 %all-gather.12.cloned.1.call-start = ((), (), s32[]{:S(2)}) async-start(), calls=%async_computation.8 | async-start | bytes 3932160 | tf_op jit(solution)/shard_map/all_gather | solution.py:1072
  516.4 218.6 %reduce-scatter.10.cloned.1.call-start = ((), (), s32[]{:S(2)}) async-start(), calls=%async_computation.9 | async-start | bytes 3932160
  526.3 107.2 %collective-permute-start.49 = (bf16[3,5,192,512]{3,2,1,0:T(8,128)(2,1)}, bf16[3,5,192,512]{3,2,1,0:T(8,128)(2,1)}, u32[]{:S(2)}, u32[]{:S(2)}) collective-permute-start(bf16[3,5,192,512]{3,2,1,0:T(8,128)(2,1)} %add_convert_fusion.5), channel_id=1, source_target_pairs={{0,16},{8,24},{16,0},{24,8},{1,17},{9,25},{17,1},{25,9},{2,18},{10... | collective-permute-start | bytes 8847368 | tf_op jit(solution)/shard_map/ppermute | solution.py:49
  527.4 106.1 %collective-permute-start.50 = (bf16[3,5,192,512]{3,2,1,0:T(8,128)(2,1)}, bf16[3,5,192,512]{3,2,1,0:T(8,128)(2,1)}, u32[]{:S(2)}, u32[]{:S(2)}) collective-permute-start(bf16[3,5,192,512]{3,2,1,0:T(8,128)(2,1)} %add_convert_fusion.4), channel_id=1, source_target_pairs={{0,8},{8,0},{16,24},{24,16},{1,9},{9,1},{17,25},{25,17},{2,10},{10... | collective-permute-start | bytes 8847368 | tf_op jit(solution)/shard_map/ppermute | solution.py:49
  532.5 101.0 %collective-permute-start.51 = (bf16[2,5,192,512]{3,2,1,0:T(8,128)(2,1)}, bf16[2,5,192,512]{3,2,1,0:T(8,128)(2,1)}, u32[]{:S(2)}, u32[]{:S(2)}) collective-permute-start(bf16[2,5,192,512]{3,2,1,0:T(8,128)(2,1)} %get-tuple-element.286), channel_id=1, source_target_pairs={{0,8},{8,0},{16,24},{24,16},{1,9},{9,1},{17,25},{25,17},{2,10},{10... | collective-permute-start | bytes 5898248 | tf_op jit(solution)/shard_map/ppermute | solution.py:49
  533.8 99.7 %collective-permute-start.52 = (bf16[2,5,192,512]{3,2,1,0:T(8,128)(2,1)}, bf16[2,5,192,512]{3,2,1,0:T(8,128)(2,1)}, u32[]{:S(2)}, u32[]{:S(2)}) collective-permute-start(bf16[2,5,192,512]{3,2,1,0:T(8,128)(2,1)} %get-tuple-element.287), channel_id=1, source_target_pairs={{0,16},{8,24},{16,0},{24,8},{1,17},{9,25},{17,1},{25,9},{2,18},{10... | collective-permute-start | bytes 5898248 | tf_op jit(solution)/shard_map/ppermute | solution.py:49
  537.6 231.4 %reduce-scatter.12.cloned.1.call-start = ((), (), s32[]{:S(2)}) async-start(), calls=%async_computation.10 | async-start | bytes 3932160
  716.7 41.8 %collective-permute-start.63 = (bf16[3,5,192,512]{3,2,1,0:T(8,128)(2,1)}, bf16[3,5,192,512]{3,2,1,0:T(8,128)(2,1)}, u32[]{:S(2)}, u32[]{:S(2)}) collective-permute-start(bf16[3,5,192,512]{3,2,1,0:T(8,128)(2,1)} %add_convert_fusion.2), channel_id=1, source_target_pairs={{0,4},{4,0},{1,5},{5,1},{2,6},{6,2},{3,7},{7,3},{8,12},{12,8},{9,1... | collective-permute-start | bytes 8847368 | tf_op jit(solution)/shard_map/ppermute | solution.py:49
  (134 other events, 1890.9 us)
Sparse Core Ops, SparseCore 0:
  9.6 66.2 all-gather.5
  116.8 61.6 all-gather.7
  231.6 62.2 all-gather.9
  399.9 63.0 reduce-scatter.7
  516.5 61.3 all-gather.11
  580.6 58.8 reduce-scatter.9
  695.7 58.0 reduce-scatter.11

commit v4 on v3

--- a/solution.py
+++ b/solution.py
@@ -167,24 +167,13 @@
     return place_rows(jnp.stack([p * rows for p in places]).astype(i32), parts)
 
 
-def shared_reduce(values, rows):
-    chips, share, core = lax.axis_size("chip"), lax.axis_size("core"), lax.axis_index("core")
-
-    def blocks_of(k):
-        return jnp.stack(
-            [
-                lax.dynamic_slice_in_dim(values, p * rows, rows, 0)
-                for p in shared_places(chips, share, k)
-            ]
-        )
-
+def shared_reduce(held, other):
     def add(left, right):
         return (left.astype(f32) + right.astype(f32)).astype(left.dtype)
 
-    held = blocks_of(core)
-    if share == 2:
-        held = add(held, swap_core(blocks_of(1 - core)))
-    for level in reversed(range(len(chip_bits(chips)))):
+    if other is not None:
+        held = add(held, swap_core(other))
+    for level in reversed(range(len(chip_bits(lax.axis_size("chip"))))):
         half = 1 << level
         held = add(held[:half], shared_swap(held[half:], level))
     return held[0].astype(f32)
@@ -794,6 +783,47 @@
     )(mixed, x, gain, matrix)
 
 
+def rows_of(columns):
+    return columns[...].astype(f32).T.astype(bf16)
+
+
+def matrix_grad_kernel(
+    offsets, h_one, project_grad, branch_grad, mixed, h_two, logit_grad, project, *rest
+):
+    outs, gain, total = rest[:-2], rest[-2], rest[-1]
+    wide = project_grad.shape[0]
+    end = wide + mixed.shape[0]
+    late = dot_dims(h_one[...], rows_of(project_grad), 0, 0)
+    gain[...] = jnp.sum(late * project[...].astype(f32), axis=1, keepdims=True)
+    total[:, :wide] = late
+    total[:, wide:end] = dot_dims(branch_grad[...], rows_of(mixed), 0, 0)
+    total[:, end:] = dot_dims(h_two[...], rows_of(logit_grad), 0, 0)
+    for k, out in enumerate(outs):
+        count, rows, _ = out.shape
+        for p in range(count):
+            at = pl.ds(pl.multiple_of(offsets[k * count + p], rows), rows)
+            out[p] = total[at, :].astype(bf16)
+
+
+def matrix_grads_of(offsets, share, arrays):
+    width = sum(a.shape[0] for a in (arrays[1], arrays[3], arrays[5]))
+    count = offsets.shape[0] // share
+    out = jax.ShapeDtypeStruct((count, D // (count * share), width), bf16)
+    return pl.pallas_call(
+        matrix_grad_kernel,
+        name="matrix_grads",
+        grid_spec=pltpu.PrefetchScalarGridSpec(
+            num_scalar_prefetch=1,
+            grid=(1,),
+            in_specs=[whole(a.shape) for a in arrays],
+            out_specs=[whole(out.shape)] * share + [whole((D, 1))],
+            scratch_shapes=[pltpu.VMEM((D, width), f32)],
+        ),
+        out_shape=[out] * share + [jax.ShapeDtypeStruct((D, 1), f32)],
+        compiler_params=pltpu.CompilerParams(vmem_limit_bytes=VMEM_LIMIT),
+    )(offsets, *arrays)
+
+
 def rotate(values, cosine, sine):
     first = values[..., : HD // 2, :]
     second = values[..., HD // 2 :, :]
@@ -873,12 +903,6 @@
         return [values] + ([swap_core(values)] if share == 2 else [])
 
     x_full = lax.all_gather(layer_input, "col", axis=1, tiled=True)
-    x_full, w_out_here = tie(x_full, w_out)
-    out_columns = jnp.zeros((weight_rows, D), bf16)
-    for c, part in [(column, w_out_here)] + column_shifts(lambda _: w_out_here):
-        out_columns = lax.dynamic_update_slice_in_dim(out_columns, part, c * part.shape[1], 1)
-    cotangent_here, out_columns = tie(cotangent, out_columns)
-    cotangent_full = lax.all_gather(cotangent_here, "col", axis=1, tiled=True)
     index_groups = groups_of(jnp.concatenate([routes, priority, ancestry], axis=1))
     index_arrays = jnp.stack(index_groups)
 
@@ -920,10 +944,17 @@
     chosen = jnp.any(all_routes[:, None, :, :] == expert_ids[None, :, None, None], axis=3)
 
     key_bits = (jnp.int32(1) << own_all)[None, :]
+    early_tables = (ranks, rank_columns, codes, path_bits, chosen, cosine, sine, project)
+    x_full, w_out_here, early_tables = tie(x_full, w_out, early_tables)
+    ranks, rank_columns, codes, path_bits, chosen, cosine, sine, project = early_tables
+    out_columns = jnp.zeros((weight_rows, D), bf16)
+    for c, part in [(column, w_out_here)] + column_shifts(lambda _: w_out_here):
+        out_columns = lax.dynamic_update_slice_in_dim(out_columns, part, c * part.shape[1], 1)
+    cotangent_here, out_columns = tie(cotangent, out_columns)
+    cotangent_full = lax.all_gather(cotangent_here, "col", axis=1, tiled=True)
     tables = (ranks, rank_columns, cosine, sine, path_bits, codes, chosen, key_bits, project, gains)
     out_parts = [jnp.concatenate([out_columns, w_router], axis=1)]
-    out_parts = shared_level(out_parts, 0)
-    x_full, weights_held, tables, out_parts = tie(x_full, weights_held, tables, out_parts)
+    x_full, weights_held, tables = tie(x_full, weights_held, tables)
     ranks, rank_columns, cosine, sine, path_bits, codes, chosen, key_bits, project, gains = tables
     x_wide = x_full.astype(f32)
     inverse_one = lax.rsqrt(jnp.mean(x_wide * x_wide, axis=1, keepdims=True) + epsilon)
@@ -945,7 +976,7 @@
     received = [own_sent] + ([swap_core(other_sent)] if share == 2 else [])
     query_groups = jnp.stack([r[:, 2:] for r in received], axis=1)
     pairs = [r[:, :2].reshape(own_heads, 2 * HD, rows) for r in received]
-    for level in levels_here[1:]:
+    for level in levels_here:
         out_parts = shared_level(out_parts, level)
     pairs, weights_held, out_parts = tie(pairs, weights_held, out_parts)
     kv_parts = gather_parts(pairs, chips)
@@ -1146,11 +1177,15 @@
     h_one_grad = lax.psum_scatter(h_one_part, "col", scatter_dimension=0, tiled=True)
     inner_one = column_sum(jnp.sum(project_grad.astype(f32) * projected, axis=0))[:, None]
     sums = [functools.reduce(jnp.add, [p.astype(f32) for p in own]).astype(bf16) for own in arrived]
-    returned = swap_core(sums[1]) if share == 2 else None
-    late = dot_dims(h_one, project_grad, 0, 1)
-    early = [dot_dims(branch_later, mixed, 0, 1), dot_dims(h_two, logit_grad, 0, 1)]
-    small_grads = jnp.concatenate([late] + early, axis=1).astype(bf16)
-    gain_attention_part = jnp.sum(late * project.astype(f32), axis=1) / gains[0]
+    small_places = shared_places(chips, share, core)
+    if share == 2:
+        small_places = small_places + shared_places(chips, share, 1 - core)
+    *small_parts, gain_column = matrix_grads_of(
+        jnp.stack([p * weight_rows for p in small_places]).astype(i32),
+        share,
+        (h_one, project_grad, branch_later, mixed, h_two, logit_grad, project),
+    )
+    gain_attention_part = gain_column[:, 0] / gains[0]
     gain_parts = jnp.stack([gain_attention_part, gain_mixture_part])
 
     def own_features(array, c):
@@ -1159,7 +1194,9 @@
     gain_sums = own_features(gain_parts, column)
     for _, other in column_shifts(lambda c: own_features(gain_parts, c)):
         gain_sums = gain_sums + other
-    small_sum = shared_reduce(small_grads, weight_rows)
+    small_parts, sums = tie(small_parts, sums)
+    returned = swap_core(sums[1]) if share == 2 else None
+    small_sum = shared_reduce(small_parts[0], small_parts[1] if share == 2 else None)
     gain_sums = row_sum(gain_sums)
     matrix_grads = [
         in_core_order(sums[0][m], None if returned is None else returned[m], core)

time: 794 us -> 770 us (0.970)
  Pallas kernels: 194 us -> 207 us
  local copies, waits for them, and re-layouts: 60.2 us -> 48.2 us
  matrix products: 29.3 us -> 18.8 us
  waiting for transfers between devices: 311 us -> 302 us
    all_gather x1, waiting for transfers between devices: 24.2 us -> 3.08 us  [body(): x_full = lax.all_gather(layer_input, 'col', axis=1, tiled=True)]
    unnamed x9, waiting for transfers between devices: 0.78 us -> 14.5 us
    pallas_call x0 -> x1, Pallas kernels: none -> 13.1 us  [matrix_grads_of(): pl.pallas_call(matrix_grad_kernel, name='matrix_grads', grid_spec=pltpu.P...]
    dynamic_slice x9 -> x0, local copies, waits for them, and re-layouts: 10.4 us -> none  [blocks_of(): lax.dynamic_slice_in_dim(values, p * rows, rows, 0)]
    dot_general x7 -> x4, matrix products: 19.5 us -> 10.5 us  [dot_dims(): lax.dot_general(left, right, (((left_dim,), (right_dim,)), ((), ())), pre...]
  transfers between devices with their start and end apart: 84 -> 84, of which waited for: 37 -> 45; matrix products, arithmetic and copies ran while one was open for 20% -> 17% of each run, Pallas kernels for 15% -> 17%
where the time goes in v4:
time: 770 us; the launch traced here: 760 us
  waiting for transfers between devices  302 us (39%)
  Pallas kernels  207 us (27%)
  other arithmetic  86.7 us (11%)
  starting transfers between devices  71.2 us (9%)
  local copies, waits for them, and re-layouts  48.2 us (6%)
  matrix products  18.8 us (2%)
  between operations  15.9 us (2%)
  blocking collectives  10.1 us (1%)
    ppermute x53, waiting for transfers between devices, swap(): return lax.ppermute(values, axis, [(i, i ^ bit) for i in range(size)])  250 us
    pallas_call x1, Pallas kernels, run_experts(): pl.pallas_call(functools.partial(expert_kernel, parts=parts, groups=group...  57 us
    ppermute x53, starting transfers between devices, swap(): return lax.ppermute(values, axis, [(i, i ^ bit) for i in range(size)])  34.2 us
    pallas_call x4, Pallas kernels, combine(): pl.pallas_call(functools.partial(combine_kernel, experts=experts), name='...  32.4 us
    pallas_call x1, Pallas kernels, attend_backward(): pl.pallas_call(kernel, name='attend_backward', grid_spec=pltpu.PrefetchSc...  30.5 us
    pallas_call x1, Pallas kernels, expert_grads(): pl.pallas_call(functools.partial(expert_grad_kernel, pieces=[(n, begin) f...  23.1 us
    ppermute x15, starting transfers between devices, column_shifts(): lax.ppermute(values_for((me + d) % size), 'col', [(i, (i + d) % size) for...  22.3 us
    ppermute x8, waiting for transfers between devices, shared_swap(): return lax.ppermute(values, ('chip', 'core'), pairs)  22.1 us
  transfers between devices with their start and end apart: 84, of which 45 were waited for; matrix products, arithmetic and copies ran while one was open for 17% of the time, Pallas kernels for 17%

profile of v4, /device:TPU:0, one launch (start us, length us, event | category | flops | bytes accessed | tf_op | source)
XLA Modules:
  0.0 760.0 jit_solution(5516588386716643036)
XLA Ops:
  13.6 10.1 %all-gather = s32[8192,1]{0,1:T(1,128)S(1)} all-gather(s32[1024,1]{0,1:T(1,128)S(1)} %slice-done.1), channel_id=2, replica_groups=mesh['chip'=4,'core'=2,'col'=4] {'chip','core'}, dimensions={0}, use_global_device_ids=true | all-gather | bytes 36864 | tf_op jit(solution)/shard_map/all_gather | solution.py:909
  54.7 8.5 %slot_ranks.1.ranks = s32[2,8,1024]{2,1,0:T(8,128)} custom-call(s32[1]{0:T(128)} %bitcast.8.first, s32[2,8,1024]{2,1,0:T(8,128)} %copy.150.route_rows, s32[2,8,1024]{2,1,0:T(8,128)} %copy.151.priority_rows, s32[2,1024,8]{2,1,0:T(8,128)} %copy-done.7, s32[2,1024,8]{2,1,0:T(8,128)} %get-tuple-element.459.priority_columns), custom_call_target="tpu_custom_call" | custom-call | tf_op jit(solution)/shard_map/slot_ranks/pallas_call | solution.py:564
  118.8 8.5 %collective-permute-done.19.rest_2_ = bf16[192,1576]{1,0:T(8,128)(2,1)S(1)} collective-permute-done((bf16[192,1576]{1,0:T(8,128)(2,1)}, bf16[192,1576]{1,0:T(8,128)(2,1)S(1)}, u32[]{:S(2)}, u32[]{:S(2)}) %collective-permute-start.19) | collective-permute-done | bytes 605216 | tf_op jit(solution)/shard_map/ppermute | solution.py:152
  127.3 6.8 collective-permute-done.20.rest_3_
  160.1 21.0 %attend_forward.1 = (f32[2,3,64,1024]{3,2,1,0:T(8,128)}, bf16[2,3,64,1024]{3,2,1,0:T(8,128)(2,1)}, f32[2,3,1,1024]{3,2,1,0:T(1,128)}) custom-call(s32[8]{0:T(128)} %stack.227.offsets, s32[4]{0:T(128)} %get-tuple-element.433.starts, s32[64]{0:T(128)} %select_n.257.codes, bf16[2,3,64,1024]{3,2,1,0:T(8,128)(2,1)} %maximum_bitcast_fusion.query, ...), custom_call_target="tpu_custom_call" | custom-call | tf_op jit(solution)/shard_map/attend_forward/pallas_call | solution.py:419
  181.2 37.1 %collective-permute-done.27.rest_10_ = bf16[3,5,192,512]{3,2,1,0:T(8,128)(2,1)S(1)} collective-permute-done((bf16[3,5,192,512]{3,2,1,0:T(8,128)(2,1)}, bf16[3,5,192,512]{3,2,1,0:T(8,128)(2,1)S(1)}, u32[]{:S(2)}, u32[]{:S(2)}) %collective-permute-start.27) | collective-permute-done | bytes 2949152 | tf_op jit(solution)/shard_map/ppermute | solution.py:49
  231.9 5.9 place_rows.3.matrix
  237.8 53.2 %collective-permute-done.30.rest_12_ = bf16[3,5,192,512]{3,2,1,0:T(8,128)(2,1)} collective-permute-done((bf16[3,5,192,512]{3,2,1,0:T(8,128)(2,1)}, bf16[3,5,192,512]{3,2,1,0:T(8,128)(2,1)}, u32[]{:S(2)}, u32[]{:S(2)}) %collective-permute-start.30) | collective-permute-done | bytes 2949152 | tf_op jit(solution)/shard_map/ppermute | solution.py:49
  291.8 11.8 %project_out.1 = (f32[1024,1536]{1,0:T(8,128)}, bf16[1024,1536]{1,0:T(8,128)(2,1)}, f32[1024,1]{1,0:T(8,128)}) custom-call(bf16[1536,1024]{1,0:T(8,128)(2,1)} %all-gather.10.cloned.1.call-done.mixed, bf16[1024,1536]{1,0:T(8,128)(2,1)} %all-gather.6.cloned.1.call-done.x, f32[1,1536]{1,0:T(1,128)} %get-tuple-element.478.gain, bf16[1536,1576]{1,0:T(8,128)(2,1)} %place_rows.3.matrix), custom_call_target="tpu_custom_call" | custom-call | tf_op jit(solution)/shard_map/project_out/pallas_call | solution.py:764
  315.1 57.0 %experts.1 = (bf16[2,5,256,1536]{3,2,1,0:T(8,128)(2,1)}, bf16[2,5,256,1536]{3,2,1,0:T(8,128)(2,1)}, bf16[5,512,1536]{2,1,0:T(8,128)(2,1)}, bf16[5,512,1536]{2,1,...) custom-call(s32[8]{0:T(128)} %stack.258.offsets, s32[1]{0:T(128)} %bitcast.8.first, ...), custom_call_target="tpu_custom_call" | custom-call | tf_op jit(solution)/shard_map/experts/pallas_call | solution.py:636
  372.1 8.2 %combine.5 = bf16[1024,1536]{1,0:T(8,128)(2,1)} custom-call(s32[2,1024,8]{2,1,0:T(8,128)} %bitcast.244, bf16[2,1280,1536]{2,1,0:T(8,128)(2,1)} %bitcast.242), custom_call_target="tpu_custom_call" | custom-call | tf_op jit(solution)/shard_map/combine/pallas_call | solution.py:735
  380.5 8.0 %combine.4 = bf16[1024,1536]{1,0:T(8,128)(2,1)} custom-call(s32[2,1024,8]{2,1,0:T(8,128)} %bitcast.245, bf16[2,1280,1536]{2,1,0:T(8,128)(2,1)} %bitcast.243), custom_call_target="tpu_custom_call" | custom-call | tf_op jit(solution)/shard_map/combine/pallas_call | solution.py:735
  392.9 8.1 %combine.7 = bf16[1024,1536]{1,0:T(8,128)(2,1)} custom-call(s32[2,1024,8]{2,1,0:T(8,128)} %bitcast.246, bf16[2,1280,1536]{2,1,0:T(8,128)(2,1)} %bitcast.240), custom_call_target="tpu_custom_call" | custom-call | tf_op jit(solution)/shard_map/combine/pallas_call | solution.py:735
  412.4 8.0 %combine.6 = bf16[1024,1536]{1,0:T(8,128)(2,1)} custom-call(s32[2,1024,8]{2,1,0:T(8,128)} %bitcast.247, bf16[2,1280,1536]{2,1,0:T(8,128)(2,1)} %bitcast.241), custom_call_target="tpu_custom_call" | custom-call | tf_op jit(solution)/shard_map/combine/pallas_call | solution.py:735
  420.4 23.1 %expert_grads.1 = (bf16[3,5,192,512]{3,2,1,0:T(8,128)(2,1)}, bf16[3,5,192,512]{3,2,1,0:T(8,128)(2,1)}, bf16[1,5,192,512]{3,2,1,0:T(8,128)(2,1)}, bf16[2,5,192,51...) custom-call(s32[8]{0:T(128)} %stack.258.offsets, ...), custom_call_target="tpu_custom_call" | custom-call | tf_op jit(solution)/shard_map/expert_grads/pallas_call | solution.py:696
  453.4 15.1 %collective-permute-done.44 = bf16[1,5,192,512]{3,2,1,0:T(8,128)(2,1)} collective-permute-done((bf16[1,5,192,512]{3,2,1,0:T(8,128)(2,1)}, bf16[1,5,192,512]{3,2,1,0:T(8,128)(2,1)}, u32[]{:S(2)}, u32[]{:S(2)}) %collective-permute-start.44) | collective-permute-done | bytes 983072 | tf_op jit(solution)/shard_map/ppermute | solution.py:49
  485.7 23.3 %collective-permute-done.46 = bf16[2,5,192,512]{3,2,1,0:T(8,128)(2,1)} collective-permute-done((bf16[2,5,192,512]{3,2,1,0:T(8,128)(2,1)}, bf16[2,5,192,512]{3,2,1,0:T(8,128)(2,1)}, u32[]{:S(2)}, u32[]{:S(2)}) %collective-permute-start.46) | collective-permute-done | bytes 1966112 | tf_op jit(solution)/shard_map/ppermute | solution.py:49
  510.5 5.4 add_convert_fusion.5
  535.5 30.5 %attend_backward.1 = (f32[2,3,64,1024]{3,2,1,0:T(8,128)}, bf16[1024,128]{1,0:T(8,128)(2,1)}, bf16[1024,128]{1,0:T(8,128)(2,1)}, bf16[1024,128]{1,0:T(8,128)(2,1)...) custom-call(s32[8]{0:T(128)} %stack.227.offsets, ...), custom_call_target="tpu_custom_call" | custom-call | tf_op jit(solution)/shard_map/attend_backward/pallas_call | solution.py:468
  566.0 61.5 %collective-permute-done.51 = bf16[2,5,192,512]{3,2,1,0:T(8,128)(2,1)} collective-permute-done((bf16[2,5,192,512]{3,2,1,0:T(8,128)(2,1)}, bf16[2,5,192,512]{3,2,1,0:T(8,128)(2,1)}, u32[]{:S(2)}, u32[]{:S(2)}) %collective-permute-start.51) | collective-permute-done | bytes 1966112 | tf_op jit(solution)/shard_map/ppermute | solution.py:49
  643.4 6.7 collective-permute-done.59
  661.9 13.1 %matrix_grads.1 = (bf16[4,192,1064]{2,1,0:T(8,128)(2,1)}, bf16[4,192,1064]{2,1,0:T(8,128)(2,1)}, f32[1536,1]{1,0:T(8,128)}) custom-call(s32[8]{0:T(128)} %stack.244.offsets, bf16[1024,1536]{1,0:T(8,128)(2,1)} %copy-done.2, bf16[640,1024]{1,0:T(8,128)(2,1)} %copy-done.3, bf16[1024,1536]{1,0:T(8,128)(2,1)} %all-gather.12.cloned.1.call-done.branch_grad, ...), custom_call_target="tpu_custom_call" | custom-call | tf_op jit(solution)/shard_map/matrix_grads/pallas_call | solution.py:812
  681.7 5.6 add_convert_fusion.2
  731.3 14.4 %reduce-scatter.12.cloned.1.call-done = bf16[384,1024]{1,0:T(8,128)(2,1)} async-done(((bf16[1536,1024]{1,0:T(8,128)(2,1)}), bf16[384,1024]{1,0:T(8,128)(2,1)}) %reduce-scatter.12.cloned.1.call-update) | async-done | bytes 786448
  (491 shorter events, 293.0 us)
Async XLA Ops:
  7.2 72.4 %all-gather.6.cloned.1.call-start = ((), (), s32[]{:S(2)}) async-start(), calls=%async_computation.4 | async-start | bytes 3932160 | tf_op jit(solution)/shard_map/all_gather | solution.py:905
  13.5 167.6 %all-gather.8.cloned.1.call-start = ((), (), s32[]{:S(2)}) async-start(), calls=%async_computation.5 | async-start | bytes 3932160 | tf_op jit(solution)/shard_map/all_gather | solution.py:954
  39.3 63.9 %collective-permute-start.9 = (bf16[3,5,192,512]{3,2,1,0:T(8,128)(2,1)}, bf16[3,5,192,512]{3,2,1,0:T(8,128)(2,1)}, u32[]{:S(2)}, u32[]{:S(2)}) collective-permute-start(bf16[3,5,192,512]{3,2,1,0:T(8,128)(2,1)} %get-tuple-element.254.rest_6_), channel_id=1, source_target_pairs={{0,8},{8,0},{16,24},{24,16},{1,9},{9,1},{17,25},{25,17},{2,10},{10... | collective-permute-start | bytes 8847368 | tf_op jit(solution)/shard_map/ppermute | solution.py:49
  40.9 67.1 %collective-permute-start.10 = (bf16[3,5,192,512]{3,2,1,0:T(8,128)(2,1)}, bf16[3,5,192,512]{3,2,1,0:T(8,128)(2,1)}, u32[]{:S(2)}, u32[]{:S(2)}) collective-permute-start(bf16[3,5,192,512]{3,2,1,0:T(8,128)(2,1)} %collective-permute-done.3.rest_7_), channel_id=1, source_target_pairs={{0,16},{8,24},{16,0},{24,8},{1,17},{9,25},{17,1},{25,9},{2,18},{10... | collective-permute-start | bytes 8847368 | tf_op jit(solution)/shard_map/ppermute | solution.py:49
  98.2 193.6 %all-gather.10.cloned.1.call-start = ((), (), s32[]{:S(2)}) async-start(), calls=%async_computation.6 | async-start | bytes 3932160 | tf_op jit(solution)/shard_map/all_gather | solution.py:1006
  153.6 64.7 %collective-permute-start.27 = (bf16[3,5,192,512]{3,2,1,0:T(8,128)(2,1)}, bf16[3,5,192,512]{3,2,1,0:T(8,128)(2,1)S(1)}, u32[]{:S(2)}, u32[]{:S(2)}) collective-permute-start(bf16[3,5,192,512]{3,2,1,0:T(8,128)(2,1)} %get-tuple-element.254.rest_6_), channel_id=1, source_target_pairs={{0,16},{8,24},{16,0},{24,8},{1,17},{9,25},{17,1},{25,9},{2,18},{10... | collective-permute-start | bytes 8847368 | tf_op jit(solution)/shard_map/ppermute | solution.py:49
  155.3 64.5 %collective-permute-start.28 = (bf16[3,5,192,512]{3,2,1,0:T(8,128)(2,1)}, bf16[3,5,192,512]{3,2,1,0:T(8,128)(2,1)}, u32[]{:S(2)}, u32[]{:S(2)}) collective-permute-start(bf16[3,5,192,512]{3,2,1,0:T(8,128)(2,1)} %collective-permute-done.3.rest_7_), channel_id=1, source_target_pairs={{0,8},{8,0},{16,24},{24,16},{1,9},{9,1},{17,25},{25,17},{2,10},{10... | collective-permute-start | bytes 8847368 | tf_op jit(solution)/shard_map/ppermute | solution.py:49
  224.7 245.4 %reduce-scatter.8.cloned.1.call-start = ((), (), s32[]{:S(2)}) async-start(), calls=%async_computation.7 | async-start | bytes 3932160 | tf_op jit(solution)/shard_map/reduce_scatter | solution.py:1040
  224.7 66.3 %collective-permute-start.30 = (bf16[3,5,192,512]{3,2,1,0:T(8,128)(2,1)}, bf16[3,5,192,512]{3,2,1,0:T(8,128)(2,1)}, u32[]{:S(2)}, u32[]{:S(2)}) collective-permute-start(bf16[3,5,192,512]{3,2,1,0:T(8,128)(2,1)} %collective-permute-done.9.rest_8_), channel_id=1, source_target_pairs={{0,16},{8,24},{16,0},{24,8},{1,17},{9,25},{17,1},{25,9},{2,18},{10... | collective-permute-start | bytes 8847368 | tf_op jit(solution)/shard_map/ppermute | solution.py:49
  225.8 66.0 %collective-permute-start.31 = (bf16[3,5,192,512]{3,2,1,0:T(8,128)(2,1)}, bf16[3,5,192,512]{3,2,1,0:T(8,128)(2,1)}, u32[]{:S(2)}, u32[]{:S(2)}) collective-permute-start(bf16[3,5,192,512]{3,2,1,0:T(8,128)(2,1)} %collective-permute-done.10.rest_11_), channel_id=1, source_target_pairs={{0,8},{8,0},{16,24},{24,16},{1,9},{9,1},{17,25},{25,17},{2,10},{10... | collective-permute-start | bytes 8847368 | tf_op jit(solution)/shard_map/ppermute | solution.py:49
  401.0 48.7 %collective-permute-start.39 = (bf16[1024,1536]{1,0:T(8,128)(2,1)}, bf16[1024,1536]{1,0:T(8,128)(2,1)}, u32[]{:S(2)}, u32[]{:S(2)}) collective-permute-start(bf16[1024,1536]{1,0:T(8,128)(2,1)} %combine.7), channel_id=1, source_target_pairs={{0,4},{4,0},{1,5},{5,1},{2,6},{6,2},{3,7},{7,3},{8,12},{12,8},{9,1... | collective-permute-start | bytes 9437192 | tf_op jit(solution)/shard_map/ppermute | solution.py:49
  405.8 39.2 %collective-permute-start.41 = (f32[10,1024]{1,0:T(8,128)S(1)}, f32[10,1024]{1,0:T(8,128)S(1)}, u32[]{:S(2)}, u32[]{:S(2)}) collective-permute-start(f32[10,1024]{1,0:T(8,128)S(1)} %reshape.402), channel_id=1, source_target_pairs={{0,1},{1,2},{2,3},{3,0},{4,5},{5,6},{6,7},{7,4},{8,9},{9,10},{10,1... | collective-permute-start | bytes 122888 | tf_op jit(solution)/shard_map/ppermute | solution.py:188
  406.7 39.7 %collective-permute-start.42 = (f32[10,1024]{1,0:T(8,128)S(1)}, f32[10,1024]{1,0:T(8,128)S(1)}, u32[]{:S(2)}, u32[]{:S(2)}) collective-permute-start(f32[10,1024]{1,0:T(8,128)S(1)} %reshape.402), channel_id=1, source_target_pairs={{0,2},{1,3},{2,0},{3,1},{4,6},{5,7},{6,4},{7,5},{8,10},{9,11},{10,... | collective-permute-start | bytes 122888 | tf_op jit(solution)/shard_map/ppermute | solution.py:188
  409.0 38.9 %collective-permute-start.43 = (f32[10,1024]{1,0:T(8,128)S(1)}, f32[10,1024]{1,0:T(8,128)S(1)}, u32[]{:S(2)}, u32[]{:S(2)}) collective-permute-start(f32[10,1024]{1,0:T(8,128)S(1)} %reshape.402), channel_id=1, source_target_pairs={{0,3},{1,0},{2,1},{3,2},{4,7},{5,4},{6,5},{7,6},{8,11},{9,8},{10,9... | collective-permute-start | bytes 122888 | tf_op jit(solution)/shard_map/ppermute | solution.py:188
  446.5 62.5 %collective-permute-start.46 = (bf16[2,5,192,512]{3,2,1,0:T(8,128)(2,1)}, bf16[2,5,192,512]{3,2,1,0:T(8,128)(2,1)}, u32[]{:S(2)}, u32[]{:S(2)}) collective-permute-start(bf16[2,5,192,512]{3,2,1,0:T(8,128)(2,1)} %get-tuple-element.275), channel_id=1, source_target_pairs={{0,8},{8,0},{16,24},{24,16},{1,9},{9,1},{17,25},{25,17},{2,10},{10... | collective-permute-start | bytes 5898248 | tf_op jit(solution)/shard_map/ppermute | solution.py:49
  447.9 62.3 %collective-permute-start.47 = (bf16[2,5,192,512]{3,2,1,0:T(8,128)(2,1)}, bf16[2,5,192,512]{3,2,1,0:T(8,128)(2,1)}, u32[]{:S(2)}, u32[]{:S(2)}) collective-permute-start(bf16[2,5,192,512]{3,2,1,0:T(8,128)(2,1)} %get-tuple-element.276), channel_id=1, source_target_pairs={{0,16},{8,24},{16,0},{24,8},{1,17},{9,25},{17,1},{25,9},{2,18},{10... | collective-permute-start | bytes 5898248 | tf_op jit(solution)/shard_map/ppermute | solution.py:49
  485.6 141.9 %all-gather.12.cloned.1.call-start = ((), (), s32[]{:S(2)}) async-start(), calls=%async_computation.8 | async-start | bytes 3932160 | tf_op jit(solution)/shard_map/all_gather | solution.py:1103
  510.2 204.3 %reduce-scatter.10.cloned.1.call-start = ((), (), s32[]{:S(2)}) async-start(), calls=%async_computation.9 | async-start | bytes 3932160
  520.4 107.1 %collective-permute-start.49 = (bf16[3,5,192,512]{3,2,1,0:T(8,128)(2,1)}, bf16[3,5,192,512]{3,2,1,0:T(8,128)(2,1)}, u32[]{:S(2)}, u32[]{:S(2)}) collective-permute-start(bf16[3,5,192,512]{3,2,1,0:T(8,128)(2,1)} %add_convert_fusion.5), channel_id=1, source_target_pairs={{0,16},{8,24},{16,0},{24,8},{1,17},{9,25},{17,1},{25,9},{2,18},{10... | collective-permute-start | bytes 8847368 | tf_op jit(solution)/shard_map/ppermute | solution.py:49
  521.4 106.1 %collective-permute-start.50 = (bf16[3,5,192,512]{3,2,1,0:T(8,128)(2,1)}, bf16[3,5,192,512]{3,2,1,0:T(8,128)(2,1)}, u32[]{:S(2)}, u32[]{:S(2)}) collective-permute-start(bf16[3,5,192,512]{3,2,1,0:T(8,128)(2,1)} %add_convert_fusion.4), channel_id=1, source_target_pairs={{0,8},{8,0},{16,24},{24,16},{1,9},{9,1},{17,25},{25,17},{2,10},{10... | collective-permute-start | bytes 8847368 | tf_op jit(solution)/shard_map/ppermute | solution.py:49
  526.9 100.6 %collective-permute-start.51 = (bf16[2,5,192,512]{3,2,1,0:T(8,128)(2,1)}, bf16[2,5,192,512]{3,2,1,0:T(8,128)(2,1)}, u32[]{:S(2)}, u32[]{:S(2)}) collective-permute-start(bf16[2,5,192,512]{3,2,1,0:T(8,128)(2,1)} %get-tuple-element.305), channel_id=1, source_target_pairs={{0,8},{8,0},{16,24},{24,16},{1,9},{9,1},{17,25},{25,17},{2,10},{10... | collective-permute-start | bytes 5898248 | tf_op jit(solution)/shard_map/ppermute | solution.py:49
  527.9 99.6 %collective-permute-start.52 = (bf16[2,5,192,512]{3,2,1,0:T(8,128)(2,1)}, bf16[2,5,192,512]{3,2,1,0:T(8,128)(2,1)}, u32[]{:S(2)}, u32[]{:S(2)}) collective-permute-start(bf16[2,5,192,512]{3,2,1,0:T(8,128)(2,1)} %get-tuple-element.306), channel_id=1, source_target_pairs={{0,16},{8,24},{16,0},{24,8},{1,17},{9,25},{17,1},{25,9},{2,18},{10... | collective-permute-start | bytes 5898248 | tf_op jit(solution)/shard_map/ppermute | solution.py:49
  531.8 213.9 %reduce-scatter.12.cloned.1.call-start = ((), (), s32[]{:S(2)}) async-start(), calls=%async_computation.10 | async-start | bytes 3932160
  689.5 31.3 %collective-permute-start.63 = (bf16[3,5,192,512]{3,2,1,0:T(8,128)(2,1)}, bf16[3,5,192,512]{3,2,1,0:T(8,128)(2,1)}, u32[]{:S(2)}, u32[]{:S(2)}) collective-permute-start(bf16[3,5,192,512]{3,2,1,0:T(8,128)(2,1)} %add_convert_fusion.2), channel_id=1, source_target_pairs={{0,4},{4,0},{1,5},{5,1},{2,6},{6,2},{3,7},{7,3},{8,12},{12,8},{9,1... | collective-permute-start | bytes 8847368 | tf_op jit(solution)/shard_map/ppermute | solution.py:49
  (141 other events, 1950.5 us)
Sparse Core Ops, SparseCore 0:
  13.6 65.9 all-gather.5
  98.3 65.5 all-gather.7
  224.8 63.2 all-gather.9
  393.0 64.2 reduce-scatter.7
  510.3 60.7 all-gather.11
  573.8 58.8 reduce-scatter.9
  687.5 58.1 reduce-scatter.11

commit v5 on v4

--- a/solution.py
+++ b/solution.py
@@ -719,21 +719,22 @@
     return [found[n] for n in range(parts)]
 
 
-def combine_kernel(ranks, rows_in, out, *, experts):
-    count = out.shape[0]
+def combine_kernel(ranks, rows_in, out, *, experts, turned):
+    count = ranks.shape[1]
     slot = lax.broadcasted_iota(i32, (count, SLOTS), 1)
     pick = jnp.concatenate(
         [(ranks[0, :, e : e + 1] == slot).astype(bf16) for e in range(experts)], axis=1
     )
-    out[...] = dot(pick, rows_in[0]).astype(bf16)
-
-
-def combine(ranks, slot_rows, g):
+    total = dot(pick, rows_in[0])
+    out[...] = (total.T if turned else total).astype(bf16)
+
+
+def combine(ranks, slot_rows, g, turned):
     groups, rows, columns = ranks.shape
     experts = slot_rows.shape[1]
     block = min(256, rows)
     return pl.pallas_call(
-        functools.partial(combine_kernel, experts=experts),
+        functools.partial(combine_kernel, experts=experts, turned=turned),
         name="combine",
         grid=(rows // block,),
         in_specs=[
@@ -742,8 +743,12 @@
                 (1, experts * SLOTS, D), lambda i: (g, 0, 0), pipeline_mode=pl.Buffered(1)
             ),
         ],
-        out_specs=pl.BlockSpec((block, D), lambda i: (i, 0)),
-        out_shape=jax.ShapeDtypeStruct((rows, D), bf16),
+        out_specs=(
+            pl.BlockSpec((D, block), lambda i: (0, i))
+            if turned
+            else pl.BlockSpec((block, D), lambda i: (i, 0))
+        ),
+        out_shape=jax.ShapeDtypeStruct((D, rows) if turned else (rows, D), bf16),
         compiler_params=pltpu.CompilerParams(vmem_limit_bytes=VMEM_LIMIT),
     )(ranks, slot_rows.reshape(groups, experts * SLOTS, D))
 
@@ -908,10 +913,10 @@
 
     own_all = lax.all_gather(ancestry[:, 0], row_axes, axis=0, tiled=True)
     project_part = jnp.concatenate([w_query, w_key, w_value], axis=1)
-    own_all, project_part = tie(own_all, project_part)
     levels_here = range(len(chip_bits(chips)))
-    project_parts = [project_part]
-    for level in levels_here:
+    project_parts = shared_level([project_part], 0)
+    own_all, project_parts = tie(own_all, project_parts)
+    for level in levels_here[1:]:
         project_parts = shared_level(project_parts, level)
 
     stacked = jnp.stack([m.transpose(1, 0, 2) for m in (w_gate, w_up, w_down)])
@@ -1029,14 +1034,14 @@
         listed(weights_held, chips),
     )
 
-    def combine_groups(slot_rows):
+    def combine_groups(slot_rows, turned):
         if share == 1:
-            return combine(rank_columns, slot_rows, 0)
-        received = swap_core(combine(rank_columns, slot_rows, 1))
-        own = combine(rank_columns, slot_rows, 0)
+            return combine(rank_columns, slot_rows, 0, turned)
+        received = swap_core(combine(rank_columns, slot_rows, 1, turned))
+        own = combine(rank_columns, slot_rows, 0, turned)
         return (own.astype(f32) + received.astype(f32)).astype(bf16)
 
-    token_sum = combine_groups(slot_token_grads)
+    token_sum = combine_groups(slot_token_grads, False)
     token_grads = lax.psum_scatter(token_sum, "col", scatter_dimension=0, tiled=True)
     pair_other = swap_core(pair_rows[1, :experts]) if share == 2 else None
     pair_columns = in_core_order(pair_rows[0, :experts], pair_other, core)
@@ -1044,7 +1049,7 @@
     pair_grad = column_rows(pair_columns)
     picked_grad = gates[0] * (pair_grad - jnp.sum(gates[0] * pair_grad, axis=0, keepdims=True))
     logit_grad = picked_grad.astype(bf16)
-    mix_sum = combine_groups(weighted_out)
+    mix_sum = combine_groups(weighted_out, True)
 
     levels = reduce_levels(chips, share)
     first = [[m for m in moves if m[1]] for moves in levels[0]]
@@ -1142,7 +1147,7 @@
         )
         for head in range(own_heads)
     ]
-    mix_slice = lax.psum_scatter(mix_sum, "col", scatter_dimension=1, tiled=True).astype(f32)
+    mix_slice = lax.psum_scatter(mix_sum, "col", scatter_dimension=0, tiled=True).astype(f32).T
     feature_start = column * width
     x_middle_slice = lax.dynamic_slice_in_dim(x_middle, feature_start, width, 1)
     result = (x_middle_slice + branch_scale * mix_slice).astype(bf16)

time: 770 us -> 764 us (level)
  waiting for transfers between devices: 302 us -> 289 us
    unnamed x9 -> x8, waiting for transfers between devices: 14.5 us -> 3.74 us
  transfers between devices with their start and end apart: 84 -> 84, of which waited for: 45 -> 41; matrix products, arithmetic and copies ran while one was open for 17% -> 18% of each run, Pallas kernels for 17% -> 17%
where the time goes in v5:
time: 764 us; the launch traced here: 753 us
  waiting for transfers between devices  289 us (38%)
  Pallas kernels  208 us (27%)
  other arithmetic  92.6 us (12%)
  starting transfers between devices  69.9 us (9%)
  local copies, waits for them, and re-layouts  50.1 us (7%)
  matrix products  18.6 us (2%)
  between operations  15.9 us (2%)
  blocking collectives  9.03 us (1%)
    ppermute x53, waiting for transfers between devices, swap(): return lax.ppermute(values, axis, [(i, i ^ bit) for i in range(size)])  247 us
    pallas_call x1, Pallas kernels, run_experts(): pl.pallas_call(functools.partial(expert_kernel, parts=parts, groups=group...  57.1 us
    ppermute x53, starting transfers between devices, swap(): return lax.ppermute(values, axis, [(i, i ^ bit) for i in range(size)])  35 us
    pallas_call x4, Pallas kernels, combine(): pl.pallas_call(functools.partial(combine_kernel, experts=experts, turned=...  33 us
    pallas_call x1, Pallas kernels, attend_backward(): pl.pallas_call(kernel, name='attend_backward', grid_spec=pltpu.PrefetchSc...  30.9 us
    pallas_call x1, Pallas kernels, expert_grads(): pl.pallas_call(functools.partial(expert_grad_kernel, pieces=[(n, begin) f...  23.4 us
    pallas_call x1, Pallas kernels, attend_forward(): pl.pallas_call(kernel, name='attend_forward', grid_spec=pltpu.PrefetchSca...  21 us
    ppermute x15, starting transfers between devices, column_shifts(): lax.ppermute(values_for((me + d) % size), 'col', [(i, (i + d) % size) for...  20.7 us
  transfers between devices with their start and end apart: 84, of which 41 were waited for; matrix products, arithmetic and copies ran while one was open for 18% of the time, Pallas kernels for 17%

profile of v5, /device:TPU:0, one launch (start us, length us, event | category | flops | bytes accessed | tf_op | source)
XLA Modules:
  0.0 753.5 jit_solution(1894585199697074237)
XLA Ops:
  18.5 9.0 %all-gather = s32[8192,1]{0,1:T(1,128)S(1)} all-gather(s32[1024,1]{0,1:T(1,128)S(1)} %slice-done.1), channel_id=2, replica_groups=mesh['chip'=4,'core'=2,'col'=4] {'chip','core'}, dimensions={0}, use_global_device_ids=true | all-gather | bytes 36864 | tf_op jit(solution)/shard_map/all_gather | solution.py:914
  54.0 8.5 %slot_ranks.1.ranks = s32[2,8,1024]{2,1,0:T(8,128)} custom-call(s32[1]{0:T(128)} %bitcast.8.first, s32[2,8,1024]{2,1,0:T(8,128)} %copy.160.route_rows, s32[2,8,1024]{2,1,0:T(8,128)} %copy.161.priority_rows, s32[2,1024,8]{2,1,0:T(8,128)} %copy-done.6, s32[2,1024,8]{2,1,0:T(8,128)} %get-tuple-element.461.priority_columns), custom_call_target="tpu_custom_call" | custom-call | tf_op jit(solution)/shard_map/slot_ranks/pallas_call | solution.py:564
  72.3 7.3 all-gather.6.cloned.1.call-done.x
  96.9 5.8 collective-permute-done.9.rest_8_
  115.6 8.5 %collective-permute-done.19.rest_2_ = bf16[192,1576]{1,0:T(8,128)(2,1)S(1)} collective-permute-done((bf16[192,1576]{1,0:T(8,128)(2,1)}, bf16[192,1576]{1,0:T(8,128)(2,1)S(1)}, u32[]{:S(2)}, u32[]{:S(2)}) %collective-permute-start.19) | collective-permute-done | bytes 605216 | tf_op jit(solution)/shard_map/ppermute | solution.py:152
  124.1 6.8 collective-permute-done.20.rest_3_
  158.5 21.0 %attend_forward.1 = (f32[2,3,64,1024]{3,2,1,0:T(8,128)}, bf16[2,3,64,1024]{3,2,1,0:T(8,128)(2,1)}, f32[2,3,1,1024]{3,2,1,0:T(1,128)}) custom-call(s32[8]{0:T(128)} %stack.227.offsets, s32[4]{0:T(128)} %get-tuple-element.435.starts, s32[64]{0:T(128)} %select_n.257.codes, bf16[2,3,64,1024]{3,2,1,0:T(8,128)(2,1)} %maximum_bitcast_fusion.query, ...), custom_call_target="tpu_custom_call" | custom-call | tf_op jit(solution)/shard_map/attend_forward/pallas_call | solution.py:419
  179.5 36.4 %collective-permute-done.27.rest_10_ = bf16[3,5,192,512]{3,2,1,0:T(8,128)(2,1)S(1)} collective-permute-done((bf16[3,5,192,512]{3,2,1,0:T(8,128)(2,1)}, bf16[3,5,192,512]{3,2,1,0:T(8,128)(2,1)S(1)}, u32[]{:S(2)}, u32[]{:S(2)}) %collective-permute-start.27) | collective-permute-done | bytes 2949152 | tf_op jit(solution)/shard_map/ppermute | solution.py:49
  229.2 5.9 place_rows.3.matrix
  235.0 53.2 %collective-permute-done.30.rest_12_ = bf16[3,5,192,512]{3,2,1,0:T(8,128)(2,1)} collective-permute-done((bf16[3,5,192,512]{3,2,1,0:T(8,128)(2,1)}, bf16[3,5,192,512]{3,2,1,0:T(8,128)(2,1)}, u32[]{:S(2)}, u32[]{:S(2)}) %collective-permute-start.30) | collective-permute-done | bytes 2949152 | tf_op jit(solution)/shard_map/ppermute | solution.py:49
  288.9 11.8 %project_out.1 = (f32[1024,1536]{1,0:T(8,128)}, bf16[1024,1536]{1,0:T(8,128)(2,1)}, f32[1024,1]{1,0:T(8,128)}) custom-call(bf16[1536,1024]{1,0:T(8,128)(2,1)} %all-gather.10.cloned.1.call-done.mixed, bf16[1024,1536]{1,0:T(8,128)(2,1)} %all-gather.6.cloned.1.call-done.x, f32[1,1536]{1,0:T(1,128)} %get-tuple-element.480.gain, bf16[1536,1576]{1,0:T(8,128)(2,1)} %place_rows.3.matrix), custom_call_target="tpu_custom_call" | custom-call | tf_op jit(solution)/shard_map/project_out/pallas_call | solution.py:769
  312.1 57.1 %experts.1 = (bf16[2,5,256,1536]{3,2,1,0:T(8,128)(2,1)}, bf16[2,5,256,1536]{3,2,1,0:T(8,128)(2,1)}, bf16[5,512,1536]{2,1,0:T(8,128)(2,1)}, bf16[5,512,1536]{2,1,...) custom-call(s32[8]{0:T(128)} %stack.258.offsets, s32[1]{0:T(128)} %bitcast.8.first, ...), custom_call_target="tpu_custom_call" | custom-call | tf_op jit(solution)/shard_map/experts/pallas_call | solution.py:636
  369.2 8.2 %combine.5 = bf16[1024,1536]{1,0:T(8,128)(2,1)} custom-call(s32[2,1024,8]{2,1,0:T(8,128)} %bitcast.246, bf16[2,1280,1536]{2,1,0:T(8,128)(2,1)} %bitcast.244), custom_call_target="tpu_custom_call" | custom-call | tf_op jit(solution)/shard_map/combine/pallas_call | solution.py:736
  377.6 8.0 %combine.4 = bf16[1024,1536]{1,0:T(8,128)(2,1)} custom-call(s32[2,1024,8]{2,1,0:T(8,128)} %bitcast.247, bf16[2,1280,1536]{2,1,0:T(8,128)(2,1)} %bitcast.245), custom_call_target="tpu_custom_call" | custom-call | tf_op jit(solution)/shard_map/combine/pallas_call | solution.py:736
  390.0 8.4 %combine.7 = bf16[1536,1024]{1,0:T(8,128)(2,1)} custom-call(s32[2,1024,8]{2,1,0:T(8,128)} %bitcast.248, bf16[2,1280,1536]{2,1,0:T(8,128)(2,1)} %bitcast.242), custom_call_target="tpu_custom_call" | custom-call | tf_op jit(solution)/shard_map/combine/pallas_call | solution.py:736
  410.2 8.3 %combine.6 = bf16[1536,1024]{1,0:T(8,128)(2,1)} custom-call(s32[2,1024,8]{2,1,0:T(8,128)} %bitcast.249, bf16[2,1280,1536]{2,1,0:T(8,128)(2,1)} %bitcast.243), custom_call_target="tpu_custom_call" | custom-call | tf_op jit(solution)/shard_map/combine/pallas_call | solution.py:736
  418.5 23.4 %expert_grads.1 = (bf16[3,5,192,512]{3,2,1,0:T(8,128)(2,1)}, bf16[3,5,192,512]{3,2,1,0:T(8,128)(2,1)}, bf16[1,5,192,512]{3,2,1,0:T(8,128)(2,1)}, bf16[2,5,192,51...) custom-call(s32[8]{0:T(128)} %stack.258.offsets, ...), custom_call_target="tpu_custom_call" | custom-call | tf_op jit(solution)/shard_map/expert_grads/pallas_call | solution.py:696
  455.5 11.5 %collective-permute-done.44 = bf16[1,5,192,512]{3,2,1,0:T(8,128)(2,1)} collective-permute-done((bf16[1,5,192,512]{3,2,1,0:T(8,128)(2,1)}, bf16[1,5,192,512]{3,2,1,0:T(8,128)(2,1)}, u32[]{:S(2)}, u32[]{:S(2)}) %collective-permute-start.44) | collective-permute-done | bytes 983072 | tf_op jit(solution)/shard_map/ppermute | solution.py:49
  482.8 24.5 %collective-permute-done.46 = bf16[2,5,192,512]{3,2,1,0:T(8,128)(2,1)} collective-permute-done((bf16[2,5,192,512]{3,2,1,0:T(8,128)(2,1)}, bf16[2,5,192,512]{3,2,1,0:T(8,128)(2,1)}, u32[]{:S(2)}, u32[]{:S(2)}) %collective-permute-start.46) | collective-permute-done | bytes 1966112 | tf_op jit(solution)/shard_map/ppermute | solution.py:49
  526.3 30.9 %attend_backward.1 = (f32[2,3,64,1024]{3,2,1,0:T(8,128)}, bf16[1024,128]{1,0:T(8,128)(2,1)}, bf16[1024,128]{1,0:T(8,128)(2,1)}, bf16[1024,128]{1,0:T(8,128)(2,1)...) custom-call(s32[8]{0:T(128)} %stack.227.offsets, ...), custom_call_target="tpu_custom_call" | custom-call | tf_op jit(solution)/shard_map/attend_backward/pallas_call | solution.py:468
  557.2 68.7 %collective-permute-done.51 = bf16[2,5,192,512]{3,2,1,0:T(8,128)(2,1)} collective-permute-done((bf16[2,5,192,512]{3,2,1,0:T(8,128)(2,1)}, bf16[2,5,192,512]{3,2,1,0:T(8,128)(2,1)}, u32[]{:S(2)}, u32[]{:S(2)}) %collective-permute-start.51) | collective-permute-done | bytes 1966112 | tf_op jit(solution)/shard_map/ppermute | solution.py:49
  655.3 13.1 %matrix_grads.1 = (bf16[4,192,1064]{2,1,0:T(8,128)(2,1)}, bf16[4,192,1064]{2,1,0:T(8,128)(2,1)}, f32[1536,1]{1,0:T(8,128)}) custom-call(s32[8]{0:T(128)} %stack.244.offsets, bf16[1024,1536]{1,0:T(8,128)(2,1)} %copy-done.2, bf16[640,1024]{1,0:T(8,128)(2,1)} %copy-done.4, bf16[1024,1536]{1,0:T(8,128)(2,1)} %all-gather.12.cloned.1.call-done.branch_grad, ...), custom_call_target="tpu_custom_call" | custom-call | tf_op jit(solution)/shard_map/matrix_grads/pallas_call | solution.py:817
  675.5 5.6 add_convert_fusion.2
  697.6 6.5 copy.173
  (479 shorter events, 288.9 us)
Async XLA Ops:
  7.2 72.4 %all-gather.6.cloned.1.call-start = ((), (), s32[]{:S(2)}) async-start(), calls=%async_computation.4 | async-start | bytes 3932160 | tf_op jit(solution)/shard_map/all_gather | solution.py:910
  13.5 166.0 %all-gather.8.cloned.1.call-start = ((), (), s32[]{:S(2)}) async-start(), calls=%async_computation.5 | async-start | bytes 3932160 | tf_op jit(solution)/shard_map/all_gather | solution.py:959
  37.2 65.6 %collective-permute-start.9 = (bf16[3,5,192,512]{3,2,1,0:T(8,128)(2,1)}, bf16[3,5,192,512]{3,2,1,0:T(8,128)(2,1)}, u32[]{:S(2)}, u32[]{:S(2)}) collective-permute-start(bf16[3,5,192,512]{3,2,1,0:T(8,128)(2,1)} %get-tuple-element.256.rest_6_), channel_id=1, source_target_pairs={{0,8},{8,0},{16,24},{24,16},{1,9},{9,1},{17,25},{25,17},{2,10},{10... | collective-permute-start | bytes 8847368 | tf_op jit(solution)/shard_map/ppermute | solution.py:49
  37.7 67.1 %collective-permute-start.10 = (bf16[3,5,192,512]{3,2,1,0:T(8,128)(2,1)}, bf16[3,5,192,512]{3,2,1,0:T(8,128)(2,1)}, u32[]{:S(2)}, u32[]{:S(2)}) collective-permute-start(bf16[3,5,192,512]{3,2,1,0:T(8,128)(2,1)} %collective-permute-done.3.rest_7_), channel_id=1, source_target_pairs={{0,16},{8,24},{16,0},{24,8},{1,17},{9,25},{17,1},{25,9},{2,18},{10... | collective-permute-start | bytes 8847368 | tf_op jit(solution)/shard_map/ppermute | solution.py:49
  96.9 192.0 %all-gather.10.cloned.1.call-start = ((), (), s32[]{:S(2)}) async-start(), calls=%async_computation.6 | async-start | bytes 3932160 | tf_op jit(solution)/shard_map/all_gather | solution.py:1011
  151.3 64.7 %collective-permute-start.27 = (bf16[3,5,192,512]{3,2,1,0:T(8,128)(2,1)}, bf16[3,5,192,512]{3,2,1,0:T(8,128)(2,1)S(1)}, u32[]{:S(2)}, u32[]{:S(2)}) collective-permute-start(bf16[3,5,192,512]{3,2,1,0:T(8,128)(2,1)} %get-tuple-element.256.rest_6_), channel_id=1, source_target_pairs={{0,16},{8,24},{16,0},{24,8},{1,17},{9,25},{17,1},{25,9},{2,18},{10... | collective-permute-start | bytes 8847368 | tf_op jit(solution)/shard_map/ppermute | solution.py:49
  152.1 64.7 %collective-permute-start.28 = (bf16[3,5,192,512]{3,2,1,0:T(8,128)(2,1)}, bf16[3,5,192,512]{3,2,1,0:T(8,128)(2,1)}, u32[]{:S(2)}, u32[]{:S(2)}) collective-permute-start(bf16[3,5,192,512]{3,2,1,0:T(8,128)(2,1)} %collective-permute-done.3.rest_7_), channel_id=1, source_target_pairs={{0,8},{8,0},{16,24},{24,16},{1,9},{9,1},{17,25},{25,17},{2,10},{10... | collective-permute-start | bytes 8847368 | tf_op jit(solution)/shard_map/ppermute | solution.py:49
  221.8 246.9 %reduce-scatter.6.cloned.1.call-start = ((), (), s32[]{:S(2)}) async-start(), calls=%async_computation.7 | async-start | bytes 3932160 | tf_op jit(solution)/shard_map/reduce_scatter | solution.py:1045
  221.9 66.3 %collective-permute-start.30 = (bf16[3,5,192,512]{3,2,1,0:T(8,128)(2,1)}, bf16[3,5,192,512]{3,2,1,0:T(8,128)(2,1)}, u32[]{:S(2)}, u32[]{:S(2)}) collective-permute-start(bf16[3,5,192,512]{3,2,1,0:T(8,128)(2,1)} %collective-permute-done.9.rest_8_), channel_id=1, source_target_pairs={{0,16},{8,24},{16,0},{24,8},{1,17},{9,25},{17,1},{25,9},{2,18},{10... | collective-permute-start | bytes 8847368 | tf_op jit(solution)/shard_map/ppermute | solution.py:49
  222.9 66.0 %collective-permute-start.31 = (bf16[3,5,192,512]{3,2,1,0:T(8,128)(2,1)}, bf16[3,5,192,512]{3,2,1,0:T(8,128)(2,1)}, u32[]{:S(2)}, u32[]{:S(2)}) collective-permute-start(bf16[3,5,192,512]{3,2,1,0:T(8,128)(2,1)} %collective-permute-done.10.rest_11_), channel_id=1, source_target_pairs={{0,8},{8,0},{16,24},{24,16},{1,9},{9,1},{17,25},{25,17},{2,10},{10... | collective-permute-start | bytes 8847368 | tf_op jit(solution)/shard_map/ppermute | solution.py:49
  398.4 51.9 %collective-permute-start.39 = (bf16[1536,1024]{1,0:T(8,128)(2,1)}, bf16[1536,1024]{1,0:T(8,128)(2,1)}, u32[]{:S(2)}, u32[]{:S(2)}) collective-permute-start(bf16[1536,1024]{1,0:T(8,128)(2,1)} %combine.7), channel_id=1, source_target_pairs={{0,4},{4,0},{1,5},{5,1},{2,6},{6,2},{3,7},{7,3},{8,12},{12,8},{9,1... | collective-permute-start | bytes 9437192 | tf_op jit(solution)/shard_map/ppermute | solution.py:49
  403.2 40.5 %collective-permute-start.41 = (f32[10,1024]{1,0:T(8,128)S(1)}, f32[10,1024]{1,0:T(8,128)}, u32[]{:S(2)}, u32[]{:S(2)}) collective-permute-start(f32[10,1024]{1,0:T(8,128)S(1)} %reshape.402), channel_id=1, source_target_pairs={{0,1},{1,2},{2,3},{3,0},{4,5},{5,6},{6,7},{7,4},{8,9},{9,10},{10,1... | collective-permute-start | bytes 122888 | tf_op jit(solution)/shard_map/ppermute | solution.py:188
  404.5 41.4 %collective-permute-start.42 = (f32[10,1024]{1,0:T(8,128)S(1)}, f32[10,1024]{1,0:T(8,128)}, u32[]{:S(2)}, u32[]{:S(2)}) collective-permute-start(f32[10,1024]{1,0:T(8,128)S(1)} %reshape.402), channel_id=1, source_target_pairs={{0,2},{1,3},{2,0},{3,1},{4,6},{5,7},{6,4},{7,5},{8,10},{9,11},{10,... | collective-permute-start | bytes 122888 | tf_op jit(solution)/shard_map/ppermute | solution.py:188
  406.1 42.0 %collective-permute-start.43 = (f32[10,1024]{1,0:T(8,128)S(1)}, f32[10,1024]{1,0:T(8,128)}, u32[]{:S(2)}, u32[]{:S(2)}) collective-permute-start(f32[10,1024]{1,0:T(8,128)S(1)} %reshape.402), channel_id=1, source_target_pairs={{0,3},{1,0},{2,1},{3,2},{4,7},{5,4},{6,5},{7,6},{8,11},{9,8},{10,9... | collective-permute-start | bytes 122888 | tf_op jit(solution)/shard_map/ppermute | solution.py:188
  446.0 61.4 %collective-permute-start.46 = (bf16[2,5,192,512]{3,2,1,0:T(8,128)(2,1)}, bf16[2,5,192,512]{3,2,1,0:T(8,128)(2,1)}, u32[]{:S(2)}, u32[]{:S(2)}) collective-permute-start(bf16[2,5,192,512]{3,2,1,0:T(8,128)(2,1)} %get-tuple-element.277), channel_id=1, source_target_pairs={{0,8},{8,0},{16,24},{24,16},{1,9},{9,1},{17,25},{25,17},{2,10},{10... | collective-permute-start | bytes 5898248 | tf_op jit(solution)/shard_map/ppermute | solution.py:49
  448.1 60.9 %collective-permute-start.47 = (bf16[2,5,192,512]{3,2,1,0:T(8,128)(2,1)}, bf16[2,5,192,512]{3,2,1,0:T(8,128)(2,1)}, u32[]{:S(2)}, u32[]{:S(2)}) collective-permute-start(bf16[2,5,192,512]{3,2,1,0:T(8,128)(2,1)} %get-tuple-element.278), channel_id=1, source_target_pairs={{0,16},{8,24},{16,0},{24,8},{1,17},{9,25},{17,1},{25,9},{2,18},{10... | collective-permute-start | bytes 5898248 | tf_op jit(solution)/shard_map/ppermute | solution.py:49
  482.8 143.1 %all-gather.12.cloned.1.call-start = ((), (), s32[]{:S(2)}) async-start(), calls=%async_computation.9 | async-start | bytes 3932160 | tf_op jit(solution)/shard_map/all_gather | solution.py:1108
  509.0 207.6 %reduce-scatter.8.cloned.1.call-start = ((), (), s32[]{:S(2)}) async-start(), calls=%async_computation.8 | async-start | bytes 3932160 | tf_op jit(solution)/shard_map/reduce_scatter | solution.py:1150
  518.9 107.0 %collective-permute-start.49 = (bf16[3,5,192,512]{3,2,1,0:T(8,128)(2,1)}, bf16[3,5,192,512]{3,2,1,0:T(8,128)(2,1)}, u32[]{:S(2)}, u32[]{:S(2)}) collective-permute-start(bf16[3,5,192,512]{3,2,1,0:T(8,128)(2,1)} %add_convert_fusion.5), channel_id=1, source_target_pairs={{0,16},{8,24},{16,0},{24,8},{1,17},{9,25},{17,1},{25,9},{2,18},{10... | collective-permute-start | bytes 8847368 | tf_op jit(solution)/shard_map/ppermute | solution.py:49
  519.9 106.0 %collective-permute-start.50 = (bf16[3,5,192,512]{3,2,1,0:T(8,128)(2,1)}, bf16[3,5,192,512]{3,2,1,0:T(8,128)(2,1)}, u32[]{:S(2)}, u32[]{:S(2)}) collective-permute-start(bf16[3,5,192,512]{3,2,1,0:T(8,128)(2,1)} %add_convert_fusion.4), channel_id=1, source_target_pairs={{0,8},{8,0},{16,24},{24,16},{1,9},{9,1},{17,25},{25,17},{2,10},{10... | collective-permute-start | bytes 8847368 | tf_op jit(solution)/shard_map/ppermute | solution.py:49
  521.4 104.5 %collective-permute-start.51 = (bf16[2,5,192,512]{3,2,1,0:T(8,128)(2,1)}, bf16[2,5,192,512]{3,2,1,0:T(8,128)(2,1)}, u32[]{:S(2)}, u32[]{:S(2)}) collective-permute-start(bf16[2,5,192,512]{3,2,1,0:T(8,128)(2,1)} %get-tuple-element.307), channel_id=1, source_target_pairs={{0,8},{8,0},{16,24},{24,16},{1,9},{9,1},{17,25},{25,17},{2,10},{10... | collective-permute-start | bytes 5898248 | tf_op jit(solution)/shard_map/ppermute | solution.py:49
  522.4 103.5 %collective-permute-start.52 = (bf16[2,5,192,512]{3,2,1,0:T(8,128)(2,1)}, bf16[2,5,192,512]{3,2,1,0:T(8,128)(2,1)}, u32[]{:S(2)}, u32[]{:S(2)}) collective-permute-start(bf16[2,5,192,512]{3,2,1,0:T(8,128)(2,1)} %get-tuple-element.308), channel_id=1, source_target_pairs={{0,16},{8,24},{16,0},{24,8},{1,17},{9,25},{17,1},{25,9},{2,18},{10... | collective-permute-start | bytes 5898248 | tf_op jit(solution)/shard_map/ppermute | solution.py:49
  523.5 215.7 %reduce-scatter.10.cloned.1.call-start = ((), (), s32[]{:S(2)}) async-start(), calls=%async_computation.10 | async-start | bytes 3932160
  683.3 41.6 %collective-permute-start.63 = (bf16[3,5,192,512]{3,2,1,0:T(8,128)(2,1)}, bf16[3,5,192,512]{3,2,1,0:T(8,128)(2,1)}, u32[]{:S(2)}, u32[]{:S(2)}) collective-permute-start(bf16[3,5,192,512]{3,2,1,0:T(8,128)(2,1)} %add_convert_fusion.2), channel_id=1, source_target_pairs={{0,4},{4,0},{1,5},{5,1},{2,6},{6,2},{3,7},{7,3},{8,12},{12,8},{9,1... | collective-permute-start | bytes 8847368 | tf_op jit(solution)/shard_map/ppermute | solution.py:49
  (134 other events, 1900.3 us)
Sparse Core Ops, SparseCore 0:
  13.7 65.8 all-gather.5
  97.0 63.2 all-gather.7
  222.0 62.7 all-gather.9
  390.1 63.6 reduce-scatter.5
  509.1 60.6 all-gather.11
  572.6 58.8 reduce-scatter.7
  681.3 57.7 reduce-scatter.9

commit v6 on v5

--- a/solution.py
+++ b/solution.py
@@ -732,7 +732,7 @@
 def combine(ranks, slot_rows, g, turned):
     groups, rows, columns = ranks.shape
     experts = slot_rows.shape[1]
-    block = min(256, rows)
+    block = min(512, rows)
     return pl.pallas_call(
         functools.partial(combine_kernel, experts=experts, turned=turned),
         name="combine",
@@ -764,7 +764,7 @@
 
 def project_out(mixed, x, gain, matrix):
     rows = x.shape[0]
-    block = min(256, rows)
+    block = min(512, rows)
     tall = pl.BlockSpec((block, D), lambda i: (i, 0))
     return pl.pallas_call(
         project_kernel,

time: 764 us -> 763 us (level)
  no operation moved by 1% of the time
where the time goes in v6:
time: 763 us; the launch traced here: 753 us
  waiting for transfers between devices  290 us (38%)
  Pallas kernels  207 us (27%)
  other arithmetic  92.7 us (12%)
  starting transfers between devices  70 us (9%)
  local copies, waits for them, and re-layouts  50.1 us (7%)
  matrix products  18.6 us (2%)
  between operations  16.1 us (2%)
  blocking collectives  9.03 us (1%)
    ppermute x53, waiting for transfers between devices, swap(): return lax.ppermute(values, axis, [(i, i ^ bit) for i in range(size)])  248 us
    pallas_call x1, Pallas kernels, run_experts(): pl.pallas_call(functools.partial(expert_kernel, parts=parts, groups=group...  57.2 us
    ppermute x53, starting transfers between devices, swap(): return lax.ppermute(values, axis, [(i, i ^ bit) for i in range(size)])  34.7 us
    pallas_call x4, Pallas kernels, combine(): pl.pallas_call(functools.partial(combine_kernel, experts=experts, turned=...  32.2 us
    pallas_call x1, Pallas kernels, attend_backward(): pl.pallas_call(kernel, name='attend_backward', grid_spec=pltpu.PrefetchSc...  30.5 us
    pallas_call x1, Pallas kernels, expert_grads(): pl.pallas_call(functools.partial(expert_grad_kernel, pieces=[(n, begin) f...  23.4 us
    pallas_call x1, Pallas kernels, attend_forward(): pl.pallas_call(kernel, name='attend_forward', grid_spec=pltpu.PrefetchSca...  21 us
    ppermute x15, starting transfers between devices, column_shifts(): lax.ppermute(values_for((me + d) % size), 'col', [(i, (i + d) % size) for...  21 us
  transfers between devices with their start and end apart: 84, of which 41 were waited for; matrix products, arithmetic and copies ran while one was open for 18% of the time, Pallas kernels for 17%

profile of v6, /device:TPU:0, one launch (start us, length us, event | category | flops | bytes accessed | tf_op | source)
XLA Modules:
  0.0 753.3 jit_solution(9395455884994921975)
XLA Ops:
  18.5 9.0 %all-gather = s32[8192,1]{0,1:T(1,128)S(1)} all-gather(s32[1024,1]{0,1:T(1,128)S(1)} %slice-done.1), channel_id=2, replica_groups=mesh['chip'=4,'core'=2,'col'=4] {'chip','core'}, dimensions={0}, use_global_device_ids=true | all-gather | bytes 36864 | tf_op jit(solution)/shard_map/all_gather | solution.py:914
  54.0 8.5 %slot_ranks.1.ranks = s32[2,8,1024]{2,1,0:T(8,128)} custom-call(s32[1]{0:T(128)} %bitcast.8.first, s32[2,8,1024]{2,1,0:T(8,128)} %copy.160.route_rows, s32[2,8,1024]{2,1,0:T(8,128)} %copy.161.priority_rows, s32[2,1024,8]{2,1,0:T(8,128)} %copy-done.6, s32[2,1024,8]{2,1,0:T(8,128)} %get-tuple-element.461.priority_columns), custom_call_target="tpu_custom_call" | custom-call | tf_op jit(solution)/shard_map/slot_ranks/pallas_call | solution.py:564
  72.3 7.3 all-gather.6.cloned.1.call-done.x
  96.9 5.8 collective-permute-done.9.rest_8_
  115.6 8.5 %collective-permute-done.19.rest_2_ = bf16[192,1576]{1,0:T(8,128)(2,1)S(1)} collective-permute-done((bf16[192,1576]{1,0:T(8,128)(2,1)}, bf16[192,1576]{1,0:T(8,128)(2,1)S(1)}, u32[]{:S(2)}, u32[]{:S(2)}) %collective-permute-start.19) | collective-permute-done | bytes 605216 | tf_op jit(solution)/shard_map/ppermute | solution.py:152
  124.1 6.8 collective-permute-done.20.rest_3_
  158.5 21.0 %attend_forward.1 = (f32[2,3,64,1024]{3,2,1,0:T(8,128)}, bf16[2,3,64,1024]{3,2,1,0:T(8,128)(2,1)}, f32[2,3,1,1024]{3,2,1,0:T(1,128)}) custom-call(s32[8]{0:T(128)} %stack.227.offsets, s32[4]{0:T(128)} %get-tuple-element.435.starts, s32[64]{0:T(128)} %select_n.257.codes, bf16[2,3,64,1024]{3,2,1,0:T(8,128)(2,1)} %maximum_bitcast_fusion.query, ...), custom_call_target="tpu_custom_call" | custom-call | tf_op jit(solution)/shard_map/attend_forward/pallas_call | solution.py:419
  179.5 36.4 %collective-permute-done.27.rest_10_ = bf16[3,5,192,512]{3,2,1,0:T(8,128)(2,1)S(1)} collective-permute-done((bf16[3,5,192,512]{3,2,1,0:T(8,128)(2,1)}, bf16[3,5,192,512]{3,2,1,0:T(8,128)(2,1)S(1)}, u32[]{:S(2)}, u32[]{:S(2)}) %collective-permute-start.27) | collective-permute-done | bytes 2949152 | tf_op jit(solution)/shard_map/ppermute | solution.py:49
  229.2 5.9 place_rows.3.matrix
  235.0 53.2 %collective-permute-done.30.rest_12_ = bf16[3,5,192,512]{3,2,1,0:T(8,128)(2,1)} collective-permute-done((bf16[3,5,192,512]{3,2,1,0:T(8,128)(2,1)}, bf16[3,5,192,512]{3,2,1,0:T(8,128)(2,1)}, u32[]{:S(2)}, u32[]{:S(2)}) %collective-permute-start.30) | collective-permute-done | bytes 2949152 | tf_op jit(solution)/shard_map/ppermute | solution.py:49
  288.9 11.5 %project_out.1 = (f32[1024,1536]{1,0:T(8,128)}, bf16[1024,1536]{1,0:T(8,128)(2,1)}, f32[1024,1]{1,0:T(8,128)}) custom-call(bf16[1536,1024]{1,0:T(8,128)(2,1)} %all-gather.10.cloned.1.call-done.mixed, bf16[1024,1536]{1,0:T(8,128)(2,1)} %all-gather.6.cloned.1.call-done.x, f32[1,1536]{1,0:T(1,128)} %get-tuple-element.480.gain, bf16[1536,1576]{1,0:T(8,128)(2,1)} %place_rows.3.matrix), custom_call_target="tpu_custom_call" | custom-call | tf_op jit(solution)/shard_map/project_out/pallas_call | solution.py:769
  311.9 57.2 %experts.1 = (bf16[2,5,256,1536]{3,2,1,0:T(8,128)(2,1)}, bf16[2,5,256,1536]{3,2,1,0:T(8,128)(2,1)}, bf16[5,512,1536]{2,1,0:T(8,128)(2,1)}, bf16[5,512,1536]{2,1,...) custom-call(s32[8]{0:T(128)} %stack.258.offsets, s32[1]{0:T(128)} %bitcast.8.first, ...), custom_call_target="tpu_custom_call" | custom-call | tf_op jit(solution)/shard_map/experts/pallas_call | solution.py:636
  369.1 7.9 %combine.5 = bf16[1024,1536]{1,0:T(8,128)(2,1)} custom-call(s32[2,1024,8]{2,1,0:T(8,128)} %bitcast.246, bf16[2,1280,1536]{2,1,0:T(8,128)(2,1)} %bitcast.244), custom_call_target="tpu_custom_call" | custom-call | tf_op jit(solution)/shard_map/combine/pallas_call | solution.py:736
  377.2 7.9 %combine.4 = bf16[1024,1536]{1,0:T(8,128)(2,1)} custom-call(s32[2,1024,8]{2,1,0:T(8,128)} %bitcast.247, bf16[2,1280,1536]{2,1,0:T(8,128)(2,1)} %bitcast.245), custom_call_target="tpu_custom_call" | custom-call | tf_op jit(solution)/shard_map/combine/pallas_call | solution.py:736
  389.4 8.4 %combine.7 = bf16[1536,1024]{1,0:T(8,128)(2,1)} custom-call(s32[2,1024,8]{2,1,0:T(8,128)} %bitcast.248, bf16[2,1280,1536]{2,1,0:T(8,128)(2,1)} %bitcast.242), custom_call_target="tpu_custom_call" | custom-call | tf_op jit(solution)/shard_map/combine/pallas_call | solution.py:736
  409.6 8.0 %combine.6 = bf16[1536,1024]{1,0:T(8,128)(2,1)} custom-call(s32[2,1024,8]{2,1,0:T(8,128)} %bitcast.249, bf16[2,1280,1536]{2,1,0:T(8,128)(2,1)} %bitcast.243), custom_call_target="tpu_custom_call" | custom-call | tf_op jit(solution)/shard_map/combine/pallas_call | solution.py:736
  417.7 23.4 %expert_grads.1 = (bf16[3,5,192,512]{3,2,1,0:T(8,128)(2,1)}, bf16[3,5,192,512]{3,2,1,0:T(8,128)(2,1)}, bf16[1,5,192,512]{3,2,1,0:T(8,128)(2,1)}, bf16[2,5,192,51...) custom-call(s32[8]{0:T(128)} %stack.258.offsets, ...), custom_call_target="tpu_custom_call" | custom-call | tf_op jit(solution)/shard_map/expert_grads/pallas_call | solution.py:696
  454.6 11.5 %collective-permute-done.44 = bf16[1,5,192,512]{3,2,1,0:T(8,128)(2,1)} collective-permute-done((bf16[1,5,192,512]{3,2,1,0:T(8,128)(2,1)}, bf16[1,5,192,512]{3,2,1,0:T(8,128)(2,1)}, u32[]{:S(2)}, u32[]{:S(2)}) %collective-permute-start.44) | collective-permute-done | bytes 983072 | tf_op jit(solution)/shard_map/ppermute | solution.py:49
  482.1 24.4 %collective-permute-done.46 = bf16[2,5,192,512]{3,2,1,0:T(8,128)(2,1)} collective-permute-done((bf16[2,5,192,512]{3,2,1,0:T(8,128)(2,1)}, bf16[2,5,192,512]{3,2,1,0:T(8,128)(2,1)}, u32[]{:S(2)}, u32[]{:S(2)}) %collective-permute-start.46) | collective-permute-done | bytes 1966112 | tf_op jit(solution)/shard_map/ppermute | solution.py:49
  525.7 30.5 %attend_backward.1 = (f32[2,3,64,1024]{3,2,1,0:T(8,128)}, bf16[1024,128]{1,0:T(8,128)(2,1)}, bf16[1024,128]{1,0:T(8,128)(2,1)}, bf16[1024,128]{1,0:T(8,128)(2,1)...) custom-call(s32[8]{0:T(128)} %stack.227.offsets, ...), custom_call_target="tpu_custom_call" | custom-call | tf_op jit(solution)/shard_map/attend_backward/pallas_call | solution.py:468
  556.3 69.0 %collective-permute-done.51 = bf16[2,5,192,512]{3,2,1,0:T(8,128)(2,1)} collective-permute-done((bf16[2,5,192,512]{3,2,1,0:T(8,128)(2,1)}, bf16[2,5,192,512]{3,2,1,0:T(8,128)(2,1)}, u32[]{:S(2)}, u32[]{:S(2)}) %collective-permute-start.51) | collective-permute-done | bytes 1966112 | tf_op jit(solution)/shard_map/ppermute | solution.py:49
  655.1 13.1 %matrix_grads.1 = (bf16[4,192,1064]{2,1,0:T(8,128)(2,1)}, bf16[4,192,1064]{2,1,0:T(8,128)(2,1)}, f32[1536,1]{1,0:T(8,128)}) custom-call(s32[8]{0:T(128)} %stack.244.offsets, bf16[1024,1536]{1,0:T(8,128)(2,1)} %copy-done.2, bf16[640,1024]{1,0:T(8,128)(2,1)} %copy-done.4, bf16[1024,1536]{1,0:T(8,128)(2,1)} %all-gather.12.cloned.1.call-done.branch_grad, ...), custom_call_target="tpu_custom_call" | custom-call | tf_op jit(solution)/shard_map/matrix_grads/pallas_call | solution.py:817
  675.0 5.6 add_convert_fusion.2
  697.2 6.5 copy.173
  (479 shorter events, 289.5 us)
Async XLA Ops:
  7.2 72.4 %all-gather.6.cloned.1.call-start = ((), (), s32[]{:S(2)}) async-start(), calls=%async_computation.4 | async-start | bytes 3932160 | tf_op jit(solution)/shard_map/all_gather | solution.py:910
  13.5 166.0 %all-gather.8.cloned.1.call-start = ((), (), s32[]{:S(2)}) async-start(), calls=%async_computation.5 | async-start | bytes 3932160 | tf_op jit(solution)/shard_map/all_gather | solution.py:959
  37.2 65.6 %collective-permute-start.9 = (bf16[3,5,192,512]{3,2,1,0:T(8,128)(2,1)}, bf16[3,5,192,512]{3,2,1,0:T(8,128)(2,1)}, u32[]{:S(2)}, u32[]{:S(2)}) collective-permute-start(bf16[3,5,192,512]{3,2,1,0:T(8,128)(2,1)} %get-tuple-element.256.rest_6_), channel_id=1, source_target_pairs={{0,8},{8,0},{16,24},{24,16},{1,9},{9,1},{17,25},{25,17},{2,10},{10... | collective-permute-start | bytes 8847368 | tf_op jit(solution)/shard_map/ppermute | solution.py:49
  37.7 67.1 %collective-permute-start.10 = (bf16[3,5,192,512]{3,2,1,0:T(8,128)(2,1)}, bf16[3,5,192,512]{3,2,1,0:T(8,128)(2,1)}, u32[]{:S(2)}, u32[]{:S(2)}) collective-permute-start(bf16[3,5,192,512]{3,2,1,0:T(8,128)(2,1)} %collective-permute-done.3.rest_7_), channel_id=1, source_target_pairs={{0,16},{8,24},{16,0},{24,8},{1,17},{9,25},{17,1},{25,9},{2,18},{10... | collective-permute-start | bytes 8847368 | tf_op jit(solution)/shard_map/ppermute | solution.py:49
  96.9 192.0 %all-gather.10.cloned.1.call-start = ((), (), s32[]{:S(2)}) async-start(), calls=%async_computation.6 | async-start | bytes 3932160 | tf_op jit(solution)/shard_map/all_gather | solution.py:1011
  151.3 64.7 %collective-permute-start.27 = (bf16[3,5,192,512]{3,2,1,0:T(8,128)(2,1)}, bf16[3,5,192,512]{3,2,1,0:T(8,128)(2,1)S(1)}, u32[]{:S(2)}, u32[]{:S(2)}) collective-permute-start(bf16[3,5,192,512]{3,2,1,0:T(8,128)(2,1)} %get-tuple-element.256.rest_6_), channel_id=1, source_target_pairs={{0,16},{8,24},{16,0},{24,8},{1,17},{9,25},{17,1},{25,9},{2,18},{10... | collective-permute-start | bytes 8847368 | tf_op jit(solution)/shard_map/ppermute | solution.py:49
  152.1 64.7 %collective-permute-start.28 = (bf16[3,5,192,512]{3,2,1,0:T(8,128)(2,1)}, bf16[3,5,192,512]{3,2,1,0:T(8,128)(2,1)}, u32[]{:S(2)}, u32[]{:S(2)}) collective-permute-start(bf16[3,5,192,512]{3,2,1,0:T(8,128)(2,1)} %collective-permute-done.3.rest_7_), channel_id=1, source_target_pairs={{0,8},{8,0},{16,24},{24,16},{1,9},{9,1},{17,25},{25,17},{2,10},{10... | collective-permute-start | bytes 8847368 | tf_op jit(solution)/shard_map/ppermute | solution.py:49
  221.8 246.2 %reduce-scatter.6.cloned.1.call-start = ((), (), s32[]{:S(2)}) async-start(), calls=%async_computation.7 | async-start | bytes 3932160 | tf_op jit(solution)/shard_map/reduce_scatter | solution.py:1045
  221.9 66.3 %collective-permute-start.30 = (bf16[3,5,192,512]{3,2,1,0:T(8,128)(2,1)}, bf16[3,5,192,512]{3,2,1,0:T(8,128)(2,1)}, u32[]{:S(2)}, u32[]{:S(2)}) collective-permute-start(bf16[3,5,192,512]{3,2,1,0:T(8,128)(2,1)} %collective-permute-done.9.rest_8_), channel_id=1, source_target_pairs={{0,16},{8,24},{16,0},{24,8},{1,17},{9,25},{17,1},{25,9},{2,18},{10... | collective-permute-start | bytes 8847368 | tf_op jit(solution)/shard_map/ppermute | solution.py:49
  222.9 66.0 %collective-permute-start.31 = (bf16[3,5,192,512]{3,2,1,0:T(8,128)(2,1)}, bf16[3,5,192,512]{3,2,1,0:T(8,128)(2,1)}, u32[]{:S(2)}, u32[]{:S(2)}) collective-permute-start(bf16[3,5,192,512]{3,2,1,0:T(8,128)(2,1)} %collective-permute-done.10.rest_11_), channel_id=1, source_target_pairs={{0,8},{8,0},{16,24},{24,16},{1,9},{9,1},{17,25},{25,17},{2,10},{10... | collective-permute-start | bytes 8847368 | tf_op jit(solution)/shard_map/ppermute | solution.py:49
  397.9 51.6 %collective-permute-start.39 = (bf16[1536,1024]{1,0:T(8,128)(2,1)}, bf16[1536,1024]{1,0:T(8,128)(2,1)}, u32[]{:S(2)}, u32[]{:S(2)}) collective-permute-start(bf16[1536,1024]{1,0:T(8,128)(2,1)} %combine.7), channel_id=1, source_target_pairs={{0,4},{4,0},{1,5},{5,1},{2,6},{6,2},{3,7},{7,3},{8,12},{12,8},{9,1... | collective-permute-start | bytes 9437192 | tf_op jit(solution)/shard_map/ppermute | solution.py:49
  402.6 40.4 %collective-permute-start.41 = (f32[10,1024]{1,0:T(8,128)S(1)}, f32[10,1024]{1,0:T(8,128)}, u32[]{:S(2)}, u32[]{:S(2)}) collective-permute-start(f32[10,1024]{1,0:T(8,128)S(1)} %reshape.402), channel_id=1, source_target_pairs={{0,1},{1,2},{2,3},{3,0},{4,5},{5,6},{6,7},{7,4},{8,9},{9,10},{10,1... | collective-permute-start | bytes 122888 | tf_op jit(solution)/shard_map/ppermute | solution.py:188
  404.1 41.0 %collective-permute-start.42 = (f32[10,1024]{1,0:T(8,128)S(1)}, f32[10,1024]{1,0:T(8,128)}, u32[]{:S(2)}, u32[]{:S(2)}) collective-permute-start(f32[10,1024]{1,0:T(8,128)S(1)} %reshape.402), channel_id=1, source_target_pairs={{0,2},{1,3},{2,0},{3,1},{4,6},{5,7},{6,4},{7,5},{8,10},{9,11},{10,... | collective-permute-start | bytes 122888 | tf_op jit(solution)/shard_map/ppermute | solution.py:188
  405.6 41.6 %collective-permute-start.43 = (f32[10,1024]{1,0:T(8,128)S(1)}, f32[10,1024]{1,0:T(8,128)}, u32[]{:S(2)}, u32[]{:S(2)}) collective-permute-start(f32[10,1024]{1,0:T(8,128)S(1)} %reshape.402), channel_id=1, source_target_pairs={{0,3},{1,0},{2,1},{3,2},{4,7},{5,4},{6,5},{7,6},{8,11},{9,8},{10,9... | collective-permute-start | bytes 122888 | tf_op jit(solution)/shard_map/ppermute | solution.py:188
  445.1 61.4 %collective-permute-start.46 = (bf16[2,5,192,512]{3,2,1,0:T(8,128)(2,1)}, bf16[2,5,192,512]{3,2,1,0:T(8,128)(2,1)}, u32[]{:S(2)}, u32[]{:S(2)}) collective-permute-start(bf16[2,5,192,512]{3,2,1,0:T(8,128)(2,1)} %get-tuple-element.277), channel_id=1, source_target_pairs={{0,8},{8,0},{16,24},{24,16},{1,9},{9,1},{17,25},{25,17},{2,10},{10... | collective-permute-start | bytes 5898248 | tf_op jit(solution)/shard_map/ppermute | solution.py:49
  447.2 61.0 %collective-permute-start.47 = (bf16[2,5,192,512]{3,2,1,0:T(8,128)(2,1)}, bf16[2,5,192,512]{3,2,1,0:T(8,128)(2,1)}, u32[]{:S(2)}, u32[]{:S(2)}) collective-permute-start(bf16[2,5,192,512]{3,2,1,0:T(8,128)(2,1)} %get-tuple-element.278), channel_id=1, source_target_pairs={{0,16},{8,24},{16,0},{24,8},{1,17},{9,25},{17,1},{25,9},{2,18},{10... | collective-permute-start | bytes 5898248 | tf_op jit(solution)/shard_map/ppermute | solution.py:49
  482.1 143.3 %all-gather.12.cloned.1.call-start = ((), (), s32[]{:S(2)}) async-start(), calls=%async_computation.9 | async-start | bytes 3932160 | tf_op jit(solution)/shard_map/all_gather | solution.py:1108
  508.2 208.1 %reduce-scatter.8.cloned.1.call-start = ((), (), s32[]{:S(2)}) async-start(), calls=%async_computation.8 | async-start | bytes 3932160 | tf_op jit(solution)/shard_map/reduce_scatter | solution.py:1150
  518.4 107.0 %collective-permute-start.49 = (bf16[3,5,192,512]{3,2,1,0:T(8,128)(2,1)}, bf16[3,5,192,512]{3,2,1,0:T(8,128)(2,1)}, u32[]{:S(2)}, u32[]{:S(2)}) collective-permute-start(bf16[3,5,192,512]{3,2,1,0:T(8,128)(2,1)} %add_convert_fusion.5), channel_id=1, source_target_pairs={{0,16},{8,24},{16,0},{24,8},{1,17},{9,25},{17,1},{25,9},{2,18},{10... | collective-permute-start | bytes 8847368 | tf_op jit(solution)/shard_map/ppermute | solution.py:49
  519.2 106.1 %collective-permute-start.50 = (bf16[3,5,192,512]{3,2,1,0:T(8,128)(2,1)}, bf16[3,5,192,512]{3,2,1,0:T(8,128)(2,1)}, u32[]{:S(2)}, u32[]{:S(2)}) collective-permute-start(bf16[3,5,192,512]{3,2,1,0:T(8,128)(2,1)} %add_convert_fusion.4), channel_id=1, source_target_pairs={{0,8},{8,0},{16,24},{24,16},{1,9},{9,1},{17,25},{25,17},{2,10},{10... | collective-permute-start | bytes 8847368 | tf_op jit(solution)/shard_map/ppermute | solution.py:49
  520.6 104.7 %collective-permute-start.51 = (bf16[2,5,192,512]{3,2,1,0:T(8,128)(2,1)}, bf16[2,5,192,512]{3,2,1,0:T(8,128)(2,1)}, u32[]{:S(2)}, u32[]{:S(2)}) collective-permute-start(bf16[2,5,192,512]{3,2,1,0:T(8,128)(2,1)} %get-tuple-element.307), channel_id=1, source_target_pairs={{0,8},{8,0},{16,24},{24,16},{1,9},{9,1},{17,25},{25,17},{2,10},{10... | collective-permute-start | bytes 5898248 | tf_op jit(solution)/shard_map/ppermute | solution.py:49
  521.7 103.6 %collective-permute-start.52 = (bf16[2,5,192,512]{3,2,1,0:T(8,128)(2,1)}, bf16[2,5,192,512]{3,2,1,0:T(8,128)(2,1)}, u32[]{:S(2)}, u32[]{:S(2)}) collective-permute-start(bf16[2,5,192,512]{3,2,1,0:T(8,128)(2,1)} %get-tuple-element.308), channel_id=1, source_target_pairs={{0,16},{8,24},{16,0},{24,8},{1,17},{9,25},{17,1},{25,9},{2,18},{10... | collective-permute-start | bytes 5898248 | tf_op jit(solution)/shard_map/ppermute | solution.py:49
  522.9 215.9 %reduce-scatter.10.cloned.1.call-start = ((), (), s32[]{:S(2)}) async-start(), calls=%async_computation.10 | async-start | bytes 3932160
  682.8 41.7 %collective-permute-start.63 = (bf16[3,5,192,512]{3,2,1,0:T(8,128)(2,1)}, bf16[3,5,192,512]{3,2,1,0:T(8,128)(2,1)}, u32[]{:S(2)}, u32[]{:S(2)}) collective-permute-start(bf16[3,5,192,512]{3,2,1,0:T(8,128)(2,1)} %add_convert_fusion.2), channel_id=1, source_target_pairs={{0,4},{4,0},{1,5},{5,1},{2,6},{6,2},{3,7},{7,3},{8,12},{12,8},{9,1... | collective-permute-start | bytes 8847368 | tf_op jit(solution)/shard_map/ppermute | solution.py:49
  (134 other events, 1905.8 us)
Sparse Core Ops, SparseCore 0:
  13.7 65.8 all-gather.5
  97.0 63.2 all-gather.7
  222.0 62.7 all-gather.9
  389.6 63.6 reduce-scatter.5
  508.3 60.5 all-gather.11
  571.6 58.8 reduce-scatter.7
  680.8 57.9 reduce-scatter.9
